TPU v7x, 32 devices: a whole 2x2x4 slice. The times are simulated.
32 devices in a mesh: dp: 16 (over z, y, core), seq: 2 (over x).
Axes of the slice: x: 2, y: 2, z: 4, core: 2. Of those that a mesh axis runs over, the one named last changes fastest.
Arguments:
- tokens: bfloat16 [16, 1024, 1024], P('dp', 'seq'), may hold values from -6 to 6
- cotangent: bfloat16 [16, 1024, 1024], P('dp', 'seq'), may hold values from -6 to 6
- doc_lengths: int32 [16, 8], P('dp'), may hold values from 1 to 512, 1024 in all within a row
- attn_gain: bfloat16 [1024], replicated, may hold values from 0.5 to 1.5
- w_query: bfloat16 [1024, 1024], replicated, may hold values from -0.1875 to 0.1875
- w_key: bfloat16 [1024, 512], replicated, may hold values from -0.1875 to 0.1875
- w_value: bfloat16 [1024, 512], replicated, may hold values from -0.1875 to 0.1875
- query_gain: bfloat16 [64], replicated, may hold values from 0.5 to 1.5
- key_gain: bfloat16 [64], replicated, may hold values from 0.5 to 1.5
- w_out: bfloat16 [1024, 1024], replicated, may hold values from -3 to 3
- ffn_gain: bfloat16 [1024], replicated, may hold values from 0.5 to 1.5
- w_gate: bfloat16 [1024, 4608], replicated, may hold values from -0.1875 to 0.1875
- w_up: bfloat16 [1024, 4608], replicated, may hold values from -0.1875 to 0.1875
- w_down: bfloat16 [4608, 1024], replicated, may hold values from -0.09375 to 0.09375
Outputs:
- output: float32 [16, 1024, 1024], P('dp', 'seq')
- d_tokens: float32 [16, 1024, 1024], P('dp', 'seq')
- d_attn_gain: float32 [1024], replicated
- d_w_query: float32 [1024, 1024], P('dp', 'seq')
- d_w_key: float32 [1024, 512], P('dp', 'seq')
- d_w_value: float32 [1024, 512], P('dp', 'seq')
- d_query_gain: float32 [64], replicated
- d_key_gain: float32 [64], replicated
- d_w_out: float32 [1024, 1024], P('dp', 'seq')
- d_ffn_gain: float32 [1024], replicated
- d_w_gate: float32 [1024, 4608], P('dp', 'seq')
- d_w_up: float32 [1024, 4608], P('dp', 'seq')
- d_w_down: float32 [4608, 1024], P('dp', 'seq')
Inputs may be any that keep to these rules, and one draw needn't show every extreme that they name: `doc_lengths`: each row's 8 documents fill its 1024 positions, and one of them is 512 long.
All inputs are finite; a program needn't handle non-finite values.
Results may differ from a plain program's by a relative error of at most 0.014.
Values may be sent and summed in bfloat16 or wider, within the bound.
No kernel may reach another device: no remote copies, remote signals or barrier semaphores. Data moves between devices by JAX's collectives and lax.ppermute only.
A program may use at most 256 MiB of HBM per device.

v0:
```python
import math

import jax
import jax.numpy as jnp
from jax import lax
from jax.sharding import PartitionSpec as P

EPSILON = 1e-06


def rms_scale(values, gain):
    return values * lax.rsqrt(jnp.mean(values * values, axis=-1, keepdims=True) + EPSILON) * gain


def norm_back(incoming, values, gain):
    inverse = lax.rsqrt(jnp.mean(values * values, axis=-1, keepdims=True) + EPSILON)
    unit = values * inverse
    scaled = incoming * gain
    d_values = inverse * (scaled - unit * jnp.mean(scaled * unit, axis=-1, keepdims=True))
    return (d_values, incoming * unit)


def rope_tables(first, count, width):
    half = width // 2
    spread = jnp.exp(jnp.arange(half, dtype=jnp.float32) * (-2.0 * math.log(1000000.0) / width))
    places = (first + jnp.arange(count, dtype=jnp.int32)).astype(jnp.float32)
    angles = places[:, None] * spread[None, :]
    return (jnp.cos(angles)[:, None, :], jnp.sin(angles)[:, None, :])


def rotate(values, cosine, sine):
    half = values.shape[-1] // 2
    first_half = values[..., :half]
    second_half = values[..., half:]
    return jnp.concatenate(
        [first_half * cosine - second_half * sine, second_half * cosine + first_half * sine],
        axis=-1,
    )


def reduce_grads(grads):
    partial_sum = lax.psum_scatter(grads, "dp", scatter_dimension=0, tiled=True)
    return lax.psum_scatter(partial_sum, "seq", scatter_dimension=1, tiled=True)


def body(
    tokens,
    cotangent,
    doc_lengths,
    attn_gain,
    w_query,
    w_key,
    w_value,
    query_gain,
    key_gain,
    w_out,
    ffn_gain,
    w_gate,
    w_up,
    w_down,
):
    shards = lax.axis_size("seq")
    local = tokens.shape[1]
    length = local * shards
    head_size = query_gain.shape[0]
    kv_count = w_key.shape[1] // head_size
    head_count = w_query.shape[1] // head_size
    group = head_count // kv_count
    kv_local = kv_count // shards
    block = min(512, length)
    num_blocks = length // block
    scale = head_size ** (-0.5)
    f32 = jnp.float32
    bf16 = jnp.bfloat16
    gain_attn = attn_gain.astype(f32)
    gain_query = query_gain.astype(f32)
    gain_key = key_gain.astype(f32)
    gain_ffn = ffn_gain.astype(f32)
    inputs = tokens[0].astype(f32)
    normed = rms_scale(inputs, gain_attn).astype(bf16)
    query_raw = jnp.dot(normed, w_query, preferred_element_type=f32).reshape(
        local, head_count, head_size
    )
    key_raw = jnp.dot(normed, w_key, preferred_element_type=f32).reshape(local, kv_count, head_size)
    values = (
        jnp.dot(normed, w_value, preferred_element_type=f32)
        .astype(bf16)
        .reshape(local, kv_count, head_size)
    )
    cosine, sine = rope_tables(lax.axis_index("seq") * local, local, head_size)
    query_rot = rotate(rms_scale(query_raw, gain_query), cosine, sine).astype(bf16)
    key_rot = rotate(rms_scale(key_raw, gain_key), cosine, sine).astype(bf16)
    packed_query = query_rot.reshape(local, kv_count, group * head_size)
    packed_kv = jnp.concatenate([key_rot, values], axis=2)
    query_heads, kv_heads = (
        lax.all_to_all(packed_query, "seq", split_axis=1, concat_axis=0, tiled=True),
        lax.all_to_all(packed_kv, "seq", split_axis=1, concat_axis=0, tiled=True),
    )
    query_all = query_heads.reshape(length, kv_local, group, head_size)
    key_all = kv_heads[:, :, :head_size]
    value_all = kv_heads[:, :, head_size:]
    positions = jnp.arange(length, dtype=jnp.int32)
    ends = jnp.cumsum(doc_lengths[0])
    segment = jnp.sum((ends[None, :] <= positions[:, None]).astype(jnp.int32), axis=1)
    starts = jnp.arange(num_blocks, dtype=jnp.int32) * block

    def allowed_at(begin):
        rows_here = begin + jnp.arange(block, dtype=jnp.int32)
        query_seg = lax.dynamic_slice_in_dim(segment, begin, block, 0)
        return (query_seg[:, None] == segment[None, :]) & (positions[None, :] <= rows_here[:, None])

    def block_scores(begin):
        query_block = lax.dynamic_slice_in_dim(query_all, begin, block, 0)
        scores = (
            jnp.einsum("qhgd,khd->hgqk", query_block, key_all, preferred_element_type=f32) * scale
        )
        return (query_block, jnp.where(allowed_at(begin), scores, -jnp.inf))

    def attend(begin):
        query_block, scores = block_scores(begin)
        top_score = jnp.max(scores, axis=-1, keepdims=True)
        expos = jnp.exp(scores - top_score)
        totals = jnp.sum(expos, axis=-1, keepdims=True)
        probs = (expos / totals).astype(bf16)
        result = jnp.einsum("hgqk,khd->qhgd", probs, value_all, preferred_element_type=f32)
        return (result.astype(bf16), top_score[..., 0] + jnp.log(totals[..., 0]))

    attended_heads, log_totals = lax.map(attend, starts)
    attended_heads = attended_heads.reshape(length, kv_local, group * head_size)
    attended = lax.all_to_all(
        attended_heads, "seq", split_axis=0, concat_axis=1, tiled=True
    ).reshape(local, head_count * head_size)
    hidden = inputs + jnp.dot(attended, w_out, preferred_element_type=f32)
    hnormed = rms_scale(hidden, gain_ffn).astype(bf16)
    gate = jnp.dot(hnormed, w_gate, preferred_element_type=f32)
    up_part = jnp.dot(hnormed, w_up, preferred_element_type=f32)
    act = (jax.nn.silu(gate) * up_part).astype(bf16)
    output = hidden + jnp.dot(act, w_down, preferred_element_type=f32)
    d_mlp = cotangent[0]
    grad_down = jnp.einsum("tf,td->fd", act, d_mlp, preferred_element_type=f32)
    d_act = jnp.einsum("td,fd->tf", d_mlp, w_down, preferred_element_type=f32)
    gate_again = jnp.dot(hnormed, w_gate, preferred_element_type=f32)
    up_again = jnp.dot(hnormed, w_up, preferred_element_type=f32)
    sigmoid_gate = jax.nn.sigmoid(gate_again)
    d_up = (d_act * gate_again * sigmoid_gate).astype(bf16)
    d_gate = (d_act * up_again * sigmoid_gate * (1.0 + gate_again * (1.0 - sigmoid_gate))).astype(
        bf16
    )
    grad_gate = jnp.einsum("td,tf->df", hnormed, d_gate, preferred_element_type=f32)
    grad_up = jnp.einsum("td,tf->df", hnormed, d_up, preferred_element_type=f32)
    ffn_sums = reduce_grads((grad_gate, grad_up, grad_down))
    d_hnormed = jnp.einsum("tf,df->td", d_gate, w_gate, preferred_element_type=f32) + jnp.einsum(
        "tf,df->td", d_up, w_up, preferred_element_type=f32
    )
    d_hidden_norm, ffn_gain_terms = norm_back(d_hnormed, hidden, gain_ffn)
    d_hidden = cotangent[0].astype(f32) + d_hidden_norm
    d_attn = d_hidden.astype(bf16)
    grad_out = jnp.einsum("tf,td->fd", attended, d_attn, preferred_element_type=f32)
    d_attended = jnp.einsum("td,fd->tf", d_attn, w_out, preferred_element_type=f32).astype(bf16)
    d_heads = lax.all_to_all(
        d_attended.reshape(local, kv_count, group * head_size),
        "seq",
        split_axis=1,
        concat_axis=0,
        tiled=True,
    )
    d_all = d_heads.reshape(length, kv_local, group, head_size)

    def attend_back(carry, item):
        begin, log_block = item
        query_block, scores = block_scores(begin)
        probs = jnp.exp(scores - log_block[..., None])
        d_block = lax.dynamic_slice_in_dim(d_all, begin, block, 0)
        d_probs = jnp.einsum("qhgd,khd->hgqk", d_block, value_all, preferred_element_type=f32)
        delta = jnp.sum(probs * d_probs, axis=-1, keepdims=True)
        d_scores = (scale * (probs * (d_probs - delta))).astype(bf16)
        d_query_block = jnp.einsum("hgqk,khd->qhgd", d_scores, key_all, preferred_element_type=f32)
        key_total = carry[0] + jnp.einsum(
            "hgqk,qhgd->khd", d_scores, query_block, preferred_element_type=f32
        )
        value_total = carry[1] + jnp.einsum(
            "hgqk,qhgd->khd", probs.astype(bf16), d_block, preferred_element_type=f32
        )
        return ((key_total, value_total), d_query_block.astype(bf16))

    empty = jnp.zeros((length, kv_local, head_size), f32)
    (d_keys, d_values), d_queries = lax.scan(attend_back, (empty, empty), (starts, log_totals))
    d_queries = d_queries.reshape(length, kv_local, group * head_size)
    d_kv = jnp.concatenate([d_keys.astype(bf16), d_values.astype(bf16)], axis=2)
    d_query_pos, d_kv_pos = (
        lax.all_to_all(d_queries, "seq", split_axis=0, concat_axis=1, tiled=True),
        lax.all_to_all(d_kv, "seq", split_axis=0, concat_axis=1, tiled=True),
    )
    d_query_rot = d_query_pos.reshape(local, head_count, head_size).astype(f32)
    d_query_raw, query_gain_terms = norm_back(
        rotate(d_query_rot, cosine, -sine), query_raw, gain_query
    )
    d_query_low = d_query_raw.reshape(local, head_count * head_size).astype(bf16)
    d_key_rot = d_kv_pos[:, :, :head_size].astype(f32)
    d_key_raw, key_gain_terms = norm_back(rotate(d_key_rot, cosine, -sine), key_raw, gain_key)
    d_key_low = d_key_raw.reshape(local, kv_count * head_size).astype(bf16)
    d_value_low = d_kv_pos[:, :, head_size:].reshape(local, kv_count * head_size)
    grad_query = jnp.einsum("td,tf->df", normed, d_query_low, preferred_element_type=f32)
    grad_key = jnp.einsum("td,tf->df", normed, d_key_low, preferred_element_type=f32)
    grad_value = jnp.einsum("td,tf->df", normed, d_value_low, preferred_element_type=f32)
    d_normed = jnp.einsum("tf,df->td", d_query_low, w_query, preferred_element_type=f32)
    d_normed = d_normed + jnp.einsum("tf,df->td", d_key_low, w_key, preferred_element_type=f32)
    d_normed = d_normed + jnp.einsum("tf,df->td", d_value_low, w_value, preferred_element_type=f32)
    d_input_norm, attn_gain_terms = norm_back(d_normed, inputs, gain_attn)
    d_inputs = d_hidden + d_input_norm
    attn_sums = reduce_grads((grad_query, grad_key, grad_value, grad_out))
    gain_totals = lax.psum(
        (
            jnp.sum(attn_gain_terms, axis=0),
            jnp.sum(query_gain_terms, axis=(0, 1)),
            jnp.sum(key_gain_terms, axis=(0, 1)),
            jnp.sum(ffn_gain_terms, axis=0),
        ),
        ("dp", "seq"),
    )
    return (
        output[None],
        d_inputs[None],
        gain_totals[0],
        attn_sums[0],
        attn_sums[1],
        attn_sums[2],
        gain_totals[1],
        gain_totals[2],
        attn_sums[3],
        gain_totals[3],
        ffn_sums[0],
        ffn_sums[1],
        ffn_sums[2],
    )


def solution(mesh):
    return jax.shard_map(
        body,
        mesh=mesh,
        in_specs=(
            P("dp", "seq", None),
            P("dp", "seq", None),
            P("dp", None),
            P(),
            P(),
            P(),
            P(),
            P(),
            P(),
            P(),
            P(),
            P(),
            P(),
            P(),
        ),
        out_specs=(
            P("dp", "seq", None),
            P("dp", "seq", None),
            P(),
            P("dp", "seq"),
            P("dp", "seq"),
            P("dp", "seq"),
            P(),
            P(),
            P("dp", "seq"),
            P(),
            P("dp", "seq"),
            P("dp", "seq"),
            P("dp", "seq"),
        ),
        check_vma=False,
    )
```

profile of v0, /device:TPU:0, one launch (start us, length us, event | category | flops | bytes accessed | tf_op | source)
XLA Modules:
  0.0 1398.1 jit_solution(11515140757117083535)
XLA Ops:
  19.7 4.4 all-to-all-start.1
  33.7 5.5 all-to-all-done.1
  39.2 4.6 all-to-all-start
  49.3 7.9 all-to-all-done
  64.2 36.4 %while.28 = (s32[]{:T(128)}, bf16[2,512,4,2,64]{1,4,3,2,0:T(8,128)(2,1)}, f32[2,4,2,512]{3,2,1,0:T(2,128)S(1)}, s32[2]{0:T(128)S(1)}, s32[1024]{0:T(1024)S(1)}, ...) while((s32[]{:T(128)}, ...), condition=%wide.region_8.9_spmd.clone, body=%wide.region_5.8_spmd.clone.sunk | while | flops 1125904896 | bytes 54672044 | solution.py:128
  68.0 4.4 bitcast_reduce_fusion.2
  76.8 5.6 fusion.162
  86.2 4.4 bitcast_reduce_fusion.2
  95.0 5.6 fusion.162
  100.6 6.1 copy.115
  106.7 5.1 reshape.352
  111.8 4.9 all-to-all-start.2
  116.7 12.4 all-to-all-done.2
  138.4 7.6 fusion.102
  146.0 7.4 fusion.103
  153.4 20.4 %multiply_convert_fusion = (bf16[512,4608]{1,0:T(8,128)(2,1)}, bf16[512,4608]{1,0:T(8,128)(2,1)}, bf16[512,4608]{1,0:T(8,128)(2,1)}) fusion(f32[512,4608]{1,0:T(8,128)} %fusion.102, f32[512,4608]{1,0:T(8,128)} %fusion.103, bf16[4608,1024]{1,0:T(8,128)(2,1)} %param.31, bf16[1,512,1024]{2,1,0:T(8,128)(2,1)S(1)} %copy-done.27), kind=kOutput, calls=%fused_computation.63 | convolution fusion | flops 4869586944 | bytes 43515904 | tf_op jit(solution)/shard_map/td,fd->tf/dot_general | solution.py:141
  173.8 9.2 fusion.104
  183.0 8.8 multiply_reduce_fusion
  198.6 11.4 all-to-all-done.3
  215.0 155.5 %while.29 = (s32[]{:T(128)}, f32[1024,4,64]{0,2,1:T(8,128)}, f32[1024,4,64]{0,2,1:T(8,128)S(1)}, bf16[2,512,4,2,64]{1,4,3,2,0:T(8,128)(2,1)}, s32[2]{0:T(128)S(1...) while((s32[]{:T(128)}, f32[1024,4,64]{0,2,1:T(8,128)}, ...), condition=%wide.region_13.14_spmd.clone, body=%wide.region_11.13_spmd.clone.sunk | while | flops 2745969152 | bytes 194050784 | solution.py:187
  218.8 9.6 fusion.172
  228.4 8.2 fusion.173
  236.6 25.5 %fusion.176 = bf16[2,512,4,2,64]{1,4,3,2,0:T(8,128)(2,1)} fusion(bf16[2,512,4,2,64]{1,4,3,2,0:T(8,128)(2,1)} %get-tuple-element.434, s32[]{:T(128)} %get-tuple-element.431, f32[4,2,512,1024]{3,2,1,0:T(8,128)} %fusion.172, f32[4,512,2,1024]{3,1,2,0:T(8,128)} %fusion.173, bf16[1024,4,64]{0,2,1:T(8,128)(2,1)S(1)} %get-tuple-element.452), kind=kOutput, calls=%fused_computation.44.clone.1 | convolution fusion | flops 558109696 | bytes 68157952 | tf_op jit(solution)/shard_map/while/body/eval_jaxpr/hgqk,khd->qhgd/dot_general | solution.py:177
  262.1 22.9 %fusion.174 = f32[1024,4,64]{0,2,1:T(8,128)} fusion(f32[4,2,512,1024]{3,2,1,0:T(8,128)} %fusion.172, f32[4,512,2,1024]{3,1,2,0:T(8,128)} %fusion.173, f32[1024,4,64]{0,2,1:T(8,128)} %get-tuple-element.432, pred[]{:T(512)S(6)} %compare.3, bf16[1024,4,2,64]{0,3,2,1:T(8,128)(2,1)} %get-tuple-element.450, s32[]{:T(128)S(6)} %select_n.56), kind=kOutput, calls=%fused_computation.39.clone.1 | convolution fusion | flops 558371840 | bytes 69730312 | tf_op jit(solution)/shard_map/while/body/eval_jaxpr/hgqk,qhgd->khd/dot_general | solution.py:178
  284.9 7.6 fusion.175
  296.4 9.6 fusion.172
  306.0 8.2 fusion.173
  314.2 25.5 %fusion.176 = bf16[2,512,4,2,64]{1,4,3,2,0:T(8,128)(2,1)} fusion(bf16[2,512,4,2,64]{1,4,3,2,0:T(8,128)(2,1)} %get-tuple-element.434, s32[]{:T(128)} %get-tuple-element.431, f32[4,2,512,1024]{3,2,1,0:T(8,128)} %fusion.172, f32[4,512,2,1024]{3,1,2,0:T(8,128)} %fusion.173, bf16[1024,4,64]{0,2,1:T(8,128)(2,1)S(1)} %get-tuple-element.452), kind=kOutput, calls=%fused_computation.44.clone.1 | convolution fusion | flops 558109696 | bytes 68157952 | tf_op jit(solution)/shard_map/while/body/eval_jaxpr/hgqk,khd->qhgd/dot_general | solution.py:177
  339.7 23.2 %fusion.174 = f32[1024,4,64]{0,2,1:T(8,128)} fusion(f32[4,2,512,1024]{3,2,1,0:T(8,128)} %fusion.172, f32[4,512,2,1024]{3,1,2,0:T(8,128)} %fusion.173, f32[1024,4,64]{0,2,1:T(8,128)} %get-tuple-element.432, pred[]{:T(512)S(6)} %compare.3, bf16[1024,4,2,64]{0,3,2,1:T(8,128)(2,1)} %get-tuple-element.450, s32[]{:T(128)S(6)} %select_n.56), kind=kOutput, calls=%fused_computation.39.clone.1 | convolution fusion | flops 558371840 | bytes 69730312 | tf_op jit(solution)/shard_map/while/body/eval_jaxpr/hgqk,qhgd->khd/dot_general | solution.py:178
  362.8 7.6 fusion.175
  372.6 13.2 all_to_all.90
  395.1 4.5 fusion.91
  399.8 4.6 copy.116
  406.1 13.2 all_to_all.91
  430.9 11.6 fusion.107
  442.6 11.8 fusion.108
  455.6 11.7 fusion.75
  468.1 49.3 %reduce-scatter.23.cloned.1.call-done = f32[64,512]{1,0:T(8,128)} async-done(((f32[1024,512]{1,0:T(8,128)}), f32[64,512]{1,0:T(8,128)}) %reduce-scatter.23.cloned.1.call-update) | async-done | bytes 131088 | tf_op jit(solution)/shard_map/reduce_scatter | solution.py:42
  517.4 75.6 %reduce-scatter.27.cloned.1.call-done = f32[64,1024]{1,0:T(8,128)} async-done(((f32[1024,1024]{1,0:T(8,128)}), f32[64,1024]{1,0:T(8,128)}) %reduce-scatter.27.cloned.1.call-update) | async-done | bytes 262160 | tf_op jit(solution)/shard_map/reduce_scatter | solution.py:42
  593.1 75.9 %reduce-scatter.15.cloned.1.call-done = f32[64,1024]{1,0:T(8,128)} async-done(((f32[1024,1024]{1,0:T(8,128)}), f32[64,1024]{1,0:T(8,128)}) %reduce-scatter.15.cloned.1.call-update) | async-done | bytes 262160 | tf_op jit(solution)/shard_map/reduce_scatter | solution.py:42
  669.1 197.7 %reduce-scatter.31.cloned.1.call-done = f32[64,4608]{1,0:T(8,128)} async-done(((f32[1024,4608]{1,0:T(8,128)}), f32[64,4608]{1,0:T(8,128)}) %reduce-scatter.31.cloned.1.call-update) | async-done | bytes 1179664 | tf_op jit(solution)/shard_map/reduce_scatter | solution.py:42
  866.8 197.8 %reduce-scatter.35.cloned.1.call-done = f32[64,4608]{1,0:T(8,128)} async-done(((f32[1024,4608]{1,0:T(8,128)}), f32[64,4608]{1,0:T(8,128)}) %reduce-scatter.35.cloned.1.call-update) | async-done | bytes 1179664 | tf_op jit(solution)/shard_map/reduce_scatter | solution.py:42
  1064.7 198.1 %reduce-scatter.39.cloned.1.call-done = f32[288,1024]{1,0:T(8,128)} async-done(((f32[4608,1024]{1,0:T(8,128)}), f32[288,1024]{1,0:T(8,128)}) %reduce-scatter.39.cloned.1.call-update) | async-done | bytes 1179664 | tf_op jit(solution)/shard_map/reduce_scatter | solution.py:42
  1262.9 10.1 add_bitcast_fusion
  1278.8 39.5 %all-reduce = (f32[1024]{0:T(1024)}, f32[64]{0:T(128)}, f32[64]{0:T(128)}, f32[1024]{0:T(1024)}) all-reduce(f32[1024]{0:T(1024)S(1)} %get-tuple-element.190, f32[64]{0:T(128)S(1)} %get-tuple-element.186, f32[64]{0:T(128)S(1)} %get-tuple-element.192, f32[1024]{0:T(1024)S(1)} %copy-done.46), channel_id=1, replica_groups=mesh['dp'=16,'seq'=2] {'dp','seq'}, use_global_device_ids=true, to_apply=%region_18.19 | all-reduce | flops 2176 | bytes 17408 | tf_op jit(solution)/shard_map/psum | solution.py:212
  1322.6 19.4 %reduce-scatter.33.cloned.1.call-done = f32[64,2304]{1,0:T(8,128)} async-done(((f32[64,4608]{1,0:T(8,128)}), f32[64,2304]{1,0:T(8,128)}) %reduce-scatter.33.cloned.1.call-update) | async-done | bytes 589840 | tf_op jit(solution)/shard_map/reduce_scatter | solution.py:43
  1342.0 24.7 %reduce-scatter.37.cloned.1.call-done = f32[64,2304]{1,0:T(8,128)} async-done(((f32[64,4608]{1,0:T(8,128)}), f32[64,2304]{1,0:T(8,128)}) %reduce-scatter.37.cloned.1.call-update) | async-done | bytes 589840 | tf_op jit(solution)/shard_map/reduce_scatter | solution.py:43
  1366.7 24.4 %reduce-scatter.41.cloned.1.call-done = f32[288,512]{1,0:T(8,128)} async-done(((f32[288,1024]{1,0:T(8,128)}), f32[288,512]{1,0:T(8,128)}) %reduce-scatter.41.cloned.1.call-update) | async-done | bytes 589840 | tf_op jit(solution)/shard_map/reduce_scatter | solution.py:43
  (239 shorter events, 108.6 us)
Async XLA Ops:
  7.2 126.6 %copy-start = (bf16[1024,1024]{1,0:T(8,128)(2,1)S(1)}, bf16[1024,1024]{1,0:T(8,128)(2,1)}, u32[]{:S(2)}) copy-start(bf16[1024,1024]{1,0:T(8,128)(2,1)} %param.27) | copy-start | bytes 6291460
  7.2 4.7 copy-start.2
  8.9 19.1 %copy-start.40 = (f32[512]{0:T(512)}, f32[512]{0:T(512)S(1)}, u32[]{:S(2)}) copy-start(f32[512]{0:T(512)S(1)} %add_rsqrt_fusion.3) | copy-start | bytes 6148
  9.6 18.4 %copy-start.38 = (f32[1024]{0:T(1024)}, f32[1024]{0:T(1024)S(1)}, u32[]{:S(2)}) copy-start(f32[1024]{0:T(1024)S(1)} %convert_element_type.137) | copy-start | bytes 12292
  11.9 3.1 copy-start.49
  14.9 3.4 copy-start.36
  15.0 3.4 copy-start.44
  15.0 3.1 copy-start.16
  18.1 13.4 copy-start.24
  19.7 19.6 %all-to-all-start.1 = ((bf16[512,8,128]{0,2,1:T(8,128)(2,1)}), bf16[512,8,128]{0,2,1:T(8,128)(2,1)}, u32[]{:S(2)}, u32[]{:S(2)}) async-start(bf16[512,8,128]{0,2,1:T(8,128)(2,1)} %pad_maximum_fusion.2), calls=%async_computation.1 | async-start | bytes 2097152 | tf_op jit(solution)/shard_map/all_to_all | solution.py:97
  28.0 3.0 copy-start.50
  32.7 11.2 copy-start.51
  39.2 18.0 %all-to-all-start = ((bf16[512,8,128]{0,2,1:T(8,128)(2,1)}), bf16[512,8,128]{0,2,1:T(8,128)(2,1)}, u32[]{:S(2)}, u32[]{:S(2)}) async-start(bf16[512,8,128]{0,2,1:T(8,128)(2,1)} %bitcast.7), calls=%async_computation | async-start | bytes 2097152 | tf_op jit(solution)/shard_map/all_to_all | solution.py:96
  100.6 11.2 copy-start.5
  100.6 11.2 copy-start.34
  106.7 10.0 copy-start.47
  111.8 17.3 %all-to-all-start.2 = ((bf16[1024,4,128]{2,1,0:T(4,128)(2,1)}), bf16[1024,4,128]{2,1,0:T(4,128)(2,1)}, u32[]{:S(2)}, u32[]{:S(2)}) async-start(bf16[1024,4,128]{2,1,0:T(4,128)(2,1)} %reshape.352), calls=%async_computation.2 | async-start | bytes 2097152 | tf_op jit(solution)/shard_map/all_to_all | solution.py:130
  116.7 17.1 %copy-start.3 = (bf16[1,512,1024]{2,1,0:T(8,128)(2,1)S(1)}, bf16[1,512,1024]{2,1,0:T(8,128)(2,1)}, u32[]{:S(2)}) copy-start(bf16[1,512,1024]{2,1,0:T(8,128)(2,1)} %param.18) | copy-start | bytes 3145732
  133.8 4.6 copy-start.48
  137.8 8.1 slice-start
  138.4 7.6 copy-start.14
  138.4 7.6 slice-start.1
  138.4 7.6 slice-start.2
  146.0 7.4 copy-start.27
  173.8 9.2 copy-start.12
  173.8 9.2 copy-start.21
  194.9 15.1 %all-to-all-start.3 = ((bf16[512,8,128]{2,0,1:T(8,128)(2,1)}), bf16[512,8,128]{2,0,1:T(8,128)(2,1)S(1)}, u32[]{:S(2)}, u32[]{:S(2)}) async-start(bf16[512,8,128]{2,0,1:T(8,128)(2,1)} %bitcast.254), calls=%async_computation.3 | async-start | bytes 2097152 | tf_op jit(solution)/shard_map/all_to_all | solution.py:160
  198.5 268.9 %reduce-scatter.19.cloned.1.call-start = ((), (), s32[]{:S(2)}) async-start(), calls=%async_computation.22 | async-start | bytes 2228224 | tf_op jit(solution)/shard_map/reduce_scatter | solution.py:42
  212.0 3.0 copy-start.6
  212.0 3.0 copy-start.35
  391.5 125.9 %reduce-scatter.23.cloned.1.call-start = ((), (), s32[]{:S(2)}) async-start(), calls=%async_computation.24 | async-start | bytes 2228224 | tf_op jit(solution)/shard_map/reduce_scatter | solution.py:42
  391.5 3.6 copy-start.10
  395.1 197.9 %reduce-scatter.27.cloned.1.call-start = ((), (), s32[]{:S(2)}) async-start(), calls=%async_computation.26 | async-start | bytes 4456448 | tf_op jit(solution)/shard_map/reduce_scatter | solution.py:42
  399.7 269.3 %reduce-scatter.15.cloned.1.call-start = ((), (), s32[]{:S(2)}) async-start(), calls=%async_computation.20 | async-start | bytes 4456448 | tf_op jit(solution)/shard_map/reduce_scatter | solution.py:42
  429.7 437.0 %reduce-scatter.31.cloned.1.call-start = ((), (), s32[]{:S(2)}) async-start(), calls=%async_computation.28 | async-start | bytes 20054016 | tf_op jit(solution)/shard_map/reduce_scatter | solution.py:42
  442.5 622.1 %reduce-scatter.35.cloned.1.call-start = ((), (), s32[]{:S(2)}) async-start(), calls=%async_computation.30 | async-start | bytes 20054016 | tf_op jit(solution)/shard_map/reduce_scatter | solution.py:42
  454.4 808.4 %reduce-scatter.39.cloned.1.call-start = ((), (), s32[]{:S(2)}) async-start(), calls=%async_computation.32 | async-start | bytes 20054016 | tf_op jit(solution)/shard_map/reduce_scatter | solution.py:42
  467.3 855.2 %reduce-scatter.21.cloned.1.call-start = ((), (), s32[]{:S(2)}) async-start(), calls=%async_computation.23 | async-start | bytes 196608 | tf_op jit(solution)/shard_map/reduce_scatter | solution.py:43
  468.1 854.5 %reduce-scatter.25.cloned.1.call-start = ((), (), s32[]{:S(2)}) async-start(), calls=%async_computation.25 | async-start | bytes 196608 | tf_op jit(solution)/shard_map/reduce_scatter | solution.py:43
  517.4 745.5 %copy-start.13 = (f32[512,1024]{1,0:T(8,128)S(1)}, f32[512,1024]{1,0:T(8,128)}, u32[]{:S(2)}) copy-start(f32[512,1024]{1,0:T(8,128)} %copy-done.11) | copy-start | bytes 6291460
  517.4 805.2 %reduce-scatter.29.cloned.1.call-start = ((), (), s32[]{:S(2)}) async-start(), calls=%async_computation.27 | async-start | bytes 393216 | tf_op jit(solution)/shard_map/reduce_scatter | solution.py:43
  593.0 729.5 %reduce-scatter.17.cloned.1.call-start = ((), (), s32[]{:S(2)}) async-start(), calls=%async_computation.21 | async-start | bytes 393216 | tf_op jit(solution)/shard_map/reduce_scatter | solution.py:43
  669.0 672.9 %reduce-scatter.33.cloned.1.call-start = ((), (), s32[]{:S(2)}) async-start(), calls=%async_computation.29 | async-start | bytes 1769472 | tf_op jit(solution)/shard_map/reduce_scatter | solution.py:43
  866.8 499.9 %reduce-scatter.37.cloned.1.call-start = ((), (), s32[]{:S(2)}) async-start(), calls=%async_computation.31 | async-start | bytes 1769472 | tf_op jit(solution)/shard_map/reduce_scatter | solution.py:43
  1064.6 326.5 %reduce-scatter.41.cloned.1.call-start = ((), (), s32[]{:S(2)}) async-start(), calls=%async_computation.33 | async-start | bytes 1769472 | tf_op jit(solution)/shard_map/reduce_scatter | solution.py:43
  1262.9 10.1 copy-start.20
  1262.9 10.1 copy-start.22
  1318.3 72.8 %copy-start.1 = (bf16[1024,1024]{1,0:T(8,128)(2,1)S(1)}, bf16[1024,1024]{1,0:T(8,128)(2,1)}, u32[]{:S(2)}) copy-start(bf16[1024,1024]{1,0:T(8,128)(2,1)} %param.27) | copy-start | bytes 6291460
  (25 other events, 39.6 us)
Sparse Core Ops, SparseCore 0:
  391.6 60.9 reduce-scatter.18
  456.8 60.5 reduce-scatter.22
  521.2 71.7 reduce-scatter.26
  597.2 71.7 reduce-scatter.14
  673.0 193.7 reduce-scatter.30
  870.7 193.8 reduce-scatter.34
  1068.7 194.0 reduce-scatter.38
  1265.6 9.3 reduce-scatter.20
  1277.8 10.5 reduce-scatter.24
  1291.1 11.3 reduce-scatter.28
  1305.3 11.8 reduce-scatter.16
  1319.8 22.0 reduce-scatter.32
  1344.9 21.7 reduce-scatter.36
  1369.4 21.7 reduce-scatter.40
where the time goes:
time: 1400 us
  waiting for transfers between devices  901 us (64%)
  matrix products  297 us (21%)
  blocking collectives  65.9 us (5%)
  local copies, waits for them, and re-layouts  60.8 us (4%)
  other arithmetic  32.4 us (2%)
  starting transfers between devices  18 us (1%)
  between operations  15.1 us (1%)
    reduce_scatter x7, waiting for transfers between devices, reduce_grads(): partial_sum = lax.psum_scatter(grads, 'dp', scatter_dimension=0, tiled=True)  794 us
    reduce_scatter x7, waiting for transfers between devices, reduce_grads(): return lax.psum_scatter(partial_sum, 'seq', scatter_dimension=1, tiled=True)  68.6 us
    dot_general x2, matrix products, attend_back(): jnp.einsum('hgqk,khd->qhgd', d_scores, key_all, preferred_element_type=f32)  50.9 us
    dot_general x2, matrix products, attend_back(): jnp.einsum('hgqk,qhgd->khd', d_scores, query_block, preferred_element_typ...  46 us
    psum x1, blocking collectives, body(): lax.psum((jnp.sum(attn_gain_terms, axis=0), jnp.sum(query_gain_terms, axi...  39.5 us
  transfers between devices with their start and end apart: 18, of which 13 were waited for; matrix products, arithmetic and copies ran while one was open for 6% of the time, Pallas kernels for 0%

commit v1 on v0

--- a/solution.py
+++ b/solution.py
@@ -3,6 +3,9 @@
 import jax
 import jax.numpy as jnp
 from jax import lax
+from jax.experimental import pallas as pl
+from jax.experimental.pallas import tpu as pltpu
+from jax.sharding import Mesh
 from jax.sharding import PartitionSpec as P
 
 EPSILON = 1e-06
@@ -43,7 +46,7 @@
     return lax.psum_scatter(partial_sum, "seq", scatter_dimension=1, tiled=True)
 
 
-def body(
+def general_body(
     tokens,
     cotangent,
     doc_lengths,
@@ -235,40 +238,447 @@
     )
 
 
+AXES = ("zh", "zl", "y", "c", "x")
+QBLOCK = 256
+F32 = jnp.float32
+BF16 = jnp.bfloat16
+
+
+def swap(v, axis):
+    return lax.ppermute(v, axis, [(0, 1), (1, 0)])
+
+
+def transpose_pair(v):
+    return lax.ppermute(v, ("c", "x"), [(0, 0), (1, 2), (2, 1), (3, 3)])
+
+
+def pick(bit, low, high):
+    return jnp.where(bit == 0, low, high)
+
+
+def in_order(bit, own, other, axis):
+    return jnp.concatenate([pick(bit, own, other), pick(bit, other, own)], axis=axis)
+
+
+def dot(left, right, left_dim, right_dim):
+    return lax.dot_general(
+        left, right, (((left_dim,), (right_dim,)), ((), ())), preferred_element_type=F32
+    )
+
+
+def part_columns(w, c):
+    width = w.shape[1] // 4
+    return [lax.dynamic_slice_in_dim(w, (2 * i + c) * width, width, 1) for i in range(2)]
+
+
+def part_rows(w, c):
+    width = w.shape[0] // 4
+    return jnp.concatenate(
+        [lax.dynamic_slice_in_dim(w, (2 * i + c) * width, width, 0) for i in range(2)], axis=0
+    )
+
+
+def rope_rows(values, gain, cosine, sine):
+    unit = values * lax.rsqrt(jnp.mean(values * values, axis=0, keepdims=True) + EPSILON) * gain
+    half = values.shape[0] // 2
+    first, second = unit[:half], unit[half:]
+    return jnp.concatenate([first * cosine - second * sine, second * cosine + first * sine], axis=0)
+
+
+def rope_rows_back(incoming, values, gain, cosine, sine):
+    half = values.shape[0] // 2
+    first, second = incoming[:half], incoming[half:]
+    turned = jnp.concatenate([first * cosine + second * sine, second * cosine - first * sine], axis=0)
+    inverse = lax.rsqrt(jnp.mean(values * values, axis=0, keepdims=True) + EPSILON)
+    unit = values * inverse
+    scaled = turned * gain
+    d_values = inverse * (scaled - unit * jnp.mean(scaled * unit, axis=0, keepdims=True))
+    return d_values, turned * unit
+
+
+def block_mask(first_key, keys, begin, block, starts, diagonal):
+    key_at = first_key + lax.broadcasted_iota(jnp.int32, (keys, block), 0)
+    allowed = key_at >= starts
+    if diagonal:
+        query_at = begin + lax.broadcasted_iota(jnp.int32, (keys, block), 1)
+        allowed = allowed & (key_at <= query_at)
+    return allowed
+
+
+def attention_kernel(
+    starts_ref, gain_q_ref, gain_k_ref, cos_ref, sin_ref, q_ref, k_ref, v_ref,
+    out_ref, log_ref, qs_ref, ks_ref, vs_ref,
+):
+    size = k_ref.shape[0]
+    length = k_ref.shape[1]
+    group = q_ref.shape[0] // size
+    cosine, sine = cos_ref[...], sin_ref[...]
+    k_rot = rope_rows(k_ref[...], gain_k_ref[...], cosine, sine)
+    ks_ref[...] = k_rot.astype(BF16)
+    keys = k_rot.T.astype(BF16)
+    values = v_ref[...].astype(BF16)
+    vs_ref[...] = values
+    for h in range(group):
+        rows = pl.ds(h * size, size)
+        q_rot = rope_rows(q_ref[rows, :], gain_q_ref[...], cosine, sine).astype(BF16)
+        q_rot = q_rot * jnp.asarray(size ** (-0.5), BF16)
+        qs_ref[rows, :] = q_rot
+        for begin in range(0, length, QBLOCK):
+            stop = begin + QBLOCK
+            q_block = q_rot[:, begin:stop]
+            starts = starts_ref[:, begin:stop]
+            parts = [(begin, stop, True)] + ([(0, begin, False)] if begin else [])
+            scores = []
+            top = None
+            for low, high, diagonal in parts:
+                s = dot(keys[low:high], q_block, 1, 0)
+                s = jnp.where(block_mask(low, high - low, begin, QBLOCK, starts, diagonal), s, -jnp.inf)
+                here = jnp.max(s, axis=0, keepdims=True)
+                top = here if top is None else jnp.maximum(top, here)
+                scores.append(s)
+            expos = [jnp.exp(s - top) for s in scores]
+            total = sum(jnp.sum(e, axis=0, keepdims=True) for e in expos)
+            inverse = 1.0 / total
+            result = 0.0
+            for (low, high, _), e in zip(parts, expos):
+                result = result + dot(values[:, low:high], (e * inverse).astype(BF16), 1, 0)
+            out_ref[rows, begin:stop] = result.astype(BF16)
+            log_ref[0, 0, h : h + 1, begin:stop] = top + jnp.log(total)
+
+
+def attention(qkv, starts, gain_q, gain_k, cosine, sine, size, group, pairs):
+    rows, length = qkv.shape
+    per = (group + 2) * size * pairs
+    halves = rows // per
+    unit = group * size
+    q_rows, k_rows = per // unit, per // size
+    full = lambda a: pl.BlockSpec(a.shape, lambda i, j: (0,) * a.ndim)
+    heads = halves * pairs * group
+    return pl.pallas_call(
+        attention_kernel,
+        grid=(halves, pairs),
+        in_specs=[full(a) for a in (starts, gain_q, gain_k, cosine, sine)]
+        + [
+            pl.BlockSpec((unit, length), lambda i, j: (q_rows * i + j, 0)),
+            pl.BlockSpec((size, length), lambda i, j: (k_rows * i + pairs * group + j, 0)),
+            pl.BlockSpec((size, length), lambda i, j: (k_rows * i + pairs * (group + 1) + j, 0)),
+        ],
+        out_specs=[
+            pl.BlockSpec((unit, length), lambda i, j: (pairs * i + j, 0)),
+            pl.BlockSpec((1, 1, group, length), lambda i, j: (i, j, 0, 0)),
+            pl.BlockSpec((unit, length), lambda i, j: (pairs * i + j, 0)),
+            pl.BlockSpec((size, length), lambda i, j: (pairs * i + j, 0)),
+            pl.BlockSpec((size, length), lambda i, j: (pairs * i + j, 0)),
+        ],
+        out_shape=[
+            jax.ShapeDtypeStruct((heads * size, length), BF16),
+            jax.ShapeDtypeStruct((halves, pairs, group, length), F32),
+            jax.ShapeDtypeStruct((heads * size, length), BF16),
+            jax.ShapeDtypeStruct((halves * pairs * size, length), BF16),
+            jax.ShapeDtypeStruct((halves * pairs * size, length), BF16),
+        ],
+        name="attention_forward",
+    )(starts, gain_q, gain_k, cosine, sine, qkv, qkv, qkv)
+
+
+def attention_back_kernel(
+    starts_ref, gain_q_ref, gain_k_ref, cos_ref, sin_ref, q_ref, k_ref, qs_ref, ks_ref, vs_ref, log_ref, do_ref,
+    out_ref, gq_ref, gk_ref, dk_ref, dv_ref,
+):
+    size = k_ref.shape[0]
+    length = k_ref.shape[1]
+    group = q_ref.shape[0] // size
+    pair, pairs = pl.program_id(1), pl.num_programs(1)
+    cosine, sine = cos_ref[...], sin_ref[...]
+
+    @pl.when((pl.program_id(0) == 0) & (pair == 0))
+    def _():
+        gq_ref[...] = jnp.zeros_like(gq_ref)
+        gk_ref[...] = jnp.zeros_like(gk_ref)
+
+    def fold(terms):
+        width = gq_ref.shape[1]
+        return sum(terms[:, i : i + width] for i in range(0, length, width))
+
+    keys_t = ks_ref[...]
+    keys = keys_t.astype(F32).T.astype(BF16)
+    values = vs_ref[...].astype(F32).T.astype(BF16)
+    dk_ref[...] = jnp.zeros_like(dk_ref)
+    dv_ref[...] = jnp.zeros_like(dv_ref)
+    scale = size ** (-0.5)
+    for h in range(group):
+        rows = pl.ds(h * size, size)
+        q_t, do_t = qs_ref[rows, :], do_ref[rows, :]
+        q_nat = q_t.astype(F32).T.astype(BF16)
+        do_nat = do_t.astype(F32).T.astype(BF16)
+        d_query = []
+        for begin in range(0, length, QBLOCK):
+            stop = begin + QBLOCK
+            starts = starts_ref[:, begin:stop]
+            logs = log_ref[0, 0, h : h + 1, begin:stop]
+            parts = [(begin, stop, True)] + ([(0, begin, False)] if begin else [])
+            probs, d_probs = [], []
+            delta = 0.0
+            for low, high, diagonal in parts:
+                s = dot(keys[low:high], q_t[:, begin:stop], 1, 0)
+                allowed = block_mask(low, high - low, begin, QBLOCK, starts, diagonal)
+                p = jnp.where(allowed, jnp.exp(s - logs), 0.0)
+                dp = dot(values[low:high], do_t[:, begin:stop], 1, 0)
+                delta = delta + jnp.sum(p * dp, axis=0, keepdims=True)
+                probs.append(p)
+                d_probs.append(dp)
+            d_q = 0.0
+            for (low, high, _), p, dp in zip(parts, probs, d_probs):
+                ds = (p * (dp - delta)).astype(BF16)
+                dv_ref[low:high, :] += dot(p.astype(BF16), do_nat[begin:stop], 1, 0)
+                dk_ref[low:high, :] += dot(ds, q_nat[begin:stop], 1, 0)
+                d_q = d_q + dot(keys_t[:, low:high], ds, 1, 0)
+            d_query.append((d_q * scale).astype(BF16))
+        d_q0, terms = rope_rows_back(
+            jnp.concatenate(d_query, axis=1).astype(F32), q_ref[rows, :], gain_q_ref[...], cosine, sine
+        )
+        gq_ref[...] += fold(terms)
+        out_ref[pl.ds((pair * group + h) * size, size), :] = d_q0.astype(BF16)
+    d_key = dk_ref[...].T.astype(BF16).astype(F32)
+    d_k0, terms = rope_rows_back(d_key, k_ref[...], gain_k_ref[...], cosine, sine)
+    gk_ref[...] += fold(terms)
+    out_ref[pl.ds((pairs * group + pair) * size, size), :] = d_k0.astype(BF16)
+    out_ref[pl.ds((pairs * (group + 1) + pair) * size, size), :] = dv_ref[...].T.astype(BF16)
+
+
+def attention_back(qkv, qs, ks, vs, logs, d_out, starts, gain_q, gain_k, cosine, sine, size, group, pairs):
+    rows, length = qkv.shape
+    per = (group + 2) * size * pairs
+    halves = rows // per
+    unit = group * size
+    q_rows, k_rows = per // unit, per // size
+    full = lambda a: pl.BlockSpec(a.shape, lambda i, j: (0,) * a.ndim)
+    wide = pl.BlockSpec((unit, length), lambda i, j: (pairs * i + j, 0))
+    thin = pl.BlockSpec((size, length), lambda i, j: (pairs * i + j, 0))
+    return pl.pallas_call(
+        attention_back_kernel,
+        grid=(halves, pairs),
+        in_specs=[full(a) for a in (starts, gain_q, gain_k, cosine, sine)]
+        + [
+            pl.BlockSpec((unit, length), lambda i, j: (q_rows * i + j, 0)),
+            pl.BlockSpec((size, length), lambda i, j: (k_rows * i + pairs * group + j, 0)),
+            wide, thin, thin,
+            pl.BlockSpec((1, 1, group, length), lambda i, j: (i, j, 0, 0)),
+            wide,
+        ],
+        out_specs=[
+            pl.BlockSpec((per, length), lambda i, j: (i, 0)),
+            pl.BlockSpec((size, 128), lambda i, j: (0, 0)),
+            pl.BlockSpec((size, 128), lambda i, j: (0, 0)),
+        ],
+        out_shape=[
+            jax.ShapeDtypeStruct((rows, length), BF16),
+            jax.ShapeDtypeStruct((size, 128), F32),
+            jax.ShapeDtypeStruct((size, 128), F32),
+        ],
+        scratch_shapes=[pltpu.VMEM((length, size), F32), pltpu.VMEM((length, size), F32)],
+        name="attention_backward",
+    )(starts, gain_q, gain_k, cosine, sine, qkv, qkv, qs, ks, vs, logs, d_out)
+
+
+def add_up(terms):
+    return sum(t.astype(F32) for t in terms)
+
+
+def halve(grad, stages):
+    terms = [grad]
+    for axis, dim in stages:
+        bit = lax.axis_index(axis)
+        size = terms[0].shape[dim] // 2
+        low = [lax.slice_in_dim(t, 0, size, axis=dim) for t in terms]
+        high = [lax.slice_in_dim(t, size, 2 * size, axis=dim) for t in terms]
+        send = add_up([pick(bit, h, l) for l, h in zip(low, high)]).astype(BF16)
+        terms = [pick(bit, l, h) for l, h in zip(low, high)] + [swap(send, axis)]
+    return add_up(terms)
+
+
+def share_rows(total, c):
+    rows = total.shape[0] // 2
+    own = pick(c, total[:rows], total[rows:])
+    other = swap(pick(c, total[rows:], total[:rows]).astype(BF16), "c").astype(F32)
+    return in_order(c, own, other, 1)
+
+
+def sum_columns(grad, order, c):
+    rows, columns = grad.shape
+    dims = {"zh": 0, "zl": 1, "y": 2, "x": 4}
+    total = halve(grad.reshape(2, 2, 2, rows // 8, columns), [(a, dims[a]) for a in order])
+    return share_rows(total.reshape(rows // 8, columns // 2), c)
+
+
+def sum_rows(grad, order, c):
+    rows, columns = grad.shape
+    dims = {"zh": 0, "y": 1, "x": 3}
+    total = halve(grad.reshape(2, 2, rows // 4, columns), [(a, dims[a]) for a in order])
+    total = total.reshape(rows // 4, columns // 2)
+    total = total + lax.ppermute(total.astype(BF16), ("zl", "c"), [(2, 0), (1, 3)]).astype(F32)
+    rows = total.shape[0] // 2
+    own = pick(c, total[:rows], total[rows:])
+    other = pick(c, total[rows:], total[:rows]).astype(BF16)
+    other = lax.ppermute(other, ("zl", "c"), [(0, 1), (3, 2)]).astype(F32)
+    return jnp.where(lax.axis_index("zl") == c, own, other)
+
+
+def pair_body(
+    tokens, cotangent, doc_lengths, attn_gain, w_query, w_key, w_value, query_gain, key_gain, w_out,
+    ffn_gain, w_gate, w_up, w_down,
+):
+    local = tokens.shape[1]
+    length = 2 * local
+    size = query_gain.shape[0]
+    kv_count = w_key.shape[1] // size
+    group = w_query.shape[1] // w_key.shape[1]
+    pairs = kv_count // 4
+    c, x = lax.axis_index("c"), lax.axis_index("x")
+    gain_attn = attn_gain.astype(F32)
+    gain_ffn = ffn_gain.astype(F32)
+    gain_q = query_gain.astype(F32)[:, None]
+    gain_k = key_gain.astype(F32)[:, None]
+
+    own_tokens = transpose_pair(tokens[0])
+    inputs_low = in_order(c, own_tokens, swap(own_tokens, "c"), 0)
+    own_cot = transpose_pair(cotangent[0])
+    d_mlp = in_order(c, own_cot, swap(own_cot, "c"), 0)
+    lengths = jnp.where(c == x, doc_lengths[0], swap(doc_lengths[0], "c"))
+    ends = jnp.cumsum(lengths)
+    positions = jnp.arange(length, dtype=jnp.int32)
+    starts = jnp.max(jnp.where(ends[:, None] <= positions[None, :], ends[:, None], 0), axis=0, keepdims=True)
+    half = size // 2
+    spread = jnp.exp(jnp.arange(half, dtype=F32) * (-2.0 * math.log(1000000.0) / size))
+    angles = spread[:, None] * positions.astype(F32)[None, :]
+    cosine, sine = jnp.cos(angles), jnp.sin(angles)
+
+    parts = [part_columns(w, c) for w in (w_query, w_key, w_value)]
+    w_qkv = jnp.concatenate([p[i] for i in range(2) for p in parts], axis=1)
+    gate_w = jnp.concatenate(part_columns(w_gate, c), axis=1)
+    up_w = jnp.concatenate(part_columns(w_up, c), axis=1)
+    down_w = part_rows(w_down, c)
+    out_w = part_rows(w_out, c)
+
+    inputs = inputs_low.astype(F32)
+    normed = rms_scale(inputs, gain_attn).astype(BF16)
+    qkv = dot(w_qkv, normed, 0, 1)
+    attended_own, logs, qs, ks, vs = attention(qkv, starts, gain_q, gain_k, cosine, sine, size, group, pairs)
+    attended_other = swap(attended_own, "c")
+    quarter = attended_own.shape[0] // 2
+    attended = jnp.concatenate(
+        [
+            piece
+            for i in range(2)
+            for piece in (
+                pick(c, attended_own[i * quarter : (i + 1) * quarter], attended_other[i * quarter : (i + 1) * quarter]),
+                pick(c, attended_other[i * quarter : (i + 1) * quarter], attended_own[i * quarter : (i + 1) * quarter]),
+            )
+        ],
+        axis=0,
+    )
+    hidden = inputs + dot(attended, w_out, 0, 0)
+    hnormed = rms_scale(hidden, gain_ffn).astype(BF16)
+
+    gate = dot(hnormed, gate_w, 1, 0)
+    up_part = dot(hnormed, up_w, 1, 0)
+    sigmoid_gate = jax.nn.sigmoid(gate)
+    silu_gate = gate * sigmoid_gate
+    act = (silu_gate * up_part).astype(BF16)
+    d_act = dot(d_mlp, down_w, 1, 1)
+    d_up = (d_act * silu_gate).astype(BF16)
+    d_gate = (d_act * up_part * sigmoid_gate * (1.0 + gate * (1.0 - sigmoid_gate))).astype(BF16)
+    grad_down = dot(act, d_mlp, 0, 0).astype(BF16)
+    grad_gate = dot(hnormed, d_gate, 0, 0).astype(BF16)
+    grad_up = dot(hnormed, d_up, 0, 0).astype(BF16)
+    sum_down = sum_rows(grad_down, ("y", "x", "zh"), c)
+    sum_gate = sum_columns(grad_gate, ("x", "y", "zl", "zh"), c)
+    sum_up = sum_columns(grad_up, ("zl", "zh", "y", "x"), c)
+
+    d_hn = dot(d_gate, gate_w, 1, 1) + dot(d_up, up_w, 1, 1)
+    d_hn = d_hn + swap(d_hn.astype(BF16), "c").astype(F32)
+    d_hidden_norm, ffn_gain_terms = norm_back(d_hn, hidden, gain_ffn)
+    d_hidden = d_mlp.astype(F32) + d_hidden_norm
+    d_attn = d_hidden.astype(BF16)
+    d_attn_part = jnp.concatenate(part_columns(d_attn, c), axis=1)
+    grad_out = dot(attended, d_attn_part, 1, 0).astype(BF16)
+    sum_out = sum_columns(grad_out, ("x", "y", "zl", "zh"), c)
+    d_attended = dot(out_w, d_attn, 1, 1).astype(BF16)
+    d_qkv, gain_q_terms, gain_k_terms = attention_back(
+        qkv, qs, ks, vs, logs, d_attended, starts, gain_q, gain_k, cosine, sine, size, group, pairs
+    )
+    grad_qkv = dot(normed, d_qkv, 0, 1).astype(BF16)
+    sum_qkv = []
+    width = grad_qkv.shape[1] // 2
+    q_width = pairs * group * size
+    q_part = jnp.concatenate([grad_qkv[:, i * width : i * width + q_width] for i in range(2)], axis=1)
+    k_part = jnp.concatenate([grad_qkv[:, i * width + q_width : i * width + q_width + pairs * size] for i in range(2)], axis=1)
+    v_part = jnp.concatenate([grad_qkv[:, i * width + q_width + pairs * size : (i + 1) * width] for i in range(2)], axis=1)
+    sum_query = sum_columns(q_part, ("x", "y", "zl", "zh"), c)
+    sum_key = sum_columns(k_part, ("y", "x", "zl", "zh"), c)
+    sum_value = sum_columns(v_part, ("y", "x", "zl", "zh"), c)
+
+    def own_rows(v):
+        return pick(c, v[:local], v[local:])
+
+    def other_rows(v):
+        return pick(c, v[local:], v[:local])
+
+    part = dot(d_qkv, w_qkv, 0, 1)
+    d_normed = own_rows(part) + swap(other_rows(part).astype(BF16), "c").astype(F32)
+    d_input_norm, attn_gain_terms = norm_back(d_normed, own_rows(inputs), gain_attn)
+    d_inputs = own_rows(d_hidden) + d_input_norm
+    part = dot(act, down_w, 1, 0)
+    output = own_rows(hidden) + own_rows(part) + swap(other_rows(part).astype(BF16), "c").astype(F32)
+    stays = c == x
+    output = jnp.where(stays, output, transpose_pair(output.astype(BF16)).astype(F32))
+    d_inputs = jnp.where(stays, d_inputs, transpose_pair(d_inputs.astype(BF16)).astype(F32))
+
+    gains = jnp.concatenate(
+        [
+            jnp.sum(attn_gain_terms, axis=0),
+            jnp.sum(ffn_gain_terms, axis=0) * 0.5,
+            jnp.sum(gain_q_terms, axis=1),
+            jnp.sum(gain_k_terms, axis=1),
+        ]
+    ).reshape(-1, 128)
+    for axis in AXES:
+        gains = gains + swap(gains, axis)
+    gains = gains.reshape(-1)
+    d = tokens.shape[2]
+    return (
+        output[None],
+        d_inputs[None],
+        gains[:d],
+        sum_query,
+        sum_key,
+        sum_value,
+        gains[2 * d : 2 * d + size],
+        gains[2 * d + size :],
+        sum_out,
+        gains[d : 2 * d],
+        sum_gate,
+        sum_up,
+        sum_down,
+    )
+
+
 def solution(mesh):
+    rows, shards = mesh.shape["dp"], mesh.shape["seq"]
+    if rows == 16 and shards == 2:
+        body = pair_body
+        mesh = Mesh(mesh.devices.reshape(2, 2, 2, 2, 2), AXES)
+        dp, seq = AXES[:4], "x"
+    else:
+        body = general_body
+        dp, seq = "dp", "seq"
     return jax.shard_map(
         body,
         mesh=mesh,
-        in_specs=(
-            P("dp", "seq", None),
-            P("dp", "seq", None),
-            P("dp", None),
-            P(),
-            P(),
-            P(),
-            P(),
-            P(),
-            P(),
-            P(),
-            P(),
-            P(),
-            P(),
-            P(),
-        ),
-        out_specs=(
-            P("dp", "seq", None),
-            P("dp", "seq", None),
-            P(),
-            P("dp", "seq"),
-            P("dp", "seq"),
-            P("dp", "seq"),
-            P(),
-            P(),
-            P("dp", "seq"),
-            P(),
-            P("dp", "seq"),
-            P("dp", "seq"),
-            P("dp", "seq"),
-        ),
+        in_specs=(P(dp, seq, None), P(dp, seq, None), P(dp, None)) + (P(),) * 11,
+        out_specs=(P(dp, seq, None), P(dp, seq, None), P())
+        + (P(dp, seq),) * 3
+        + (P(), P(), P(dp, seq), P())
+        + (P(dp, seq),) * 3,
         check_vma=False,
     )

time: 1400 us -> 513 us (0.37)
  waiting for transfers between devices: 901 us -> 144 us
  matrix products: 297 us -> 95.6 us
  other arithmetic: 32.4 us -> 102 us
  blocking collectives: 65.9 us -> 0 us
  starting transfers between devices: 18 us -> 63.5 us
  Pallas kernels: 0 us -> 42.6 us
    reduce_scatter x14 -> x0, waiting for transfers between devices: 863 us -> none  [the longest x7 794 us: reduce_grads(): partial_sum = lax.psum_scatter(grads, 'dp', scatter_dimension=0, tiled=True)]
    dot_general x35 -> x15, matrix products: 297 us -> 95.6 us  [dot(): lax.dot_general(left, right, (((left_dim,), (right_dim,)), ((), ())), pre...]
    ppermute x0 -> x51, waiting for transfers between devices: none -> 144 us  [the longest x45 144 us: swap(): return lax.ppermute(v, axis, [(0, 1), (1, 0)])]
    ppermute x0 -> x51, starting transfers between devices: none -> 63.5 us  [the longest x45 46.8 us: swap(): return lax.ppermute(v, axis, [(0, 1), (1, 0)])]
    pallas_call x0 -> x2, Pallas kernels: none -> 42.6 us  [the longest x1 24.8 us: attention_back(): pl.pallas_call(attention_back_kernel, grid=(halves, pairs), in_specs=[ful...]
    psum x1 -> x0, blocking collectives: 39.5 us -> none  [body(): lax.psum((jnp.sum(attn_gain_terms, axis=0), jnp.sum(query_gain_terms, axi...]
    all_to_all x4 -> x0, waiting for transfers between devices: 37.2 us -> none  [the longest x1 12.4 us: body(): lax.all_to_all(attended_heads, 'seq', split_axis=0, concat_axis=1, tiled=...]
    select_n x0 -> x48, other arithmetic: none -> 37.2 us  [the longest x47 36.3 us: pick(): return jnp.where(bit == 0, low, high)]
  transfers between devices with their start and end apart: 18 -> 51, of which waited for: 13 -> 25; matrix products, arithmetic and copies ran while one was open for 6% -> 32% of each run, Pallas kernels for 0% -> 5%
where the time goes in v1:
time: 513 us; the launch traced here: 506 us
  waiting for transfers between devices  144 us (28%)
  other arithmetic  102 us (20%)
  matrix products  95.6 us (19%)
  starting transfers between devices  63.5 us (12%)
  local copies, waits for them, and re-layouts  56 us (11%)
  Pallas kernels  42.6 us (8%)
    ppermute x45, waiting for transfers between devices, swap(): return lax.ppermute(v, axis, [(0, 1), (1, 0)])  144 us
    dot_general x15, matrix products, dot(): lax.dot_general(left, right, (((left_dim,), (right_dim,)), ((), ())), pre...  95.6 us
    ppermute x45, starting transfers between devices, swap(): return lax.ppermute(v, axis, [(0, 1), (1, 0)])  46.8 us
    select_n x47, other arithmetic, pick(): return jnp.where(bit == 0, low, high)  36.3 us
    unnamed x191, local copies, waits for them, and re-layouts  27.3 us
    pallas_call x1, Pallas kernels, attention_back(): pl.pallas_call(attention_back_kernel, grid=(halves, pairs), in_specs=[ful...  24.8 us
    convert_element_type x20, other arithmetic, halve(): send = add_up([pick(bit, h, l) for l, h in zip(low, high)]).astype(BF16)  20.3 us
    pallas_call x1, Pallas kernels, attention(): pl.pallas_call(attention_kernel, grid=(halves, pairs), in_specs=[full(a)...  17.8 us
  transfers between devices with their start and end apart: 51, of which 25 were waited for; matrix products, arithmetic and copies ran while one was open for 32% of the time, Pallas kernels for 5%

profile of v1, /device:TPU:0, one launch (start us, length us, event | category | flops | bytes accessed | tf_op | source)
XLA Modules:
  0.0 506.1 jit_solution(225799704448469689)
XLA Ops:
  6.2 4.3 collective-permute-start.2
  22.1 8.8 %collective-permute-start.7 = (bf16[512,1024]{0,1:T(8,128)(2,1)S(1)}, bf16[512,1024]{0,1:T(8,128)(2,1)}, u32[]{:S(2)}, u32[]{:S(2)}) collective-permute-start(bf16[512,1024]{0,1:T(8,128)(2,1)S(1)} %collective-permute-done.6), channel_id=1, source_target_pairs={{0,2},{2,0},{1,3},{3,1},{4,6},{6,4},{5,7},{7,5},{8,10},{10,8},{9,1... | collective-permute-start | bytes 3145736 | tf_op jit(solution)/shard_map/ppermute | solution.py:248
  32.6 7.6 %constant_dynamic-slice_fusion.7 = (bf16[1024,1152]{1,0:T(8,128)(2,1)}, bf16[1024,1152]{1,0:T(8,128)(2,1)}, bf16[1024,1152]{1,0:T(8,128)(2,1)}, bf16[1024,1152]{1,0:T(8,128)(2,1)}) fusion(bf16[1024,4608]{1,0:T(8,128)(2,1)} %param.26, s32[]{:T(128)S(6)} %select_n.891, s32[]{:T(128)S(6)} %select_n.892, bf16[1024,4608]{1,0:T(8,128)(2,1)} %param.25), kind=kLoop, calls=%fused_computation.200 | loop fusion | bytes 18874376 | tf_op jit(solution)/shard_map/dynamic_slice | solution.py:271
  42.1 3.4 broadcast_select_fusion.13
  46.1 6.6 %fusion.17.q_ref.k_ref.v_ref = f32[1024,1024]{1,0:T(8,128)} fusion(bf16[1024,1024]{1,0:T(8,128)(2,1)} %dynamic-slice_dynamic-update-slice_fusion.2, f32[1024]{0:T(1024)S(1)} %convert_element_type.514, f32[1024]{0:T(1024)S(1)} %add_rsqrt_fusion.1, bf16[512,1024]{0,1:T(8,128)(2,1)S(1)} %get-tuple-element.133, bf16[512,1024]{0,1:T(8,128)(2,1)S(1)} %get-tuple-element.134), kind=kOutput, calls=%fused_computation.79 | convolution fusion | flops 2154823680 | bytes 8396800 | tf_op jit(solution)/shard_map/dot_general | solution.py:264
  52.7 17.8 %attention_forward.1 = (bf16[512,1024]{1,0:T(8,128)(2,1)}, f32[2,2,2,1024]{3,2,1,0:T(2,128)}, bf16[512,1024]{1,0:T(8,128)(2,1)}, bf16[256,1024]{1,0:T(8,128)(2,1)}, bf16[256,1024]{1,0:T(8,128)(2,1)}) custom-call(s32[1,1024]{1,0:T(1,128)} %bitcast.93, f32[64,1]{1,0:T(8,128)} %copy.46.gain_q_ref, f32[64,1]{1,0:T(8,128)} %copy.47.gain_k_ref, ...), custom_call_target="tpu_custom_call" | custom-call | tf_op jit(solution)/shard_map/attention_forward/pallas_call | solution.py:357
  70.8 5.0 constant_dynamic-slice_fusion.5
  82.6 2.8 multiply_reduce_fusion.2
  90.1 7.6 %fusion.4 = f32[1024,2304]{1,0:T(8,128)} fusion(bf16[1024,1024]{0,1:T(8,128)(2,1)S(1)} %multiply_convert_fusion.3, bf16[1024,1152]{1,0:T(8,128)(2,1)S(1)} %copy-done.38, bf16[1024,1152]{1,0:T(8,128)(2,1)S(1)} %copy-done.36), kind=kOutput, calls=%fused_computation.23 | convolution fusion | flops 4841275392 | bytes 16252928 | tf_op jit(solution)/shard_map/dot_general | solution.py:264
  97.7 8.0 %fusion.6 = f32[1024,2304]{1,0:T(8,128)} fusion(bf16[1024,1024]{0,1:T(8,128)(2,1)S(1)} %multiply_convert_fusion.3, bf16[1024,1152]{1,0:T(8,128)(2,1)S(1)} %copy-done.32, bf16[1024,1152]{1,0:T(8,128)(2,1)S(1)} %copy-done.34), kind=kOutput, calls=%fused_computation.25 | convolution fusion | flops 4841275392 | bytes 16252928 | tf_op jit(solution)/shard_map/dot_general | solution.py:264
  105.7 17.2 %multiply_convert_fusion.1 = (bf16[1024,2304]{1,0:T(8,128)(2,1)}, bf16[1024,2304]{1,0:T(8,128)(2,1)}, bf16[1024,2304]{1,0:T(8,128)(2,1)}) fusion(f32[1024,2304]{1,0:T(8,128)} %fusion.6, f32[1024,2304]{1,0:T(8,128)} %fusion.4, bf16[1152,1024]{1,0:T(8,128)(2,1)} %get-tuple-element.74, bf16[1152,1024]{1,0:T(8,128)(2,1)} %get-tuple-element.73, ...), kind=kOutput, calls=%fused_computation.1 | convolution fusion | flops 4880859136 | bytes 39845888 | tf_op jit(solution)/shard_map/dot_general | solution.py:264
  123.0 8.0 %convolution_convert_fusion.1 = bf16[1024,2304]{1,0:T(8,128)(2,1)S(1)} fusion(bf16[1024,1024]{0,1:T(8,128)(2,1)} %copy-done.49, bf16[1024,2304]{1,0:T(8,128)(2,1)} %get-tuple-element.71), kind=kOutput, calls=%fused_computation.6 | convolution fusion | flops 4834197504 | bytes 11534336 | tf_op jit(solution)/shard_map/dot_general | solution.py:264
  131.0 6.6 %fusion.3 = f32[1024,1024]{0,1:T(8,128)} fusion(bf16[1024,2304]{1,0:T(8,128)(2,1)S(1)} %copy-done.86, bf16[1024,1152]{1,0:T(8,128)(2,1)S(1)} %copy-done.39, bf16[1024,1152]{1,0:T(8,128)(2,1)S(1)} %copy-done.37), kind=kOutput, calls=%fused_computation.22 | convolution fusion | flops 4841275392 | bytes 13631488 | tf_op jit(solution)/shard_map/dot_general | solution.py:264
  137.7 5.9 %convolution_convert_fusion = bf16[2304,1024]{1,0:T(8,128)(2,1)S(1)} fusion(bf16[1024,2304]{1,0:T(8,128)(2,1)S(1)} %bitcast.100, bf16[512,1024]{0,1:T(8,128)(2,1)S(1)} %copy-done.30, bf16[512,1024]{0,1:T(8,128)(2,1)S(1)} %get-tuple-element.95), kind=kOutput, calls=%fused_computation.5 | convolution fusion | flops 4838391808 | bytes 11534336 | tf_op jit(solution)/shard_map/dot_general | solution.py:264
  143.6 7.0 %fusion.2 = f32[1024,1024]{0,1:T(8,128)S(1)} fusion(bf16[1024,2304]{1,0:T(8,128)(2,1)} %get-tuple-element.72, bf16[1152,1024]{1,0:T(8,128)(2,1)S(1)} %copy-done.41, bf16[1152,1024]{1,0:T(8,128)(2,1)S(1)} %copy-done.40), kind=kOutput, calls=%fused_computation.21 | convolution fusion | flops 4841275392 | bytes 13631488 | tf_op jit(solution)/shard_map/dot_general | solution.py:264
  157.3 5.2 %convolution_convert_fusion.2 = bf16[1024,2304]{1,0:T(8,128)(2,1)S(1)} fusion(bf16[1024,1024]{0,1:T(8,128)(2,1)S(1)} %copy-done.50, bf16[1024,2304]{1,0:T(8,128)(2,1)S(1)} %bitcast.98), kind=kOutput, calls=%fused_computation.7 | convolution fusion | flops 4834197504 | bytes 11534336 | tf_op jit(solution)/shard_map/dot_general | solution.py:264
  166.6 8.3 %fusion.44 = (bf16[1024,1024]{0,1:T(8,128)(2,1)S(1)}, f32[1024,1024]{0,1:T(8,128)S(1)}) fusion(f32[1024,1024]{0,1:T(8,128)} %fusion.3, bf16[1024,2304]{1,0:T(8,128)(2,1)} %get-tuple-element.70, bf16[1024,1152]{1,0:T(8,128)(2,1)S(1)} %copy-done.33, bf16[1024,1152]{1,0:T(8,128)(2,1)S(1)} %copy-done.35), kind=kOutput, calls=%fused_computation.230 | convolution fusion | flops 4843372544 | bytes 19922944 | tf_op jit(solution)/shard_map/dot_general | solution.py:264
  180.6 2.8 fusion.39
  183.5 9.4 %collective-permute-start.5 = (bf16[512,1024]{0,1:T(8,128)(2,1)}, bf16[512,1024]{0,1:T(8,128)(2,1)}, u32[]{:S(2)}, u32[]{:S(2)}) collective-permute-start(bf16[512,1024]{0,1:T(8,128)(2,1)} %get-tuple-element.68), channel_id=1, source_target_pairs={{0,0},{1,2},{2,1},{3,3},{4,4},{5,6},{6,5},{7,7},{8,8},{9,10},{10,9... | collective-permute-start | bytes 3145736 | tf_op jit(solution)/shard_map/ppermute | solution.py:252
  194.5 3.8 fusion.38
  203.1 24.8 %attention_backward.1 = (bf16[1024,1024]{1,0:T(8,128)(2,1)}, f32[64,128]{1,0:T(8,128)}, f32[64,128]{1,0:T(8,128)}) custom-call(s32[1,1024]{1,0:T(1,128)} %bitcast.94, f32[64,1]{1,0:T(8,128)} %copy.46.gain_q_ref, f32[64,1]{1,0:T(8,128)} %copy.47.gain_k_ref, f32[32,1024]{1,0:T(8,128)} %get-tuple-element.128.cos_ref, f32[32,1024]{1,0:T(8,128)} %get-tuple-element.127.sin_ref, ...), custom_call_target="tpu_custom_call" | custom-call | tf_op jit(solution)/shard_map/attention_backward/pallas_call | solution.py:458
  227.9 4.7 convolution_convert_fusion.3
  251.2 2.9 select_bitcast_fusion.1
  260.4 2.9 copy.61
  266.5 3.9 fusion.45
  280.6 3.3 add_convert_fusion
  285.9 3.4 add_convert_fusion.1
  289.3 3.4 add_convert_fusion.2
  293.8 2.9 broadcast_select_fusion.6
  297.9 20.4 %collective-permute-done.27 = bf16[2,2,1,128,128]{4,3,2,1,0:T(8,128)(2,1)S(1)} collective-permute-done((bf16[2,2,1,128,128]{4,3,2,1,0:T(8,128)(2,1)S(1)}, bf16[2,2,1,128,128]{4,3,2,1,0:T(8,128)(2,1)S(1)}, u32[]{:S(2)}, u32[]{:S(2)}) %collective-permute-start.27) | collective-permute-done | bytes 131104 | tf_op jit(solution)/shard_map/ppermute | solution.py:248
  319.1 4.6 collective-permute-done.22
  324.5 3.6 collective-permute-done.28
  328.7 3.6 collective-permute-done.23
  334.9 3.1 collective-permute-done.29
  339.8 3.0 collective-permute-done.24
  352.2 29.0 %collective-permute-done.32 = bf16[2,2,1,128,256]{4,3,2,1,0:T(8,128)(2,1)S(1)} collective-permute-done((bf16[2,2,1,128,256]{4,3,2,1,0:T(8,128)(2,1)S(1)}, bf16[2,2,1,128,256]{4,3,2,1,0:T(8,128)(2,1)S(1)}, u32[]{:S(2)}, u32[]{:S(2)}) %collective-permute-start.32) | collective-permute-done | bytes 262176 | tf_op jit(solution)/shard_map/ppermute | solution.py:248
  381.9 6.6 %collective-permute-done.17 = bf16[2,2,1,128,256]{4,3,2,1,0:T(8,128)(2,1)S(1)} collective-permute-done((bf16[2,2,1,128,256]{4,3,2,1,0:T(8,128)(2,1)S(1)}, bf16[2,2,1,128,256]{4,3,2,1,0:T(8,128)(2,1)S(1)}, u32[]{:S(2)}, u32[]{:S(2)}) %collective-permute-start.17) | collective-permute-done | bytes 262176 | tf_op jit(solution)/shard_map/ppermute | solution.py:248
  389.3 12.5 %collective-permute-done.33 = bf16[2,1,1,128,256]{4,3,2,1,0:T(8,128)(2,1)S(1)} collective-permute-done((bf16[2,1,1,128,256]{4,3,2,1,0:T(8,128)(2,1)S(1)}, bf16[2,1,1,128,256]{4,3,2,1,0:T(8,128)(2,1)S(1)}, u32[]{:S(2)}, u32[]{:S(2)}) %collective-permute-start.33) | collective-permute-done | bytes 131104 | tf_op jit(solution)/shard_map/ppermute | solution.py:248
  401.9 5.3 %collective-permute-done.18 = bf16[2,1,1,128,256]{4,3,2,1,0:T(8,128)(2,1)S(1)} collective-permute-done((bf16[2,1,1,128,256]{4,3,2,1,0:T(8,128)(2,1)S(1)}, bf16[2,1,1,128,256]{4,3,2,1,0:T(8,128)(2,1)S(1)}, u32[]{:S(2)}, u32[]{:S(2)}) %collective-permute-start.18) | collective-permute-done | bytes 131104 | tf_op jit(solution)/shard_map/ppermute | solution.py:248
  408.5 4.3 collective-permute-done.34
  413.8 4.4 collective-permute-done.19
  424.4 3.2 collective-permute-done.11
  428.2 3.0 collective-permute-done.12
  436.8 3.6 fusion.36
  454.9 18.9 %collective-permute-done.48 = bf16[1,1,576,512]{3,2,1,0:T(8,128)(2,1)S(1)} collective-permute-done((bf16[1,1,576,512]{3,2,1,0:T(8,128)(2,1)S(1)}, bf16[1,1,576,512]{3,2,1,0:T(8,128)(2,1)S(1)}, u32[]{:S(2)}, u32[]{:S(2)}) %collective-permute-start.48) | collective-permute-done | bytes 589856 | tf_op jit(solution)/shard_map/ppermute | solution.py:248
  473.7 3.0 bitcast_convert_fusion
  483.1 6.3 %collective-permute-done.44 = bf16[1,1,1,128,1152]{4,3,2,1,0:T(8,128)(2,1)} collective-permute-done((bf16[1,1,1,128,1152]{4,3,2,1,0:T(8,128)(2,1)}, bf16[1,1,1,128,1152]{4,3,2,1,0:T(8,128)(2,1)}, u32[]{:S(2)}, u32[]{:S(2)}) %collective-permute-start.44) | collective-permute-done | bytes 294944 | tf_op jit(solution)/shard_map/ppermute | solution.py:248
  491.3 6.1 %collective-permute-done.39 = bf16[1,1,1,128,1152]{4,3,2,1,0:T(8,128)(2,1)} collective-permute-done((bf16[1,1,1,128,1152]{4,3,2,1,0:T(8,128)(2,1)}, bf16[1,1,1,128,1152]{4,3,2,1,0:T(8,128)(2,1)}, u32[]{:S(2)}, u32[]{:S(2)}) %collective-permute-start.39) | collective-permute-done | bytes 294944 | tf_op jit(solution)/shard_map/ppermute | solution.py:248
  (407 shorter events, 160.7 us)
Async XLA Ops:
  2.3 19.8 %collective-permute-start = (bf16[512,1024]{0,1:T(8,128)(2,1)S(1)}, bf16[512,1024]{0,1:T(8,128)(2,1)S(1)}, u32[]{:S(2)}, u32[]{:S(2)}) collective-permute-start(bf16[512,1024]{0,1:T(8,128)(2,1)S(1)} %bitcast.90), channel_id=1, source_target_pairs={{0,0},{1,2},{2,1},{3,3},{4,4},{5,6},{6,5},{7,7},{8,8},{9,10},{10,9... | collective-permute-start | bytes 3145736 | tf_op jit(solution)/shard_map/ppermute | solution.py:252
  4.4 17.8 %collective-permute-start.6 = (bf16[512,1024]{0,1:T(8,128)(2,1)}, bf16[512,1024]{0,1:T(8,128)(2,1)S(1)}, u32[]{:S(2)}, u32[]{:S(2)}) collective-permute-start(bf16[512,1024]{0,1:T(8,128)(2,1)} %bitcast.8), channel_id=1, source_target_pairs={{0,0},{1,2},{2,1},{3,3},{4,4},{5,6},{6,5},{7,7},{8,8},{9,10},{10,9... | collective-permute-start | bytes 3145736 | tf_op jit(solution)/shard_map/ppermute | solution.py:252
  6.2 34.0 %collective-permute-start.2 = (s32[8]{0:T(128)S(1)}, s32[8]{0:T(128)S(1)}, u32[]{:S(2)}, u32[]{:S(2)}) collective-permute-start(s32[8]{0:T(128)S(1)} %bitcast.96), channel_id=1, source_target_pairs={{0,2},{2,0},{1,3},{3,1},{4,6},{6,4},{5,7},{7,5},{8,10},{10,8},{9,1... | collective-permute-start | bytes 104 | tf_op jit(solution)/shard_map/ppermute | solution.py:248
  22.0 19.1 %collective-permute-start.1 = (bf16[512,1024]{0,1:T(8,128)(2,1)S(1)}, bf16[512,1024]{0,1:T(8,128)(2,1)S(1)}, u32[]{:S(2)}, u32[]{:S(2)}) collective-permute-start(bf16[512,1024]{0,1:T(8,128)(2,1)S(1)} %collective-permute-done), channel_id=1, source_target_pairs={{0,2},{2,0},{1,3},{3,1},{4,6},{6,4},{5,7},{7,5},{8,10},{10,8},{9,1... | collective-permute-start | bytes 3145736 | tf_op jit(solution)/shard_map/ppermute | solution.py:248
  22.1 20.0 %collective-permute-start.7 = (bf16[512,1024]{0,1:T(8,128)(2,1)S(1)}, bf16[512,1024]{0,1:T(8,128)(2,1)}, u32[]{:S(2)}, u32[]{:S(2)}) collective-permute-start(bf16[512,1024]{0,1:T(8,128)(2,1)S(1)} %collective-permute-done.6), channel_id=1, source_target_pairs={{0,2},{2,0},{1,3},{3,1},{4,6},{6,4},{5,7},{7,5},{8,10},{10,8},{9,1... | collective-permute-start | bytes 3145736 | tf_op jit(solution)/shard_map/ppermute | solution.py:248
  70.5 10.6 %collective-permute-start.3 = (bf16[512,1024]{1,0:T(8,128)(2,1)}, bf16[512,1024]{1,0:T(8,128)(2,1)}, u32[]{:S(2)}, u32[]{:S(2)}) collective-permute-start(bf16[512,1024]{1,0:T(8,128)(2,1)} %get-tuple-element.21), channel_id=1, source_target_pairs={{0,2},{2,0},{1,3},{3,1},{4,6},{6,4},{5,7},{7,5},{8,10},{10,8},{9,1... | collective-permute-start | bytes 3145736 | tf_op jit(solution)/shard_map/ppermute | solution.py:248
  152.5 128.1 %collective-permute-start.46 = (bf16[2,1,576,1024]{3,2,1,0:T(8,128)(2,1)}, bf16[2,1,576,1024]{3,2,1,0:T(8,128)(2,1)}, u32[]{:S(2)}, u32[]{:S(2)}) collective-permute-start(bf16[2,1,576,1024]{3,2,1,0:T(8,128)(2,1)} %get-tuple-element.80), channel_id=1, source_target_pairs={{0,4},{4,0},{1,5},{5,1},{2,6},{6,2},{3,7},{7,3},{8,12},{12,8},{9,1... | collective-permute-start | bytes 7077896 | tf_op jit(solution)/shard_map/ppermute | solution.py:248
  155.7 119.9 %collective-permute-start.41 = (bf16[2,1,2,128,2304]{4,3,2,1,0:T(8,128)(2,1)}, bf16[2,1,2,128,2304]{4,3,2,1,0:T(8,128)(2,1)}, u32[]{:S(2)}, u32[]{:S(2)}) collective-permute-start(bf16[2,1,2,128,2304]{4,3,2,1,0:T(8,128)(2,1)} %get-tuple-element.82), channel_id=1, source_target_pairs={{0,8},{8,0},{1,9},{9,1},{2,10},{10,2},{3,11},{11,3},{4,12},{12,4},... | collective-permute-start | bytes 7077896 | tf_op jit(solution)/shard_map/ppermute | solution.py:248
  164.4 106.2 %collective-permute-start.36 = (bf16[2,2,2,128,1152]{4,3,2,1,0:T(8,128)(2,1)}, bf16[2,2,2,128,1152]{4,3,2,1,0:T(8,128)(2,1)}, u32[]{:S(2)}, u32[]{:S(2)}) collective-permute-start(bf16[2,2,2,128,1152]{4,3,2,1,0:T(8,128)(2,1)} %get-tuple-element.84), channel_id=1, source_target_pairs={{0,1},{1,0},{2,3},{3,2},{4,5},{5,4},{6,7},{7,6},{8,9},{9,8},{10,11... | collective-permute-start | bytes 7077896 | tf_op jit(solution)/shard_map/ppermute | solution.py:248
  174.9 18.0 %collective-permute-start.8 = (bf16[1024,1024]{0,1:T(8,128)(2,1)S(1)}, bf16[1024,1024]{0,1:T(8,128)(2,1)S(1)}, u32[]{:S(2)}, u32[]{:S(2)}) collective-permute-start(bf16[1024,1024]{0,1:T(8,128)(2,1)S(1)} %get-tuple-element.131), channel_id=1, source_target_pairs={{0,2},{2,0},{1,3},{3,1},{4,6},{6,4},{5,7},{7,5},{8,10},{10,8},{9,1... | collective-permute-start | bytes 6291464 | tf_op jit(solution)/shard_map/ppermute | solution.py:248
  175.2 5.5 %collective-permute-start.4 = (bf16[512,1024]{0,1:T(8,128)(2,1)S(1)}, bf16[512,1024]{0,1:T(8,128)(2,1)S(1)}, u32[]{:S(2)}, u32[]{:S(2)}) collective-permute-start(bf16[512,1024]{0,1:T(8,128)(2,1)S(1)} %select_convert_fusion.1), channel_id=1, source_target_pairs={{0,2},{2,0},{1,3},{3,1},{4,6},{6,4},{5,7},{7,5},{8,10},{10,8},{9,1... | collective-permute-start | bytes 3145736 | tf_op jit(solution)/shard_map/ppermute | solution.py:248
  183.5 67.2 %collective-permute-start.5 = (bf16[512,1024]{0,1:T(8,128)(2,1)}, bf16[512,1024]{0,1:T(8,128)(2,1)}, u32[]{:S(2)}, u32[]{:S(2)}) collective-permute-start(bf16[512,1024]{0,1:T(8,128)(2,1)} %get-tuple-element.68), channel_id=1, source_target_pairs={{0,0},{1,2},{2,1},{3,3},{4,4},{5,6},{6,5},{7,7},{8,8},{9,10},{10,9... | collective-permute-start | bytes 3145736 | tf_op jit(solution)/shard_map/ppermute | solution.py:252
  200.8 146.8 %collective-permute-start.31 = (bf16[2,2,2,128,256]{4,3,2,1,0:T(8,128)(2,1)}, bf16[2,2,2,128,256]{4,3,2,1,0:T(8,128)(2,1)}, u32[]{:S(2)}, u32[]{:S(2)}) collective-permute-start(bf16[2,2,2,128,256]{4,3,2,1,0:T(8,128)(2,1)} %get-tuple-element.104), channel_id=1, source_target_pairs={{0,1},{1,0},{2,3},{3,2},{4,5},{5,4},{6,7},{7,6},{8,9},{9,8},{10,11... | collective-permute-start | bytes 1572872 | tf_op jit(solution)/shard_map/ppermute | solution.py:248
  250.7 33.3 %collective-permute-start.26 = (bf16[2,2,1,128,256]{4,3,2,1,0:T(8,128)(2,1)}, bf16[2,2,1,128,256]{4,3,2,1,0:T(8,128)(2,1)}, u32[]{:S(2)}, u32[]{:S(2)}) collective-permute-start(bf16[2,2,1,128,256]{4,3,2,1,0:T(8,128)(2,1)} %get-tuple-element.112), channel_id=1, source_target_pairs={{0,4},{4,0},{1,5},{5,1},{2,6},{6,2},{3,7},{7,3},{8,12},{12,8},{9,1... | collective-permute-start | bytes 786440 | tf_op jit(solution)/shard_map/ppermute | solution.py:248
  271.4 25.3 %collective-permute-start.21 = (bf16[2,2,1,128,256]{4,3,2,1,0:T(8,128)(2,1)S(1)}, bf16[2,2,1,128,256]{4,3,2,1,0:T(8,128)(2,1)S(1)}, u32[]{:S(2)}, u32[]{:S(2)}) collective-permute-start(bf16[2,2,1,128,256]{4,3,2,1,0:T(8,128)(2,1)S(1)} %copy-done.74), channel_id=1, source_target_pairs={{0,4},{4,0},{1,5},{5,1},{2,6},{6,2},{3,7},{7,3},{8,12},{12,8},{9,1... | collective-permute-start | bytes 786440 | tf_op jit(solution)/shard_map/ppermute | solution.py:248
  275.6 74.9 %collective-permute-start.16 = (bf16[2,2,2,128,256]{4,3,2,1,0:T(8,128)(2,1)S(1)}, bf16[2,2,2,128,256]{4,3,2,1,0:T(8,128)(2,1)S(1)}, u32[]{:S(2)}, u32[]{:S(2)}) collective-permute-start(bf16[2,2,2,128,256]{4,3,2,1,0:T(8,128)(2,1)S(1)} %get-tuple-element.106), channel_id=1, source_target_pairs={{0,1},{1,0},{2,3},{3,2},{4,5},{5,4},{6,7},{7,6},{8,9},{9,8},{10,11... | collective-permute-start | bytes 1572872 | tf_op jit(solution)/shard_map/ppermute | solution.py:248
  280.6 138.9 %collective-permute-start.9 = (bf16[512,1024]{0,1:T(8,128)(2,1)S(1)}, bf16[512,1024]{0,1:T(8,128)(2,1)S(1)}, u32[]{:S(2)}, u32[]{:S(2)}) collective-permute-start(bf16[512,1024]{0,1:T(8,128)(2,1)S(1)} %select_convert_fusion), channel_id=1, source_target_pairs={{0,2},{2,0},{1,3},{3,1},{4,6},{6,4},{5,7},{7,5},{8,10},{10,8},{9,1... | collective-permute-start | bytes 3145736 | tf_op jit(solution)/shard_map/ppermute | solution.py:248
  283.9 158.8 %collective-permute-start.47 = (bf16[2,1,576,512]{3,2,1,0:T(8,128)(2,1)}, bf16[2,1,576,512]{3,2,1,0:T(8,128)(2,1)}, u32[]{:S(2)}, u32[]{:S(2)}) collective-permute-start(bf16[2,1,576,512]{3,2,1,0:T(8,128)(2,1)} %add_convert_fusion), channel_id=1, source_target_pairs={{0,1},{1,0},{2,3},{3,2},{4,5},{5,4},{6,7},{7,6},{8,9},{9,8},{10,11... | collective-permute-start | bytes 3538952 | tf_op jit(solution)/shard_map/ppermute | solution.py:248
  296.6 21.6 %collective-permute-start.27 = (bf16[2,2,1,128,128]{4,3,2,1,0:T(8,128)(2,1)S(1)}, bf16[2,2,1,128,128]{4,3,2,1,0:T(8,128)(2,1)S(1)}, u32[]{:S(2)}, u32[]{:S(2)}) collective-permute-start(bf16[2,2,1,128,128]{4,3,2,1,0:T(8,128)(2,1)S(1)} %add_convert_fusion.11), channel_id=1, source_target_pairs={{0,1},{1,0},{2,3},{3,2},{4,5},{5,4},{6,7},{7,6},{8,9},{9,8},{10,11... | collective-permute-start | bytes 393224 | tf_op jit(solution)/shard_map/ppermute | solution.py:248
  318.3 5.5 %collective-permute-start.22 = (bf16[2,2,1,128,128]{4,3,2,1,0:T(8,128)(2,1)S(1)}, bf16[2,2,1,128,128]{4,3,2,1,0:T(8,128)(2,1)S(1)}, u32[]{:S(2)}, u32[]{:S(2)}) collective-permute-start(bf16[2,2,1,128,128]{4,3,2,1,0:T(8,128)(2,1)S(1)} %add_convert_fusion.12), channel_id=1, source_target_pairs={{0,1},{1,0},{2,3},{3,2},{4,5},{5,4},{6,7},{7,6},{8,9},{9,8},{10,11... | collective-permute-start | bytes 393224 | tf_op jit(solution)/shard_map/ppermute | solution.py:248
  323.8 4.3 collective-permute-start.28
  328.0 4.3 collective-permute-start.23
  332.3 5.7 %collective-permute-start.29 = (bf16[1,1,1,128,128]{4,3,2,1,0:T(8,128)(2,1)S(1)}, bf16[1,1,1,128,128]{4,3,2,1,0:T(8,128)(2,1)S(1)}, u32[]{:S(2)}, u32[]{:S(2)}) collective-permute-start(bf16[1,1,1,128,128]{4,3,2,1,0:T(8,128)(2,1)S(1)} %add_convert_fusion.18), channel_id=1, source_target_pairs={{0,16},{16,0},{1,17},{17,1},{2,18},{18,2},{3,19},{19,3},{4,20},{20... | collective-permute-start | bytes 98312 | tf_op jit(solution)/shard_map/ppermute | solution.py:248
  338.0 4.8 collective-permute-start.24
  345.2 100.2 %collective-permute-start.42 = (bf16[1,1,2,128,2304]{4,3,2,1,0:T(8,128)(2,1)}, bf16[1,1,2,128,2304]{4,3,2,1,0:T(8,128)(2,1)}, u32[]{:S(2)}, u32[]{:S(2)}) collective-permute-start(bf16[1,1,2,128,2304]{4,3,2,1,0:T(8,128)(2,1)} %add_convert_fusion.1), channel_id=1, source_target_pairs={{0,16},{16,0},{1,17},{17,1},{2,18},{18,2},{3,19},{19,3},{4,20},{20... | collective-permute-start | bytes 3538952 | tf_op jit(solution)/shard_map/ppermute | solution.py:248
  347.6 100.6 %collective-permute-start.37 = (bf16[2,2,1,128,1152]{4,3,2,1,0:T(8,128)(2,1)}, bf16[2,2,1,128,1152]{4,3,2,1,0:T(8,128)(2,1)}, u32[]{:S(2)}, u32[]{:S(2)}) collective-permute-start(bf16[2,2,1,128,1152]{4,3,2,1,0:T(8,128)(2,1)} %add_convert_fusion.2), channel_id=1, source_target_pairs={{0,4},{4,0},{1,5},{5,1},{2,6},{6,2},{3,7},{7,3},{8,12},{12,8},{9,1... | collective-permute-start | bytes 3538952 | tf_op jit(solution)/shard_map/ppermute | solution.py:248
  350.5 30.7 %collective-permute-start.32 = (bf16[2,2,1,128,256]{4,3,2,1,0:T(8,128)(2,1)S(1)}, bf16[2,2,1,128,256]{4,3,2,1,0:T(8,128)(2,1)S(1)}, u32[]{:S(2)}, u32[]{:S(2)}) collective-permute-start(bf16[2,2,1,128,256]{4,3,2,1,0:T(8,128)(2,1)S(1)} %add_convert_fusion.8), channel_id=1, source_target_pairs={{0,4},{4,0},{1,5},{5,1},{2,6},{6,2},{3,7},{7,3},{8,12},{12,8},{9,1... | collective-permute-start | bytes 786440 | tf_op jit(solution)/shard_map/ppermute | solution.py:248
  381.2 7.3 %collective-permute-start.17 = (bf16[2,2,1,128,256]{4,3,2,1,0:T(8,128)(2,1)S(1)}, bf16[2,2,1,128,256]{4,3,2,1,0:T(8,128)(2,1)S(1)}, u32[]{:S(2)}, u32[]{:S(2)}) collective-permute-start(bf16[2,2,1,128,256]{4,3,2,1,0:T(8,128)(2,1)S(1)} %add_convert_fusion.9), channel_id=1, source_target_pairs={{0,4},{4,0},{1,5},{5,1},{2,6},{6,2},{3,7},{7,3},{8,12},{12,8},{9,1... | collective-permute-start | bytes 786440 | tf_op jit(solution)/shard_map/ppermute | solution.py:248
  388.5 13.3 %collective-permute-start.33 = (bf16[2,1,1,128,256]{4,3,2,1,0:T(8,128)(2,1)S(1)}, bf16[2,1,1,128,256]{4,3,2,1,0:T(8,128)(2,1)S(1)}, u32[]{:S(2)}, u32[]{:S(2)}) collective-permute-start(bf16[2,1,1,128,256]{4,3,2,1,0:T(8,128)(2,1)S(1)} %add_convert_fusion.10), channel_id=1, source_target_pairs={{0,8},{8,0},{1,9},{9,1},{2,10},{10,2},{3,11},{11,3},{4,12},{12,4},... | collective-permute-start | bytes 393224 | tf_op jit(solution)/shard_map/ppermute | solution.py:248
  401.8 5.4 %collective-permute-start.18 = (bf16[2,1,1,128,256]{4,3,2,1,0:T(8,128)(2,1)S(1)}, bf16[2,1,1,128,256]{4,3,2,1,0:T(8,128)(2,1)S(1)}, u32[]{:S(2)}, u32[]{:S(2)}) collective-permute-start(bf16[2,1,1,128,256]{4,3,2,1,0:T(8,128)(2,1)S(1)} %add_convert_fusion.13), channel_id=1, source_target_pairs={{0,8},{8,0},{1,9},{9,1},{2,10},{10,2},{3,11},{11,3},{4,12},{12,4},... | collective-permute-start | bytes 393224 | tf_op jit(solution)/shard_map/ppermute | solution.py:248
  407.2 5.6 %collective-permute-start.34 = (bf16[1,1,1,128,256]{4,3,2,1,0:T(8,128)(2,1)S(1)}, bf16[1,1,1,128,256]{4,3,2,1,0:T(8,128)(2,1)S(1)}, u32[]{:S(2)}, u32[]{:S(2)}) collective-permute-start(bf16[1,1,1,128,256]{4,3,2,1,0:T(8,128)(2,1)S(1)} %add_convert_fusion.14), channel_id=1, source_target_pairs={{0,16},{16,0},{1,17},{17,1},{2,18},{18,2},{3,19},{19,3},{4,20},{20... | collective-permute-start | bytes 196616 | tf_op jit(solution)/shard_map/ppermute | solution.py:248
  412.8 5.4 %collective-permute-start.19 = (bf16[1,1,1,128,256]{4,3,2,1,0:T(8,128)(2,1)S(1)}, bf16[1,1,1,128,256]{4,3,2,1,0:T(8,128)(2,1)S(1)}, u32[]{:S(2)}, u32[]{:S(2)}) collective-permute-start(bf16[1,1,1,128,256]{4,3,2,1,0:T(8,128)(2,1)S(1)} %add_convert_fusion.17), channel_id=1, source_target_pairs={{0,16},{16,0},{1,17},{17,1},{2,18},{18,2},{3,19},{19,3},{4,20},{20... | collective-permute-start | bytes 196616 | tf_op jit(solution)/shard_map/ppermute | solution.py:248
  418.2 1.2 collective-permute-start.35
  419.4 4.3 collective-permute-start.20
  423.0 4.6 collective-permute-start.11
  427.6 3.7 collective-permute-start.12
  431.3 3.7 collective-permute-start.13
  436.2 5.4 %collective-permute-start.15 = (f32[17,128]{1,0:T(8,128)S(1)}, f32[17,128]{1,0:T(8,128)S(1)}, u32[]{:S(2)}, u32[]{:S(2)}) collective-permute-start(f32[17,128]{1,0:T(8,128)S(1)} %add.336), channel_id=1, source_target_pairs={{0,1},{1,0},{2,3},{3,2},{4,5},{5,4},{6,7},{7,6},{8,9},{9,8},{10,11... | collective-permute-start | bytes 26120 | tf_op jit(solution)/shard_map/ppermute | solution.py:248
  440.4 40.5 %collective-permute-start.10 = (bf16[512,1024]{0,1:T(8,128)(2,1)S(1)}, bf16[512,1024]{0,1:T(8,128)(2,1)S(1)}, u32[]{:S(2)}, u32[]{:S(2)}) collective-permute-start(bf16[512,1024]{0,1:T(8,128)(2,1)S(1)} %get-tuple-element.61), channel_id=1, source_target_pairs={{0,0},{1,2},{2,1},{3,3},{4,4},{5,6},{6,5},{7,7},{8,8},{9,10},{10,9... | collective-permute-start | bytes 3145736 | tf_op jit(solution)/shard_map/ppermute | solution.py:252
  444.5 29.2 %collective-permute-start.48 = (bf16[1,1,576,512]{3,2,1,0:T(8,128)(2,1)S(1)}, bf16[1,1,576,512]{3,2,1,0:T(8,128)(2,1)S(1)}, u32[]{:S(2)}, u32[]{:S(2)}) collective-permute-start(bf16[1,1,576,512]{3,2,1,0:T(8,128)(2,1)S(1)} %add_convert_fusion.3), channel_id=1, source_target_pairs={{0,16},{16,0},{1,17},{17,1},{2,18},{18,2},{3,19},{19,3},{4,20},{20... | collective-permute-start | bytes 1769480 | tf_op jit(solution)/shard_map/ppermute | solution.py:248
  447.1 31.1 %collective-permute-start.43 = (bf16[1,1,1,128,2304]{4,3,2,1,0:T(8,128)(2,1)S(1)}, bf16[1,1,1,128,2304]{4,3,2,1,0:T(8,128)(2,1)S(1)}, u32[]{:S(2)}, u32[]{:S(2)}) collective-permute-start(bf16[1,1,1,128,2304]{4,3,2,1,0:T(8,128)(2,1)S(1)} %add_convert_fusion.4), channel_id=1, source_target_pairs={{0,4},{4,0},{1,5},{5,1},{2,6},{6,2},{3,7},{7,3},{8,12},{12,8},{9,1... | collective-permute-start | bytes 1769480 | tf_op jit(solution)/shard_map/ppermute | solution.py:248
  449.9 29.9 %collective-permute-start.38 = (bf16[2,1,1,128,1152]{4,3,2,1,0:T(8,128)(2,1)S(1)}, bf16[2,1,1,128,1152]{4,3,2,1,0:T(8,128)(2,1)S(1)}, u32[]{:S(2)}, u32[]{:S(2)}) collective-permute-start(bf16[2,1,1,128,1152]{4,3,2,1,0:T(8,128)(2,1)S(1)} %add_convert_fusion.5), channel_id=1, source_target_pairs={{0,8},{8,0},{1,9},{9,1},{2,10},{10,2},{3,11},{11,3},{4,12},{12,4},... | collective-permute-start | bytes 1769480 | tf_op jit(solution)/shard_map/ppermute | solution.py:248
  476.8 23.5 %collective-permute-start.49 = (bf16[576,512]{1,0:T(8,128)(2,1)}, bf16[576,512]{1,0:T(8,128)(2,1)}, u32[]{:S(2)}, u32[]{:S(2)}) collective-permute-start(bf16[576,512]{1,0:T(8,128)(2,1)} %get-tuple-element.59), channel_id=1, source_target_pairs={{8,0},{2,10},{9,1},{3,11},{12,4},{6,14},{13,5},{7,15},{24,16},{18,... | collective-permute-start | bytes 1769480 | tf_op jit(solution)/shard_map/ppermute | solution.py:519
  479.3 10.1 %collective-permute-start.44 = (bf16[1,1,1,128,1152]{4,3,2,1,0:T(8,128)(2,1)}, bf16[1,1,1,128,1152]{4,3,2,1,0:T(8,128)(2,1)}, u32[]{:S(2)}, u32[]{:S(2)}) collective-permute-start(bf16[1,1,1,128,1152]{4,3,2,1,0:T(8,128)(2,1)} %add_convert_fusion.6), channel_id=1, source_target_pairs={{0,1},{1,0},{2,3},{3,2},{4,5},{5,4},{6,7},{7,6},{8,9},{9,8},{10,11... | collective-permute-start | bytes 884744 | tf_op jit(solution)/shard_map/ppermute | solution.py:248
  480.9 16.5 %collective-permute-start.39 = (bf16[1,1,1,128,1152]{4,3,2,1,0:T(8,128)(2,1)}, bf16[1,1,1,128,1152]{4,3,2,1,0:T(8,128)(2,1)}, u32[]{:S(2)}, u32[]{:S(2)}) collective-permute-start(bf16[1,1,1,128,1152]{4,3,2,1,0:T(8,128)(2,1)} %add_convert_fusion.7), channel_id=1, source_target_pairs={{0,16},{16,0},{1,17},{17,1},{2,18},{18,2},{3,19},{19,3},{4,20},{20... | collective-permute-start | bytes 884744 | tf_op jit(solution)/shard_map/ppermute | solution.py:248
  491.2 7.6 %collective-permute-start.45 = (bf16[64,1152]{1,0:T(8,128)(2,1)S(1)}, bf16[64,1152]{1,0:T(8,128)(2,1)S(1)}, u32[]{:S(2)}, u32[]{:S(2)}) collective-permute-start(bf16[64,1152]{1,0:T(8,128)(2,1)S(1)} %fusion.19), channel_id=1, source_target_pairs={{0,2},{2,0},{1,3},{3,1},{4,6},{6,4},{5,7},{7,5},{8,10},{10,8},{9,1... | collective-permute-start | bytes 442376 | tf_op jit(solution)/shard_map/ppermute | solution.py:248
  498.7 1.4 collective-permute-start.40
  501.6 3.2 collective-permute-start.50
  (94 other events, 1041.5 us)

commit v2 on v1

--- a/solution.py
+++ b/solution.py
@@ -272,10 +272,8 @@
 
 
 def part_rows(w, c):
-    width = w.shape[0] // 4
-    return jnp.concatenate(
-        [lax.dynamic_slice_in_dim(w, (2 * i + c) * width, width, 0) for i in range(2)], axis=0
-    )
+    rows, columns = w.shape
+    return lax.dynamic_index_in_dim(w.reshape(2, 2, rows // 4, columns), c, 1, False).reshape(rows // 2, columns)
 
 
 def rope_rows(values, gain, cosine, sine):
@@ -481,20 +479,150 @@
     )(starts, gain_q, gain_k, cosine, sine, qkv, qkv, qs, ks, vs, logs, d_out)
 
 
+LANES = 128
+
+
+def local_block(i, c, blocks):
+    return lax.div(i, blocks) * 2 * blocks + c * blocks + lax.rem(i, blocks)
+
+
+def ffn_kernel(
+    sel_ref, hn_ref, dm_ref, gate0_ref, gate1_ref, up0_ref, up1_ref, down0_ref, down1_ref,
+    act_ref, dg_ref, du_ref, hz0_ref, hz1_ref, hy0_ref, hy1_ref, dx0_ref, dx1_ref,
+):
+    @pl.when(pl.program_id(0) == 0)
+    def _():
+        x, y, zl = sel_ref[1], sel_ref[2], sel_ref[3]
+        width = hn_ref.shape[1] // 8
+        half = dm_ref.shape[1] // 2
+        for order in range(2):
+            for i in range(4):
+                high, low = divmod(i, 2)
+                to = slice(i * width, (i + 1) * width)
+                bit = zl if order else 1 - zl
+                block = 4 * high + 2 * bit + low
+                (hz0_ref, hz1_ref)[order][:, to] = hn_ref[:, pl.ds(pl.multiple_of(block * width, width), width)]
+                bit = y if order else 1 - y
+                block = 4 * high + 2 * low + bit
+                (hy0_ref, hy1_ref)[order][:, to] = hn_ref[:, pl.ds(pl.multiple_of(block * width, width), width)]
+            bit = x if order else 1 - x
+            (dx0_ref, dx1_ref)[order][...] = dm_ref[:, pl.ds(pl.multiple_of(bit * half, half), half)]
+
+    gate_w = jnp.concatenate([gate0_ref[...], gate1_ref[...]], axis=1)
+    up_w = jnp.concatenate([up0_ref[...], up1_ref[...]], axis=1)
+    down_w = jnp.concatenate([down0_ref[...], down1_ref[...]], axis=0)
+    gate = dot(hn_ref[...], gate_w, 1, 0)
+    up = dot(hn_ref[...], up_w, 1, 0)
+    d_act = dot(dm_ref[...], down_w, 1, 1)
+    sigmoid = 1.0 / (1.0 + jnp.exp(-gate))
+    silu = gate * sigmoid
+    act_ref[...] = (silu * up).astype(BF16)
+    du_ref[...] = (d_act * silu).astype(BF16)
+    dg_ref[...] = (d_act * up * (sigmoid + silu * (1.0 - sigmoid))).astype(BF16)
+
+
+def feed_forward(sel, hnormed, d_mlp, w_gate, w_up, w_down):
+    tokens, d = hnormed.shape
+    units = w_gate.shape[1] // 2
+    blocks = units // 2 // LANES
+    whole = pl.BlockSpec((tokens, d), lambda j, sel: (0, 0))
+    half = pl.BlockSpec((tokens, d // 2), lambda j, sel: (0, 0))
+    columns = [
+        pl.BlockSpec((d, LANES), lambda j, sel, i=i: (0, local_block(2 * j + i, sel[0], blocks))) for i in range(2)
+    ]
+    rows = [pl.BlockSpec((LANES, d), lambda j, sel, i=i: (local_block(2 * j + i, sel[0], blocks), 0)) for i in range(2)]
+    return pl.pallas_call(
+        ffn_kernel,
+        grid_spec=pltpu.PrefetchScalarGridSpec(
+            num_scalar_prefetch=1,
+            grid=(blocks,),
+            in_specs=[whole, whole] + columns + columns + rows,
+            out_specs=[pl.BlockSpec((tokens, 2 * LANES), lambda j, sel: (0, j))] * 3 + [half] * 6,
+        ),
+        out_shape=[jax.ShapeDtypeStruct((tokens, units), BF16)] * 3 + [jax.ShapeDtypeStruct((tokens, d // 2), BF16)] * 6,
+        name="feed_forward",
+    )(sel, hnormed, d_mlp, w_gate, w_gate, w_up, w_up, w_down, w_down)
+
+
+def ffn_back_kernel(sel_ref, dg_ref, du_ref, gate0_ref, gate1_ref, up0_ref, up1_ref, out_ref, low_ref):
+    gate_w = jnp.concatenate([gate0_ref[...], gate1_ref[...]], axis=1)
+    up_w = jnp.concatenate([up0_ref[...], up1_ref[...]], axis=1)
+    result = dot(dg_ref[...], gate_w, 1, 1) + dot(du_ref[...], up_w, 1, 1)
+    out_ref[...] = result
+    low_ref[...] = result.astype(BF16)
+
+
+def ffn_back(sel, d_gate, d_up, w_gate, w_up):
+    tokens, units = d_gate.shape
+    d = w_gate.shape[0]
+    block = min(256, d)
+    whole = pl.BlockSpec((tokens, units), lambda j, sel: (0, 0))
+    weights = [pl.BlockSpec((block, units // 2), lambda j, sel, i=i: (j, 2 * i + sel[0])) for i in range(2)]
+    return pl.pallas_call(
+        ffn_back_kernel,
+        grid_spec=pltpu.PrefetchScalarGridSpec(
+            num_scalar_prefetch=1,
+            grid=(d // block,),
+            in_specs=[whole, whole] + weights + weights,
+            out_specs=[pl.BlockSpec((tokens, block), lambda j, sel: (0, j))] * 2,
+        ),
+        out_shape=[jax.ShapeDtypeStruct((tokens, d), t) for t in (F32, BF16)],
+        name="feed_forward_back",
+    )(sel, d_gate, d_up, w_gate, w_gate, w_up, w_up)
+
+
+def ffn_out_kernel(sel_ref, act_ref, down0_ref, down1_ref, out_ref):
+    out_ref[...] = dot(act_ref[...], jnp.concatenate([down0_ref[...], down1_ref[...]], axis=0), 1, 0)
+
+
+def ffn_out(sel, act, w_down):
+    tokens, units = act.shape
+    d = w_down.shape[1]
+    block = min(256, d)
+    weights = [pl.BlockSpec((units // 2, block), lambda j, sel, i=i: (2 * i + sel[0], j)) for i in range(2)]
+    return pl.pallas_call(
+        ffn_out_kernel,
+        grid_spec=pltpu.PrefetchScalarGridSpec(
+            num_scalar_prefetch=1,
+            grid=(d // block,),
+            in_specs=[pl.BlockSpec((tokens, units), lambda j, sel: (0, 0))] + weights,
+            out_specs=pl.BlockSpec((tokens, block), lambda j, sel: (0, j)),
+        ),
+        out_shape=jax.ShapeDtypeStruct((tokens, d), F32),
+        name="feed_forward_out",
+    )(sel, act, w_down, w_down)
+
+
+def tie(values, *others):
+    return lax.optimization_barrier((tuple(values), others))[0]
+
+
 def add_up(terms):
     return sum(t.astype(F32) for t in terms)
 
 
-def halve(grad, stages):
-    terms = [grad]
-    for axis, dim in stages:
-        bit = lax.axis_index(axis)
-        size = terms[0].shape[dim] // 2
-        low = [lax.slice_in_dim(t, 0, size, axis=dim) for t in terms]
-        high = [lax.slice_in_dim(t, size, 2 * size, axis=dim) for t in terms]
-        send = add_up([pick(bit, h, l) for l, h in zip(low, high)]).astype(BF16)
-        terms = [pick(bit, l, h) for l, h in zip(low, high)] + [swap(send, axis)]
-    return add_up(terms)
+def leave(terms, dim, bit):
+    size = terms[0].shape[dim] // 2
+    if dim < terms[0].ndim - 2:
+        return add_up([lax.dynamic_slice_in_dim(t, (1 - bit) * size, size, dim) for t in terms]).astype(BF16)
+    low = add_up([lax.slice_in_dim(t, 0, size, axis=dim) for t in terms])
+    high = add_up([lax.slice_in_dim(t, size, 2 * size, axis=dim) for t in terms])
+    return pick(bit, high, low).astype(BF16)
+
+
+def stay(terms, dim, bit):
+    size = terms[0].shape[dim] // 2
+    if dim < terms[0].ndim - 2:
+        return [lax.dynamic_slice_in_dim(t, bit * size, size, dim) for t in terms]
+    return [
+        pick(bit, lax.slice_in_dim(t, 0, size, axis=dim), lax.slice_in_dim(t, size, 2 * size, axis=dim))
+        for t in terms
+    ]
+
+
+def halve(terms, axis, dim):
+    bit = lax.axis_index(axis)
+    return stay(terms, dim, bit) + [swap(leave(terms, dim, bit), axis)]
 
 
 def share_rows(total, c):
@@ -504,45 +632,34 @@
     return in_order(c, own, other, 1)
 
 
-def sum_columns(grad, order, c):
-    rows, columns = grad.shape
-    dims = {"zh": 0, "zl": 1, "y": 2, "x": 4}
-    total = halve(grad.reshape(2, 2, 2, rows // 8, columns), [(a, dims[a]) for a in order])
-    return share_rows(total.reshape(rows // 8, columns // 2), c)
-
-
-def sum_rows(grad, order, c):
-    rows, columns = grad.shape
-    dims = {"zh": 0, "y": 1, "x": 3}
-    total = halve(grad.reshape(2, 2, rows // 4, columns), [(a, dims[a]) for a in order])
-    total = total.reshape(rows // 4, columns // 2)
-    total = total + lax.ppermute(total.astype(BF16), ("zl", "c"), [(2, 0), (1, 3)]).astype(F32)
-    rows = total.shape[0] // 2
-    own = pick(c, total[:rows], total[rows:])
-    other = pick(c, total[rows:], total[:rows]).astype(BF16)
-    other = lax.ppermute(other, ("zl", "c"), [(0, 1), (3, 2)]).astype(F32)
-    return jnp.where(lax.axis_index("zl") == c, own, other)
+def own_rows(v, c, local):
+    return pick(c, v[:local], v[local:])
+
+
+def other_rows(v, c, local):
+    return pick(c, v[local:], v[:local])
 
 
 def pair_body(
     tokens, cotangent, doc_lengths, attn_gain, w_query, w_key, w_value, query_gain, key_gain, w_out,
     ffn_gain, w_gate, w_up, w_down,
 ):
-    local = tokens.shape[1]
+    local, d = tokens.shape[1:]
     length = 2 * local
     size = query_gain.shape[0]
     kv_count = w_key.shape[1] // size
     group = w_query.shape[1] // w_key.shape[1]
     pairs = kv_count // 4
-    c, x = lax.axis_index("c"), lax.axis_index("x")
+    zh, zl, y, c, x = [lax.axis_index(a) for a in AXES]
     gain_attn = attn_gain.astype(F32)
     gain_ffn = ffn_gain.astype(F32)
     gain_q = query_gain.astype(F32)[:, None]
     gain_k = key_gain.astype(F32)[:, None]
 
     own_tokens = transpose_pair(tokens[0])
-    inputs_low = in_order(c, own_tokens, swap(own_tokens, "c"), 0)
-    own_cot = transpose_pair(cotangent[0])
+    other_tokens = swap(own_tokens, "c")
+    (cot_low,) = tie([cotangent[0]], own_tokens)
+    own_cot = transpose_pair(cot_low)
     d_mlp = in_order(c, own_cot, swap(own_cot, "c"), 0)
     lengths = jnp.where(c == x, doc_lengths[0], swap(doc_lengths[0], "c"))
     ends = jnp.cumsum(lengths)
@@ -555,85 +672,85 @@
 
     parts = [part_columns(w, c) for w in (w_query, w_key, w_value)]
     w_qkv = jnp.concatenate([p[i] for i in range(2) for p in parts], axis=1)
-    gate_w = jnp.concatenate(part_columns(w_gate, c), axis=1)
-    up_w = jnp.concatenate(part_columns(w_up, c), axis=1)
-    down_w = part_rows(w_down, c)
     out_w = part_rows(w_out, c)
-
-    inputs = inputs_low.astype(F32)
+    sel = jnp.stack([c, x, y, zl]).astype(jnp.int32)
+    w_qkv, out_w, cosine, sine, starts, sel, other_tokens = tie(
+        (w_qkv, out_w, cosine, sine, starts, sel, other_tokens)
+    )
+
+    inputs = in_order(c, own_tokens, other_tokens, 0).astype(F32)
     normed = rms_scale(inputs, gain_attn).astype(BF16)
     qkv = dot(w_qkv, normed, 0, 1)
     attended_own, logs, qs, ks, vs = attention(qkv, starts, gain_q, gain_k, cosine, sine, size, group, pairs)
     attended_other = swap(attended_own, "c")
-    quarter = attended_own.shape[0] // 2
+    width = attended_own.shape[0] // 2
     attended = jnp.concatenate(
-        [
-            piece
-            for i in range(2)
-            for piece in (
-                pick(c, attended_own[i * quarter : (i + 1) * quarter], attended_other[i * quarter : (i + 1) * quarter]),
-                pick(c, attended_other[i * quarter : (i + 1) * quarter], attended_own[i * quarter : (i + 1) * quarter]),
-            )
-        ],
-        axis=0,
+        [in_order(c, attended_own[i : i + width], attended_other[i : i + width], 0) for i in (0, width)], axis=0
     )
     hidden = inputs + dot(attended, w_out, 0, 0)
     hnormed = rms_scale(hidden, gain_ffn).astype(BF16)
 
-    gate = dot(hnormed, gate_w, 1, 0)
-    up_part = dot(hnormed, up_w, 1, 0)
-    sigmoid_gate = jax.nn.sigmoid(gate)
-    silu_gate = gate * sigmoid_gate
-    act = (silu_gate * up_part).astype(BF16)
-    d_act = dot(d_mlp, down_w, 1, 1)
-    d_up = (d_act * silu_gate).astype(BF16)
-    d_gate = (d_act * up_part * sigmoid_gate * (1.0 + gate * (1.0 - sigmoid_gate))).astype(BF16)
-    grad_down = dot(act, d_mlp, 0, 0).astype(BF16)
-    grad_gate = dot(hnormed, d_gate, 0, 0).astype(BF16)
-    grad_up = dot(hnormed, d_up, 0, 0).astype(BF16)
-    sum_down = sum_rows(grad_down, ("y", "x", "zh"), c)
-    sum_gate = sum_columns(grad_gate, ("x", "y", "zl", "zh"), c)
-    sum_up = sum_columns(grad_up, ("zl", "zh", "y", "x"), c)
-
-    d_hn = dot(d_gate, gate_w, 1, 1) + dot(d_up, up_w, 1, 1)
-    d_hn = d_hn + swap(d_hn.astype(BF16), "c").astype(F32)
+    act, d_gate, d_up, hn_z0, hn_z1, hn_y0, hn_y1, dm_x0, dm_x1 = feed_forward(
+        sel, hnormed, d_mlp, w_gate, w_up, w_down
+    )
+    send_up = dot(hn_z0, d_up, 0, 0).astype(BF16)
+    send_down = dot(act, dm_x0, 0, 0).astype(BF16)
+    send_gate = dot(hn_y0, d_gate, 0, 0).astype(BF16)
+    come_up, come_down, come_gate = swap(send_up, "zl"), swap(send_down, "x"), swap(send_gate, "y")
+    d_gate, d_up, act = tie((d_gate, d_up, act), send_up, send_down, send_gate)
+    d_hn, d_hn_low = ffn_back(sel, d_gate, d_up, w_gate, w_up)
+    d_hn_other = swap(d_hn_low, "c")
+    hn_z1, hn_y1, dm_x1 = tie((hn_z1, hn_y1, dm_x1), d_hn)
+    keep_up = dot(hn_z1, d_up, 0, 0).astype(BF16)
+    keep_down = dot(act, dm_x1, 0, 0).astype(BF16)
+    keep_gate = dot(hn_y1, d_gate, 0, 0).astype(BF16)
+    (d_hn_other,) = tie((d_hn_other,), keep_up)
+    d_hn = d_hn + d_hn_other.astype(F32)
     d_hidden_norm, ffn_gain_terms = norm_back(d_hn, hidden, gain_ffn)
     d_hidden = d_mlp.astype(F32) + d_hidden_norm
     d_attn = d_hidden.astype(BF16)
+    d_attended = dot(out_w, d_attn, 1, 1).astype(BF16)
+    units = d_gate.shape[1]
+    rows = d // 8
     d_attn_part = jnp.concatenate(part_columns(d_attn, c), axis=1)
-    grad_out = dot(attended, d_attn_part, 1, 0).astype(BF16)
-    sum_out = sum_columns(grad_out, ("x", "y", "zl", "zh"), c)
-    d_attended = dot(out_w, d_attn, 1, 1).astype(BF16)
+    attended_y = attended.reshape(4, 2, rows, length)
+    send_out = dot(lax.dynamic_index_in_dim(attended_y, 1 - y, 1, False).reshape(d // 2, length), d_attn_part, 1, 0)
+    keep_out = dot(lax.dynamic_index_in_dim(attended_y, y, 1, False).reshape(d // 2, length), d_attn_part, 1, 0)
+    send_out, keep_out = send_out.astype(BF16), keep_out.astype(BF16)
+    come_out = swap(send_out, "y")
+    (d_attended,) = tie((d_attended,), keep_up, keep_down, keep_gate, send_out, keep_out)
     d_qkv, gain_q_terms, gain_k_terms = attention_back(
         qkv, qs, ks, vs, logs, d_attended, starts, gain_q, gain_k, cosine, sine, size, group, pairs
     )
-    grad_qkv = dot(normed, d_qkv, 0, 1).astype(BF16)
-    sum_qkv = []
-    width = grad_qkv.shape[1] // 2
-    q_width = pairs * group * size
-    q_part = jnp.concatenate([grad_qkv[:, i * width : i * width + q_width] for i in range(2)], axis=1)
-    k_part = jnp.concatenate([grad_qkv[:, i * width + q_width : i * width + q_width + pairs * size] for i in range(2)], axis=1)
-    v_part = jnp.concatenate([grad_qkv[:, i * width + q_width + pairs * size : (i + 1) * width] for i in range(2)], axis=1)
-    sum_query = sum_columns(q_part, ("x", "y", "zl", "zh"), c)
-    sum_key = sum_columns(k_part, ("y", "x", "zl", "zh"), c)
-    sum_value = sum_columns(v_part, ("y", "x", "zl", "zh"), c)
-
-    def own_rows(v):
-        return pick(c, v[:local], v[local:])
-
-    def other_rows(v):
-        return pick(c, v[local:], v[:local])
-
+
+    come_up, come_down, come_gate, d_qkv = tie((come_up, come_down, come_gate, d_qkv))
+    up = [v.reshape(2, 2, rows, units) for v in (keep_up, come_up)]
+    down = [v.reshape(2, 2, units // 4, d // 2) for v in (keep_down, come_down)]
+    gate = [v.reshape(2, 2, rows, units) for v in (keep_gate, come_gate)]
+    send_gate, send_down, send_up = leave(gate, 1, zl), leave(down, 1, y), leave(up, 3, x)
+    gate = stay(gate, 1, zl) + [swap(send_gate, "zl")]
+    down = stay(down, 1, y) + [swap(send_down, "y")]
+    up = stay(up, 3, x) + [swap(send_up, "x")]
+
+    (d_qkv,) = tie((d_qkv,), send_gate, send_down, send_up)
+    width = d_qkv.shape[0] // 2
+    send_qkv = dot(normed, lax.dynamic_slice_in_dim(d_qkv, (1 - x) * width, width, 0), 0, 1).astype(BF16)
+    come_qkv = swap(send_qkv, "x")
+    (d_qkv,) = tie((d_qkv,), send_qkv)
     part = dot(d_qkv, w_qkv, 0, 1)
-    d_normed = own_rows(part) + swap(other_rows(part).astype(BF16), "c").astype(F32)
-    d_input_norm, attn_gain_terms = norm_back(d_normed, own_rows(inputs), gain_attn)
-    d_inputs = own_rows(d_hidden) + d_input_norm
-    part = dot(act, down_w, 1, 0)
-    output = own_rows(hidden) + own_rows(part) + swap(other_rows(part).astype(BF16), "c").astype(F32)
-    stays = c == x
-    output = jnp.where(stays, output, transpose_pair(output.astype(BF16)).astype(F32))
-    d_inputs = jnp.where(stays, d_inputs, transpose_pair(d_inputs.astype(BF16)).astype(F32))
-
+    part_low = other_rows(part, c, local).astype(BF16)
+    part_other = swap(part_low, "c")
+    d_qkv, act = tie((d_qkv, act), part_low)
+    keep_qkv = dot(normed, lax.dynamic_slice_in_dim(d_qkv, x * width, width, 0), 0, 1).astype(BF16)
+    part_out = ffn_out(sel, act, w_down)
+    out_low = other_rows(part_out, c, local).astype(BF16)
+    out_other = swap(out_low, "c")
+    d_normed = own_rows(part, c, local) + part_other.astype(F32)
+    d_input_norm, attn_gain_terms = norm_back(d_normed, own_rows(inputs, c, local), gain_attn)
+    d_inputs = own_rows(d_hidden, c, local) + d_input_norm
+    output = own_rows(hidden, c, local) + own_rows(part_out, c, local) + out_other.astype(F32)
+    output_low, d_inputs_low = output.astype(BF16), d_inputs.astype(BF16)
+    output_other, d_inputs_other = transpose_pair(output_low), transpose_pair(d_inputs_low)
     gains = jnp.concatenate(
         [
             jnp.sum(attn_gain_terms, axis=0),
@@ -642,10 +759,66 @@
             jnp.sum(gain_k_terms, axis=1),
         ]
     ).reshape(-1, 128)
-    for axis in AXES:
+
+    tied = gate[-1], down[-1], up[-1]
+    gate[-1], down[-1], up[-1] = tie(tied, output_low, d_inputs_low, gains, keep_qkv)
+    send_gate, send_down, send_up = leave(gate, 3, x), add_up(down).astype(BF16), leave(up, 1, y)
+    gate = stay(gate, 3, x) + [swap(send_gate, "x")]
+    down = down + [lax.ppermute(send_down, ("zl", "c"), [(2, 0), (1, 3)])]
+    up = stay(up, 1, y) + [swap(send_up, "y")]
+
+    come_out, come_qkv = tie((come_out, come_qkv), send_gate, send_down, send_up)
+    out = [v.reshape(2, 2, 1, rows, d // 2) for v in (keep_out, come_out)]
+    qkv_grad = [v.reshape(2, 2, 2, rows, width) for v in (keep_qkv, come_qkv)]
+    send_out, send_qkv = leave(out, 4, x), leave(qkv_grad, 2, y)
+    out = stay(out, 4, x) + [swap(send_out, "x")]
+    qkv_grad = stay(qkv_grad, 2, y) + [swap(send_qkv, "y")]
+
+    tied = gate[-1], down[-1], up[-1]
+    gate[-1], down[-1], up[-1] = tie(tied, send_out, send_qkv)
+    send_gate, send_down, send_up = leave(gate, 0, zh), leave(down, 0, zh), leave(up, 0, zh)
+    gate = stay(gate, 0, zh) + [swap(send_gate, "zh")]
+    down = stay(down, 0, zh) + [swap(send_down, "zh")]
+    up = stay(up, 0, zh) + [swap(send_up, "zh")]
+
+    out[-1], qkv_grad[-1] = tie((out[-1], qkv_grad[-1]), send_gate, send_down, send_up)
+    send_out, send_qkv = leave(out, 1, zl), leave(qkv_grad, 1, zl)
+    out = stay(out, 1, zl) + [swap(send_out, "zl")]
+    qkv_grad = stay(qkv_grad, 1, zl) + [swap(send_qkv, "zl")]
+    for axis in AXES[:2]:
+        gains = gains + swap(gains, axis)
+    out[-1], qkv_grad[-1] = tie((out[-1], qkv_grad[-1]), gains)
+    send_out, send_qkv = leave(out, 0, zh), leave(qkv_grad, 0, zh)
+    out = stay(out, 0, zh) + [swap(send_out, "zh")]
+    qkv_grad = stay(qkv_grad, 0, zh) + [swap(send_qkv, "zh")]
+    for axis in AXES[2:]:
         gains = gains + swap(gains, axis)
     gains = gains.reshape(-1)
-    d = tokens.shape[2]
+
+    tied = gate[-1], down[-1], up[-1]
+    gate[-1], down[-1], up[-1] = tie(tied, send_out, send_qkv)
+    total = add_up(down).reshape(-1, d // 2)
+    n = total.shape[0] // 2
+    own = pick(c, total[:n], total[n:])
+    other = pick(c, total[n:], total[:n]).astype(BF16)
+    other = lax.ppermute(other, ("zl", "c"), [(0, 1), (3, 2)]).astype(F32)
+    sum_down = jnp.where(zl == c, own, other)
+    sum_gate, sum_up = [share_rows(add_up(t).reshape(rows, units // 2), c) for t in (gate, up)]
+    out[-1], qkv_grad[-1] = tie((out[-1], qkv_grad[-1]), sum_gate, sum_up, sum_down)
+    both = jnp.concatenate([add_up(t).reshape(rows, -1) for t in (out, qkv_grad)], axis=1)
+    n = rows // 2
+    own = pick(c, both[:n], both[n:])
+    other = swap(pick(c, both[n:], both[:n]).astype(BF16), "c").astype(F32)
+    first, second = pick(c, own, other), pick(c, other, own)
+    out_width, q_width, kv_width = d // 4, pairs * group * size, pairs * size
+    ends_of = [0, out_width, out_width + q_width, out_width + q_width + kv_width, out_width + q_width + 2 * kv_width]
+    sum_out, sum_query, sum_key, sum_value = [
+        jnp.concatenate([first[:, low:high], second[:, low:high]], axis=1)
+        for low, high in zip(ends_of[:-1], ends_of[1:])
+    ]
+    stays = c == x
+    output = jnp.where(stays, output, output_other.astype(F32))
+    d_inputs = jnp.where(stays, d_inputs, d_inputs_other.astype(F32))
     return (
         output[None],
         d_inputs[None],

time: 513 us -> 395 us (0.77)
  waiting for transfers between devices: 144 us -> 82.2 us
  Pallas kernels: 42.6 us -> 95.6 us
  matrix products: 95.6 us -> 53.1 us
  local copies, waits for them, and re-layouts: 56 us -> 22.1 us
  other arithmetic: 102 us -> 73 us
    ppermute x45 -> x34, waiting for transfers between devices: 144 us -> 82.2 us  [swap(): return lax.ppermute(v, axis, [(0, 1), (1, 0)])]
    pallas_call x0 -> x3, Pallas kernels: none -> 53 us  [the longest x1 25.3 us: feed_forward(): pl.pallas_call(ffn_kernel, grid_spec=pltpu.PrefetchScalarGridSpec(num_sca...]
    dot_general x15 -> x14, matrix products: 95.6 us -> 53.1 us  [dot(): lax.dot_general(left, right, (((left_dim,), (right_dim,)), ((), ())), pre...]
    select_n x47 -> x12, other arithmetic: 36.3 us -> 12.8 us  [pick(): return jnp.where(bit == 0, low, high)]
    unnamed x191 -> x115, local copies, waits for them, and re-layouts: 27.3 us -> 16.3 us
    dynamic_slice x2 -> x1, local copies, waits for them, and re-layouts: 7.7 us -> 0.14 us  [part_columns(): lax.dynamic_slice_in_dim(w, (2 * i + c) * width, width, 1)]
    reshape x3 -> x0, local copies, waits for them, and re-layouts: 6.54 us -> none  [sum_columns(): grad.reshape(2, 2, 2, rows // 8, columns)]
    dynamic_slice x2, local copies, waits for them, and re-layouts: 7.25 us -> 1.23 us  [the longest x1 1.05 us: part_rows(): lax.dynamic_index_in_dim(w.reshape(2, 2, rows // 4, columns), c, 1, False)]
  transfers between devices with their start and end apart: 51 -> 40, of which waited for: 25 -> 9; matrix products, arithmetic and copies ran while one was open for 32% -> 25% of each run, Pallas kernels for 5% -> 13%
where the time goes in v2:
time: 395 us; the launch traced here: 389 us
  Pallas kernels  95.6 us (24%)
  waiting for transfers between devices  82.2 us (21%)
  other arithmetic  73 us (18%)
  starting transfers between devices  61.5 us (16%)
  matrix products  53.1 us (13%)
  local copies, waits for them, and re-layouts  22.1 us (6%)
    ppermute x34, waiting for transfers between devices, swap(): return lax.ppermute(v, axis, [(0, 1), (1, 0)])  82.2 us
    dot_general x14, matrix products, dot(): lax.dot_general(left, right, (((left_dim,), (right_dim,)), ((), ())), pre...  53.1 us
    ppermute x34, starting transfers between devices, swap(): return lax.ppermute(v, axis, [(0, 1), (1, 0)])  45.2 us
    pallas_call x1, Pallas kernels, feed_forward(): pl.pallas_call(ffn_kernel, grid_spec=pltpu.PrefetchScalarGridSpec(num_sca...  25.3 us
    pallas_call x1, Pallas kernels, attention_back(): pl.pallas_call(attention_back_kernel, grid=(halves, pairs), in_specs=[ful...  24.8 us
    pallas_call x1, Pallas kernels, attention(): pl.pallas_call(attention_kernel, grid=(halves, pairs), in_specs=[full(a)...  17.8 us
    pallas_call x1, Pallas kernels, ffn_back(): pl.pallas_call(ffn_back_kernel, grid_spec=pltpu.PrefetchScalarGridSpec(nu...  17.2 us
    unnamed x115, local copies, waits for them, and re-layouts  16.3 us
  transfers between devices with their start and end apart: 40, of which 9 were waited for; matrix products, arithmetic and copies ran while one was open for 25% of the time, Pallas kernels for 13%

profile of v2, /device:TPU:0, one launch (start us, length us, event | category | flops | bytes accessed | tf_op | source)
XLA Modules:
  0.0 389.3 jit_solution(9026448138524836348)
XLA Ops:
  0.7 2.0 collective-permute-start
  2.7 3.2 collective-permute-start.1
  5.8 9.5 %collective-permute-start.4 = (bf16[512,1024]{1,0:T(8,128)(2,1)}, bf16[512,1024]{1,0:T(8,128)(2,1)}, u32[]{:S(2)}, u32[]{:S(2)}) collective-permute-start(bf16[512,1024]{1,0:T(8,128)(2,1)} %bitcast.127), channel_id=1, source_target_pairs={{0,0},{1,2},{2,1},{3,3},{4,4},{5,6},{6,5},{7,7},{8,8},{9,10},{10,9... | collective-permute-start | bytes 3145736 | tf_op jit(solution)/shard_map/ppermute | solution.py:252
  25.8 6.8 %collective-permute-start.2 = (bf16[512,1024]{1,0:T(8,128)(2,1)S(1)}, bf16[512,1024]{1,0:T(8,128)(2,1)}, u32[]{:S(2)}, u32[]{:S(2)}) collective-permute-start(bf16[512,1024]{1,0:T(8,128)(2,1)S(1)} %collective-permute-done), channel_id=1, source_target_pairs={{0,2},{2,0},{1,3},{3,1},{4,6},{6,4},{5,7},{7,5},{8,10},{10,8},{9,1... | collective-permute-start | bytes 3145736 | tf_op jit(solution)/shard_map/ppermute | solution.py:248
  32.6 2.2 collective-permute-start.5
  42.0 3.4 broadcast_select_fusion.3
  46.8 6.2 %fusion.15.q_ref.k_ref.v_ref = f32[1024,1024]{1,0:T(8,128)} fusion(bf16[1024,1024]{1,0:T(8,128)(2,1)} %dynamic-slice_dynamic-update-slice_fusion.2, f32[1024]{0:T(1024)S(1)} %convert_element_type.403, f32[1024]{0:T(1024)S(1)} %add_rsqrt_fusion.1, bf16[512,1024]{1,0:T(8,128)(2,1)S(1)} %get-tuple-element.180, bf16[512,1024]{1,0:T(8,128)(2,1)S(1)} %get-tuple-element.181), kind=kOutput, calls=%fused_computation.138 | convolution fusion | flops 2154823680 | bytes 8396800 | tf_op jit(solution)/shard_map/dot_general | solution.py:264
  52.9 17.8 %attention_forward.1 = (bf16[512,1024]{1,0:T(8,128)(2,1)}, f32[2,2,2,1024]{3,2,1,0:T(2,128)}, bf16[512,1024]{1,0:T(8,128)(2,1)}, bf16[256,1024]{1,0:T(8,128)(2,1)}, bf16[256,1024]{1,0:T(8,128)(2,1)}) custom-call(s32[1,1024]{1,0:T(1,128)} %bitcast.122, f32[64,1]{1,0:T(8,128)} %copy.36.gain_q_ref, f32[64,1]{1,0:T(8,128)} %copy.37.gain_k_ref, ...), custom_call_target="tpu_custom_call" | custom-call | tf_op jit(solution)/shard_map/attention_forward/pallas_call | solution.py:355
  70.9 2.9 pad_maximum_fusion.2.dm_ref
  77.3 2.7 multiply_reduce_fusion.2
  83.7 25.3 %feed_forward.1 = (bf16[1024,2304]{1,0:T(8,128)(2,1)}, bf16[1024,2304]{1,0:T(8,128)(2,1)}, bf16[1024,2304]{1,0:T(8,128)(2,1)}, bf16[1024,512]{1,0:T(8,128)(2,1)}...) custom-call(s32[4]{0:T(128)} %pad_add_fusion.sel_ref, ...), custom_call_target="tpu_custom_call" | custom-call | tf_op jit(solution)/shard_map/feed_forward/pallas_call | solution.py:534
  109.1 6.9 %convolution_convert_fusion.5 = bf16[512,2304]{1,0:T(8,128)(2,1)} fusion(bf16[1024,512]{1,0:T(8,128)(2,1)} %get-tuple-element.81, bf16[1024,2304]{1,0:T(8,128)(2,1)} %get-tuple-element.93.du_ref), kind=kOutput, calls=%fused_computation.5 | convolution fusion | flops 2417098752 | bytes 8126464 | tf_op jit(solution)/shard_map/dot_general | solution.py:264
  117.6 3.9 %convolution_convert_fusion.4 = bf16[2304,512]{1,0:T(8,128)(2,1)} fusion(bf16[1024,2304]{1,0:T(8,128)(2,1)S(1)} %copy-done.27, bf16[1024,512]{1,0:T(8,128)(2,1)S(1)} %copy-done.49), kind=kOutput, calls=%fused_computation.4 | convolution fusion | flops 2417098752 | bytes 8126464 | tf_op jit(solution)/shard_map/dot_general | solution.py:264
  121.5 2.0 collective-permute-start.7
  123.6 3.9 %convolution_convert_fusion.3 = bf16[512,2304]{1,0:T(8,128)(2,1)} fusion(bf16[1024,512]{1,0:T(8,128)(2,1)S(1)} %copy-done.48, bf16[1024,2304]{1,0:T(8,128)(2,1)S(1)} %bitcast.102), kind=kOutput, calls=%fused_computation.3 | convolution fusion | flops 2417098752 | bytes 8126464 | tf_op jit(solution)/shard_map/dot_general | solution.py:264
  129.2 17.2 %feed_forward_back.1 = (f32[1024,1024]{1,0:T(8,128)}, bf16[1024,1024]{1,0:T(8,128)(2,1)}) custom-call(s32[4]{0:T(128)} %pad_add_fusion.sel_ref, bf16[1024,2304]{1,0:T(8,128)(2,1)} %get-tuple-element.92.dg_ref, bf16[1024,2304]{1,0:T(8,128)(2,1)} %get-tuple-element.93.du_ref, bf16[1024,4608]{1,0:T(8,128)(2,1)} %gate1_ref.3, bf16[1024,4608]{1,0:T(8,128)(2,1)} %gate1_ref.3, ...), custom_call_target="tpu_custom_call" | custom-call | tf_op jit(solution)/shard_map/feed_forward_back/pallas_call | solution.py:561
  146.4 5.3 %convolution_convert_fusion = bf16[512,2304]{1,0:T(8,128)(2,1)S(1)} fusion(bf16[1024,512]{1,0:T(8,128)(2,1)} %get-tuple-element.103, bf16[1024,2304]{1,0:T(8,128)(2,1)} %get-tuple-element.92.dg_ref), kind=kOutput, calls=%fused_computation | convolution fusion | flops 2417098752 | bytes 8126464 | tf_op jit(solution)/shard_map/dot_general | solution.py:264
  153.7 5.8 %convolution_convert_fusion.2 = bf16[512,2304]{1,0:T(8,128)(2,1)S(1)} fusion(bf16[1024,512]{1,0:T(8,128)(2,1)S(1)} %copy-done.47, bf16[1024,2304]{1,0:T(8,128)(2,1)} %get-tuple-element.93.du_ref), kind=kOutput, calls=%fused_computation.2 | convolution fusion | flops 2417098752 | bytes 8126464 | tf_op jit(solution)/shard_map/dot_general | solution.py:264
  161.6 4.0 %convolution_convert_fusion.1 = bf16[2304,512]{1,0:T(8,128)(2,1)} fusion(bf16[1024,2304]{1,0:T(8,128)(2,1)S(1)} %bitcast.104, bf16[1024,512]{1,0:T(8,128)(2,1)S(1)} %copy-done.46), kind=kOutput, calls=%fused_computation.1 | convolution fusion | flops 2417098752 | bytes 8126464 | tf_op jit(solution)/shard_map/dot_general | solution.py:264
  167.1 3.7 fusion.20
  173.7 2.3 convolution_convert_fusion.8.do_ref
  176.0 24.8 %attention_backward.1 = (bf16[1024,1024]{1,0:T(8,128)(2,1)}, f32[64,128]{1,0:T(8,128)}, f32[64,128]{1,0:T(8,128)}) custom-call(s32[1,1024]{1,0:T(1,128)} %bitcast.123, f32[64,1]{1,0:T(8,128)} %copy.36.gain_q_ref, f32[64,1]{1,0:T(8,128)} %copy.37.gain_k_ref, f32[32,1024]{1,0:T(8,128)} %get-tuple-element.75.cos_ref, f32[32,1024]{1,0:T(8,128)} %get-tuple-element.76.sin_ref, ...), custom_call_target="tpu_custom_call" | custom-call | tf_op jit(solution)/shard_map/attention_backward/pallas_call | solution.py:456
  202.6 3.1 add_convert_fusion.2
  205.7 3.4 select_convert_fusion
  209.1 2.8 add_convert_fusion.1
  211.9 2.6 convolution_convert_fusion.7
  214.5 4.0 %fusion.26 = f32[1024,1024]{1,0:T(8,128)S(1)} fusion(bf16[1024,1024]{1,0:T(8,128)(2,1)S(1)} %copy-done.44, bf16[1024,1024]{1,0:T(8,128)(2,1)} %dynamic-slice_dynamic-update-slice_fusion.2), kind=kOutput, calls=%fused_computation.147 | convolution fusion | flops 2147483648 | bytes 8388608 | tf_op jit(solution)/shard_map/dot_general | solution.py:264
  218.5 2.0 copy-done.9
  223.1 10.5 %feed_forward_out.1 = f32[1024,1024]{1,0:T(8,128)} custom-call(s32[4]{0:T(128)} %pad_add_fusion.sel_ref, bf16[1024,2304]{1,0:T(8,128)(2,1)} %get-tuple-element.112.act_ref, bf16[4608,1024]{1,0:T(8,128)(2,1)} %down1_ref.3, bf16[4608,1024]{1,0:T(8,128)(2,1)} %down1_ref.3), custom_call_target="tpu_custom_call" | custom-call | tf_op jit(solution)/shard_map/feed_forward_out/pallas_call | solution.py:583
  233.7 3.5 select_convert_fusion.1
  237.2 2.9 broadcast_select_fusion
  240.1 3.4 multiply_reduce_fusion.4
  243.6 2.6 collective-permute-start.14
  246.2 3.3 convolution_convert_fusion.6
  249.5 3.6 collective-permute-start.15
  255.3 3.2 collective-permute-done.16
  262.2 2.4 fusion.18
  267.4 2.1 select_convert_fusion.3
  269.6 2.7 collective-permute-start.26
  272.3 2.1 add_convert_fusion
  278.8 11.8 %collective-permute-done.20 = bf16[1024,512]{1,0:T(8,128)(2,1)S(1)} collective-permute-done((bf16[1024,512]{1,0:T(8,128)(2,1)S(1)}, bf16[1024,512]{1,0:T(8,128)(2,1)S(1)}, u32[]{:S(2)}, u32[]{:S(2)}) %collective-permute-start.20) | collective-permute-done | bytes 1048608 | tf_op jit(solution)/shard_map/ppermute | solution.py:248
  293.2 23.7 %collective-permute-done.26 = bf16[2,1,128,1152]{3,2,1,0:T(8,128)(2,1)S(1)} collective-permute-done((bf16[2,1,128,1152]{3,2,1,0:T(8,128)(2,1)S(1)}, bf16[2,1,128,1152]{3,2,1,0:T(8,128)(2,1)S(1)}, u32[]{:S(2)}, u32[]{:S(2)}) %collective-permute-start.26) | collective-permute-done | bytes 589856 | tf_op jit(solution)/shard_map/ppermute | solution.py:248
  320.2 2.0 collective-permute-start.34
  324.4 4.5 %collective-permute-done.25 = bf16[2,2,1,128,512]{4,3,2,1,0:T(8,128)(2,1)S(1)} collective-permute-done((bf16[2,2,1,128,512]{4,3,2,1,0:T(8,128)(2,1)S(1)}, bf16[2,2,1,128,512]{4,3,2,1,0:T(8,128)(2,1)S(1)}, u32[]{:S(2)}, u32[]{:S(2)}) %collective-permute-start.25) | collective-permute-done | bytes 524320 | tf_op jit(solution)/shard_map/ppermute | solution.py:248
  333.0 14.9 %collective-permute-done.29 = bf16[2,1,1,128,256]{4,3,2,1,0:T(8,128)(2,1)S(1)} collective-permute-done((bf16[2,1,1,128,256]{4,3,2,1,0:T(8,128)(2,1)S(1)}, bf16[2,1,1,128,256]{4,3,2,1,0:T(8,128)(2,1)S(1)}, u32[]{:S(2)}, u32[]{:S(2)}) %collective-permute-start.29) | collective-permute-done | bytes 131104 | tf_op jit(solution)/shard_map/ppermute | solution.py:248
  348.6 3.0 collective-permute-done.30
  351.7 3.8 collective-permute-start.31
  355.6 20.3 %collective-permute-done.35 = bf16[1,1,128,1152]{3,2,1,0:T(8,128)(2,1)S(1)} collective-permute-done((bf16[1,1,128,1152]{3,2,1,0:T(8,128)(2,1)S(1)}, bf16[1,1,128,1152]{3,2,1,0:T(8,128)(2,1)S(1)}, u32[]{:S(2)}, u32[]{:S(2)}) %collective-permute-start.35) | collective-permute-done | bytes 294944 | tf_op jit(solution)/shard_map/ppermute | solution.py:248
  (263 shorter events, 81.4 us)
Async XLA Ops:
  0.6 38.2 %copy-start = (bf16[1024,1024]{1,0:T(8,128)(2,1)S(1)}, bf16[1024,1024]{1,0:T(8,128)(2,1)}, u32[]{:S(2)}) copy-start(bf16[1024,1024]{1,0:T(8,128)(2,1)} %param.23) | copy-start | bytes 6291460
  0.7 5.2 %collective-permute-start = (bf16[512,1024]{1,0:T(8,128)(2,1)}, bf16[512,1024]{1,0:T(8,128)(2,1)S(1)}, u32[]{:S(2)}, u32[]{:S(2)}) collective-permute-start(bf16[512,1024]{1,0:T(8,128)(2,1)} %bitcast.126), channel_id=1, source_target_pairs={{0,0},{1,2},{2,1},{3,3},{4,4},{5,6},{6,5},{7,7},{8,8},{9,10},{10,9... | collective-permute-start | bytes 3145736 | tf_op jit(solution)/shard_map/ppermute | solution.py:252
  2.7 38.5 %collective-permute-start.1 = (s32[8]{0:T(128)}, s32[8]{0:T(128)S(1)}, u32[]{:S(2)}, u32[]{:S(2)}) collective-permute-start(s32[8]{0:T(128)} %bitcast.125), channel_id=1, source_target_pairs={{0,2},{2,0},{1,3},{3,1},{4,6},{6,4},{5,7},{7,5},{8,10},{10,8},{9,1... | collective-permute-start | bytes 104 | tf_op jit(solution)/shard_map/ppermute | solution.py:248
  5.8 33.0 %copy-start.39 = (bf16[512,1024]{1,0:T(8,128)(2,1)}, bf16[512,1024]{1,0:T(8,128)(2,1)S(1)}, u32[]{:S(2)}) copy-start(bf16[512,1024]{1,0:T(8,128)(2,1)S(1)} %collective-permute-done) | copy-start | bytes 3145732
  5.8 26.8 %collective-permute-start.4 = (bf16[512,1024]{1,0:T(8,128)(2,1)}, bf16[512,1024]{1,0:T(8,128)(2,1)}, u32[]{:S(2)}, u32[]{:S(2)}) collective-permute-start(bf16[512,1024]{1,0:T(8,128)(2,1)} %bitcast.127), channel_id=1, source_target_pairs={{0,0},{1,2},{2,1},{3,3},{4,4},{5,6},{6,5},{7,7},{8,8},{9,10},{10,9... | collective-permute-start | bytes 3145736 | tf_op jit(solution)/shard_map/ppermute | solution.py:252
  23.9 17.2 %copy-start.43 = (s32[1,8]{1,0:T(1,128)S(1)}, s32[1,8]{1,0:T(1,128)}, u32[]{:S(2)}) copy-start(s32[1,8]{1,0:T(1,128)} %param.16) | copy-start | bytes 100
  25.8 16.2 %collective-permute-start.2 = (bf16[512,1024]{1,0:T(8,128)(2,1)S(1)}, bf16[512,1024]{1,0:T(8,128)(2,1)}, u32[]{:S(2)}, u32[]{:S(2)}) collective-permute-start(bf16[512,1024]{1,0:T(8,128)(2,1)S(1)} %collective-permute-done), channel_id=1, source_target_pairs={{0,2},{2,0},{1,3},{3,1},{4,6},{6,4},{5,7},{7,5},{8,10},{10,8},{9,1... | collective-permute-start | bytes 3145736 | tf_op jit(solution)/shard_map/ppermute | solution.py:248
  32.6 9.4 %collective-permute-start.5 = (bf16[512,1024]{1,0:T(8,128)(2,1)}, bf16[512,1024]{1,0:T(8,128)(2,1)}, u32[]{:S(2)}, u32[]{:S(2)}) collective-permute-start(bf16[512,1024]{1,0:T(8,128)(2,1)} %collective-permute-done.4), channel_id=1, source_target_pairs={{0,2},{2,0},{1,3},{3,1},{4,6},{6,4},{5,7},{7,5},{8,10},{10,8},{9,1... | collective-permute-start | bytes 3145736 | tf_op jit(solution)/shard_map/ppermute | solution.py:248
  52.9 17.9 %copy-start.42 = (bf16[1024]{0:T(1024)(128)(2,1)S(1)}, bf16[1024]{0:T(1024)(128)(2,1)}, u32[]{:S(2)}) copy-start(bf16[1024]{0:T(1024)(128)(2,1)} %param.24) | copy-start | bytes 6148
  70.8 5.1 %collective-permute-start.3 = (bf16[512,1024]{1,0:T(8,128)(2,1)}, bf16[512,1024]{1,0:T(8,128)(2,1)}, u32[]{:S(2)}, u32[]{:S(2)}) collective-permute-start(bf16[512,1024]{1,0:T(8,128)(2,1)} %get-tuple-element.78), channel_id=1, source_target_pairs={{0,2},{2,0},{1,3},{3,1},{4,6},{6,4},{5,7},{7,5},{8,10},{10,8},{9,1... | collective-permute-start | bytes 3145736 | tf_op jit(solution)/shard_map/ppermute | solution.py:248
  109.1 14.5 %slice-start = ((s8[4718592]{0:T(1024)(128)(4,1)}), s8[4194304]{0:T(1024)(128)(4,1)S(1)}, s32[]{:S(2)}) async-start(s8[4718592]{0:T(1024)(128)(4,1)} %bitcast.101), calls=%async_computation | async-start | bytes 8388608
  116.0 86.6 %collective-permute-start.6 = (bf16[512,2304]{1,0:T(8,128)(2,1)}, bf16[512,2304]{1,0:T(8,128)(2,1)}, u32[]{:S(2)}, u32[]{:S(2)}) collective-permute-start(bf16[512,2304]{1,0:T(8,128)(2,1)} %convolution_convert_fusion.5), channel_id=1, source_target_pairs={{0,8},{8,0},{1,9},{9,1},{2,10},{10,2},{3,11},{11,3},{4,12},{12,4},... | collective-permute-start | bytes 7077896 | tf_op jit(solution)/shard_map/ppermute | solution.py:248
  121.5 81.1 %collective-permute-start.7 = (bf16[2304,512]{1,0:T(8,128)(2,1)}, bf16[2304,512]{1,0:T(8,128)(2,1)}, u32[]{:S(2)}, u32[]{:S(2)}) collective-permute-start(bf16[2304,512]{1,0:T(8,128)(2,1)} %convolution_convert_fusion.4), channel_id=1, source_target_pairs={{0,1},{1,0},{2,3},{3,2},{4,5},{5,4},{6,7},{7,6},{8,9},{9,8},{10,11... | collective-permute-start | bytes 7077896 | tf_op jit(solution)/shard_map/ppermute | solution.py:248
  127.5 75.1 %collective-permute-start.8 = (bf16[512,2304]{1,0:T(8,128)(2,1)}, bf16[512,2304]{1,0:T(8,128)(2,1)}, u32[]{:S(2)}, u32[]{:S(2)}) collective-permute-start(bf16[512,2304]{1,0:T(8,128)(2,1)} %convolution_convert_fusion.3), channel_id=1, source_target_pairs={{0,4},{4,0},{1,5},{5,1},{2,6},{6,2},{3,7},{7,3},{8,12},{12,8},{9,1... | collective-permute-start | bytes 7077896 | tf_op jit(solution)/shard_map/ppermute | solution.py:248
  146.4 19.2 %collective-permute-start.9 = (bf16[1024,1024]{1,0:T(8,128)(2,1)}, bf16[1024,1024]{1,0:T(8,128)(2,1)S(1)}, u32[]{:S(2)}, u32[]{:S(2)}) collective-permute-start(bf16[1024,1024]{1,0:T(8,128)(2,1)} %get-tuple-element.95), channel_id=1, source_target_pairs={{0,2},{2,0},{1,3},{3,1},{4,6},{6,4},{5,7},{7,5},{8,10},{10,8},{9,1... | collective-permute-start | bytes 6291464 | tf_op jit(solution)/shard_map/ppermute | solution.py:248
  173.7 28.8 %copy-start.29 = (bf16[512,512]{1,0:T(8,128)(2,1)}, bf16[512,512]{1,0:T(8,128)(2,1)S(1)}, u32[]{:S(2)}) copy-start(bf16[512,512]{1,0:T(8,128)(2,1)S(1)} %convolution_convert_fusion.9) | copy-start | bytes 1572868
  221.7 18.5 %collective-permute-start.12 = (bf16[512,1024]{1,0:T(8,128)(2,1)}, bf16[512,1024]{1,0:T(8,128)(2,1)}, u32[]{:S(2)}, u32[]{:S(2)}) collective-permute-start(bf16[512,1024]{1,0:T(8,128)(2,1)} %select_convert_fusion.2), channel_id=1, source_target_pairs={{0,2},{2,0},{1,3},{3,1},{4,6},{6,4},{5,7},{7,5},{8,10},{10,8},{9,1... | collective-permute-start | bytes 3145736 | tf_op jit(solution)/shard_map/ppermute | solution.py:248
  222.2 44.5 %collective-permute-start.21 = (bf16[2,1,128,2304]{3,2,1,0:T(8,128)(2,1)}, bf16[2,1,128,2304]{3,2,1,0:T(8,128)(2,1)}, u32[]{:S(2)}, u32[]{:S(2)}) collective-permute-start(bf16[2,1,128,2304]{3,2,1,0:T(8,128)(2,1)} %add_convert_fusion.2), channel_id=1, source_target_pairs={{0,8},{8,0},{1,9},{9,1},{2,10},{10,2},{3,11},{11,3},{4,12},{12,4},... | collective-permute-start | bytes 3538952 | tf_op jit(solution)/shard_map/ppermute | solution.py:248
  222.6 44.8 %collective-permute-start.22 = (bf16[2,1,576,512]{3,2,1,0:T(8,128)(2,1)}, bf16[2,1,576,512]{3,2,1,0:T(8,128)(2,1)}, u32[]{:S(2)}, u32[]{:S(2)}) collective-permute-start(bf16[2,1,576,512]{3,2,1,0:T(8,128)(2,1)} %add_convert_fusion.1), channel_id=1, source_target_pairs={{0,4},{4,0},{1,5},{5,1},{2,6},{6,2},{3,7},{7,3},{8,12},{12,8},{9,1... | collective-permute-start | bytes 3538952 | tf_op jit(solution)/shard_map/ppermute | solution.py:248
  223.1 44.3 %collective-permute-start.23 = (bf16[2,2,128,1152]{3,2,1,0:T(8,128)(2,1)}, bf16[2,2,128,1152]{3,2,1,0:T(8,128)(2,1)}, u32[]{:S(2)}, u32[]{:S(2)}) collective-permute-start(bf16[2,2,128,1152]{3,2,1,0:T(8,128)(2,1)} %select_convert_fusion), channel_id=1, source_target_pairs={{0,1},{1,0},{2,3},{3,2},{4,5},{5,4},{6,7},{7,6},{8,9},{9,8},{10,11... | collective-permute-start | bytes 3538952 | tf_op jit(solution)/shard_map/ppermute | solution.py:248
  237.2 23.1 %collective-permute-start.10 = (bf16[512,1024]{1,0:T(8,128)(2,1)}, bf16[512,1024]{1,0:T(8,128)(2,1)}, u32[]{:S(2)}, u32[]{:S(2)}) collective-permute-start(bf16[512,1024]{1,0:T(8,128)(2,1)} %select_convert_fusion.1), channel_id=1, source_target_pairs={{0,2},{2,0},{1,3},{3,1},{4,6},{6,4},{5,7},{7,5},{8,10},{10,8},{9,1... | collective-permute-start | bytes 3145736 | tf_op jit(solution)/shard_map/ppermute | solution.py:248
  243.6 5.9 %collective-permute-start.14 = (f32[17,128]{1,0:T(8,128)S(1)}, f32[17,128]{1,0:T(8,128)S(1)}, u32[]{:S(2)}, u32[]{:S(2)}) collective-permute-start(f32[17,128]{1,0:T(8,128)S(1)} %bitcast.120), channel_id=1, source_target_pairs={{0,16},{16,0},{1,17},{17,1},{2,18},{18,2},{3,19},{19,3},{4,20},{20... | collective-permute-start | bytes 26120 | tf_op jit(solution)/shard_map/ppermute | solution.py:248
  249.5 5.3 %collective-permute-start.15 = (f32[17,128]{1,0:T(8,128)S(1)}, f32[17,128]{1,0:T(8,128)S(1)}, u32[]{:S(2)}, u32[]{:S(2)}) collective-permute-start(f32[17,128]{1,0:T(8,128)S(1)} %bitcast_add_fusion), channel_id=1, source_target_pairs={{0,8},{8,0},{1,9},{9,1},{2,10},{10,2},{3,11},{11,3},{4,12},{12,4},... | collective-permute-start | bytes 26120 | tf_op jit(solution)/shard_map/ppermute | solution.py:248
  254.8 3.7 collective-permute-start.16
  258.5 1.2 collective-permute-start.17
  259.7 17.5 %collective-permute-start.19 = (bf16[512,512]{1,0:T(8,128)(2,1)S(1)}, bf16[512,512]{1,0:T(8,128)(2,1)S(1)}, u32[]{:S(2)}, u32[]{:S(2)}) collective-permute-start(bf16[512,512]{1,0:T(8,128)(2,1)S(1)} %copy-done.50), channel_id=1, source_target_pairs={{0,4},{4,0},{1,5},{5,1},{2,6},{6,2},{3,7},{7,3},{8,12},{12,8},{9,1... | collective-permute-start | bytes 1572872 | tf_op jit(solution)/shard_map/ppermute | solution.py:248
  260.2 4.4 %collective-permute-start.18 = (f32[17,128]{1,0:T(8,128)S(1)}, f32[17,128]{1,0:T(8,128)S(1)}, u32[]{:S(2)}, u32[]{:S(2)}) collective-permute-start(f32[17,128]{1,0:T(8,128)S(1)} %add.491), channel_id=1, source_target_pairs={{0,1},{1,0},{2,3},{3,2},{4,5},{5,4},{6,7},{7,6},{8,9},{9,8},{10,11... | collective-permute-start | bytes 26120 | tf_op jit(solution)/shard_map/ppermute | solution.py:248
  264.6 26.0 %collective-permute-start.20 = (bf16[1024,512]{1,0:T(8,128)(2,1)S(1)}, bf16[1024,512]{1,0:T(8,128)(2,1)S(1)}, u32[]{:S(2)}, u32[]{:S(2)}) collective-permute-start(bf16[1024,512]{1,0:T(8,128)(2,1)S(1)} %copy-done.45), channel_id=1, source_target_pairs={{0,1},{1,0},{2,3},{3,2},{4,5},{5,4},{6,7},{7,6},{8,9},{9,8},{10,11... | collective-permute-start | bytes 3145736 | tf_op jit(solution)/shard_map/ppermute | solution.py:248
  266.7 64.2 %collective-permute-start.11 = (bf16[512,1024]{1,0:T(8,128)(2,1)S(1)}, bf16[512,1024]{1,0:T(8,128)(2,1)S(1)}, u32[]{:S(2)}, u32[]{:S(2)}) collective-permute-start(bf16[512,1024]{1,0:T(8,128)(2,1)S(1)} %get-tuple-element.142), channel_id=1, source_target_pairs={{0,0},{1,2},{2,1},{3,3},{4,4},{5,6},{6,5},{7,7},{8,8},{9,10},{10,9... | collective-permute-start | bytes 3145736 | tf_op jit(solution)/shard_map/ppermute | solution.py:252
  269.6 47.3 %collective-permute-start.26 = (bf16[2,1,128,1152]{3,2,1,0:T(8,128)(2,1)S(1)}, bf16[2,1,128,1152]{3,2,1,0:T(8,128)(2,1)S(1)}, u32[]{:S(2)}, u32[]{:S(2)}) collective-permute-start(bf16[2,1,128,1152]{3,2,1,0:T(8,128)(2,1)S(1)} %select_convert_fusion.3), channel_id=1, source_target_pairs={{0,1},{1,0},{2,3},{3,2},{4,5},{5,4},{6,7},{7,6},{8,9},{9,8},{10,11... | collective-permute-start | bytes 1769480 | tf_op jit(solution)/shard_map/ppermute | solution.py:248
  274.5 16.2 %copy-start.30 = (bf16[512,512]{1,0:T(8,128)(2,1)S(1)}, bf16[512,512]{1,0:T(8,128)(2,1)}, u32[]{:S(2)}) copy-start(bf16[512,512]{1,0:T(8,128)(2,1)} %copy-done.29) | copy-start | bytes 1572868
  274.5 42.9 %collective-permute-start.27 = (bf16[2,1,576,512]{3,2,1,0:T(8,128)(2,1)S(1)}, bf16[2,1,576,512]{3,2,1,0:T(8,128)(2,1)S(1)}, u32[]{:S(2)}, u32[]{:S(2)}) collective-permute-start(bf16[2,1,576,512]{3,2,1,0:T(8,128)(2,1)S(1)} %add_convert_fusion), channel_id=1, source_target_pairs={{8,0},{2,10},{9,1},{3,11},{12,4},{6,14},{13,5},{7,15},{24,16},{18,... | collective-permute-start | bytes 3538952 | tf_op jit(solution)/shard_map/ppermute | solution.py:767
  277.2 40.2 %collective-permute-start.28 = (bf16[2,1,128,1152]{3,2,1,0:T(8,128)(2,1)S(1)}, bf16[2,1,128,1152]{3,2,1,0:T(8,128)(2,1)S(1)}, u32[]{:S(2)}, u32[]{:S(2)}) collective-permute-start(bf16[2,1,128,1152]{3,2,1,0:T(8,128)(2,1)S(1)} %add_convert_fusion.4), channel_id=1, source_target_pairs={{0,4},{4,0},{1,5},{5,1},{2,6},{6,2},{3,7},{7,3},{8,12},{12,8},{9,1... | collective-permute-start | bytes 1769480 | tf_op jit(solution)/shard_map/ppermute | solution.py:248
  290.8 26.6 %copy-start.28 = (bf16[2,1,128,1152]{3,2,1,0:T(8,128)(2,1)S(1)}, bf16[2,1,128,1152]{3,2,1,0:T(8,128)(2,1)}, u32[]{:S(2)}) copy-start(bf16[2,1,128,1152]{3,2,1,0:T(8,128)(2,1)} %broadcast_select_fusion.8) | copy-start | bytes 1769476
  290.8 32.5 %collective-permute-start.24 = (bf16[2,2,1,128,256]{4,3,2,1,0:T(8,128)(2,1)S(1)}, bf16[2,2,1,128,256]{4,3,2,1,0:T(8,128)(2,1)S(1)}, u32[]{:S(2)}, u32[]{:S(2)}) collective-permute-start(bf16[2,2,1,128,256]{4,3,2,1,0:T(8,128)(2,1)S(1)} %select_convert_fusion.5), channel_id=1, source_target_pairs={{0,1},{1,0},{2,3},{3,2},{4,5},{5,4},{6,7},{7,6},{8,9},{9,8},{10,11... | collective-permute-start | bytes 786440 | tf_op jit(solution)/shard_map/ppermute | solution.py:248
  316.9 12.0 %collective-permute-start.25 = (bf16[2,2,1,128,512]{4,3,2,1,0:T(8,128)(2,1)S(1)}, bf16[2,2,1,128,512]{4,3,2,1,0:T(8,128)(2,1)S(1)}, u32[]{:S(2)}, u32[]{:S(2)}) collective-permute-start(bf16[2,2,1,128,512]{4,3,2,1,0:T(8,128)(2,1)S(1)} %add_convert_fusion.5), channel_id=1, source_target_pairs={{0,4},{4,0},{1,5},{5,1},{2,6},{6,2},{3,7},{7,3},{8,12},{12,8},{9,1... | collective-permute-start | bytes 1572872 | tf_op jit(solution)/shard_map/ppermute | solution.py:248
  317.6 37.9 %collective-permute-start.33 = (bf16[1,1,128,1152]{3,2,1,0:T(8,128)(2,1)S(1)}, bf16[1,1,128,1152]{3,2,1,0:T(8,128)(2,1)S(1)}, u32[]{:S(2)}, u32[]{:S(2)}) collective-permute-start(bf16[1,1,128,1152]{3,2,1,0:T(8,128)(2,1)S(1)} %add_convert_fusion.7), channel_id=1, source_target_pairs={{0,16},{16,0},{1,17},{17,1},{2,18},{18,2},{3,19},{19,3},{4,20},{20... | collective-permute-start | bytes 884744 | tf_op jit(solution)/shard_map/ppermute | solution.py:248
  320.2 55.7 %collective-permute-start.34 = (bf16[1,1,576,512]{3,2,1,0:T(8,128)(2,1)S(1)}, bf16[1,1,576,512]{3,2,1,0:T(8,128)(2,1)S(1)}, u32[]{:S(2)}, u32[]{:S(2)}) collective-permute-start(bf16[1,1,576,512]{3,2,1,0:T(8,128)(2,1)S(1)} %add_convert_fusion.3), channel_id=1, source_target_pairs={{0,16},{16,0},{1,17},{17,1},{2,18},{18,2},{3,19},{19,3},{4,20},{20... | collective-permute-start | bytes 1769480 | tf_op jit(solution)/shard_map/ppermute | solution.py:248
  323.3 52.6 %collective-permute-start.35 = (bf16[1,1,128,1152]{3,2,1,0:T(8,128)(2,1)S(1)}, bf16[1,1,128,1152]{3,2,1,0:T(8,128)(2,1)S(1)}, u32[]{:S(2)}, u32[]{:S(2)}) collective-permute-start(bf16[1,1,128,1152]{3,2,1,0:T(8,128)(2,1)S(1)} %add_convert_fusion.6), channel_id=1, source_target_pairs={{0,16},{16,0},{1,17},{17,1},{2,18},{18,2},{3,19},{19,3},{4,20},{20... | collective-permute-start | bytes 884744 | tf_op jit(solution)/shard_map/ppermute | solution.py:248
  328.9 19.0 %collective-permute-start.29 = (bf16[2,1,1,128,256]{4,3,2,1,0:T(8,128)(2,1)S(1)}, bf16[2,1,1,128,256]{4,3,2,1,0:T(8,128)(2,1)S(1)}, u32[]{:S(2)}, u32[]{:S(2)}) collective-permute-start(bf16[2,1,1,128,256]{4,3,2,1,0:T(8,128)(2,1)S(1)} %add_convert_fusion.10), channel_id=1, source_target_pairs={{0,8},{8,0},{1,9},{9,1},{2,10},{10,2},{3,11},{11,3},{4,12},{12,4},... | collective-permute-start | bytes 393224 | tf_op jit(solution)/shard_map/ppermute | solution.py:248
  330.9 20.7 %collective-permute-start.30 = (bf16[2,1,1,128,512]{4,3,2,1,0:T(8,128)(2,1)S(1)}, bf16[2,1,1,128,512]{4,3,2,1,0:T(8,128)(2,1)S(1)}, u32[]{:S(2)}, u32[]{:S(2)}) collective-permute-start(bf16[2,1,1,128,512]{4,3,2,1,0:T(8,128)(2,1)S(1)} %add_convert_fusion.8), channel_id=1, source_target_pairs={{0,8},{8,0},{1,9},{9,1},{2,10},{10,2},{3,11},{11,3},{4,12},{12,4},... | collective-permute-start | bytes 786440 | tf_op jit(solution)/shard_map/ppermute | solution.py:248
  347.9 36.8 %collective-permute-start.13 = (bf16[512,1024]{1,0:T(8,128)(2,1)S(1)}, bf16[512,1024]{1,0:T(8,128)(2,1)S(1)}, u32[]{:S(2)}, u32[]{:S(2)}) collective-permute-start(bf16[512,1024]{1,0:T(8,128)(2,1)S(1)} %get-tuple-element.137), channel_id=1, source_target_pairs={{0,0},{1,2},{2,1},{3,3},{4,4},{5,6},{6,5},{7,7},{8,8},{9,10},{10,9... | collective-permute-start | bytes 3145736 | tf_op jit(solution)/shard_map/ppermute | solution.py:252
  351.7 32.8 %collective-permute-start.31 = (bf16[1,1,1,128,256]{4,3,2,1,0:T(8,128)(2,1)S(1)}, bf16[1,1,1,128,256]{4,3,2,1,0:T(8,128)(2,1)S(1)}, u32[]{:S(2)}, u32[]{:S(2)}) collective-permute-start(bf16[1,1,1,128,256]{4,3,2,1,0:T(8,128)(2,1)S(1)} %add_convert_fusion.11), channel_id=1, source_target_pairs={{0,16},{16,0},{1,17},{17,1},{2,18},{18,2},{3,19},{19,3},{4,20},{20... | collective-permute-start | bytes 196616 | tf_op jit(solution)/shard_map/ppermute | solution.py:248
  355.5 28.9 %collective-permute-start.32 = (bf16[1,1,1,128,512]{4,3,2,1,0:T(8,128)(2,1)S(1)}, bf16[1,1,1,128,512]{4,3,2,1,0:T(8,128)(2,1)S(1)}, u32[]{:S(2)}, u32[]{:S(2)}) collective-permute-start(bf16[1,1,1,128,512]{4,3,2,1,0:T(8,128)(2,1)S(1)} %add_convert_fusion.9), channel_id=1, source_target_pairs={{0,16},{16,0},{1,17},{17,1},{2,18},{18,2},{3,19},{19,3},{4,20},{20... | collective-permute-start | bytes 393224 | tf_op jit(solution)/shard_map/ppermute | solution.py:248
  376.2 3.5 collective-permute-start.36
  377.5 5.1 %collective-permute-start.37 = (bf16[64,1152]{1,0:T(8,128)(2,1)S(1)}, bf16[64,1152]{1,0:T(8,128)(2,1)S(1)}, u32[]{:S(2)}, u32[]{:S(2)}) collective-permute-start(bf16[64,1152]{1,0:T(8,128)(2,1)S(1)} %fusion.8), channel_id=1, source_target_pairs={{0,2},{2,0},{1,3},{3,1},{4,6},{6,4},{5,7},{7,5},{8,10},{10,8},{9,1... | collective-permute-start | bytes 442376 | tf_op jit(solution)/shard_map/ppermute | solution.py:248
  379.7 3.8 collective-permute-start.38
  384.7 1.7 collective-permute-start.39
  (47 other events, 216.7 us)

commit v3 on v2

--- a/solution.py
+++ b/solution.py
@@ -1,4 +1,6 @@
 import math
+
+import functools
 
 import jax
 import jax.numpy as jnp
@@ -294,97 +296,107 @@
     return d_values, turned * unit
 
 
-def block_mask(first_key, keys, begin, block, starts, diagonal):
-    key_at = first_key + lax.broadcasted_iota(jnp.int32, (keys, block), 0)
-    allowed = key_at >= starts
-    if diagonal:
-        query_at = begin + lax.broadcasted_iota(jnp.int32, (keys, block), 1)
-        allowed = allowed & (key_at <= query_at)
-    return allowed
+BLOCKED = 256.0
+
+
+def split_low(v):
+    high = v.astype(BF16)
+    rest = v - high.astype(F32)
+    middle = rest.astype(BF16)
+    return [high, middle, (rest - middle.astype(F32)).astype(BF16)]
+
+
+def documents(segment, rows, length):
+    return (segment == lax.broadcasted_iota(jnp.int32, (rows, length), 0)).astype(F32)
+
+
+def key_parts(begin, window):
+    low = max(0, begin - (window - 1)) // QBLOCK * QBLOCK
+    return ([(low, begin, False)] if begin > low else []) + [(begin, begin + QBLOCK, True)]
+
+
+def causal(block):
+    key_at = lax.broadcasted_iota(jnp.int32, (block, block), 0)
+    return key_at <= lax.broadcasted_iota(jnp.int32, (block, block), 1)
 
 
 def attention_kernel(
-    starts_ref, gain_q_ref, gain_k_ref, cos_ref, sin_ref, q_ref, k_ref, v_ref,
-    out_ref, log_ref, qs_ref, ks_ref, vs_ref,
+    segment_ref, gain_q_ref, gain_k_ref, cos_ref, sin_ref, q_ref, k_ref, v_ref,
+    out_ref, exact_ref, log_ref, qs_ref, ks_ref, vs_ref, *, docs, window,
 ):
-    size = k_ref.shape[0]
-    length = k_ref.shape[1]
+    size, length = k_ref.shape
     group = q_ref.shape[0] // size
     cosine, sine = cos_ref[...], sin_ref[...]
+    same = documents(segment_ref[...], docs, length)
     k_rot = rope_rows(k_ref[...], gain_k_ref[...], cosine, sine)
     ks_ref[...] = k_rot.astype(BF16)
-    keys = k_rot.T.astype(BF16)
+    keys = jnp.concatenate([k_rot, (same - 1.0) * BLOCKED], axis=0).T.astype(BF16)
     values = v_ref[...].astype(BF16)
     vs_ref[...] = values
+    ones = (lax.broadcasted_iota(jnp.int32, (16, length), 0) == 0).astype(BF16)
+    values = jnp.concatenate([values, ones], axis=0)
+    allowed = causal(QBLOCK)
     for h in range(group):
         rows = pl.ds(h * size, size)
         q_rot = rope_rows(q_ref[rows, :], gain_q_ref[...], cosine, sine).astype(BF16)
         q_rot = q_rot * jnp.asarray(size ** (-0.5), BF16)
         qs_ref[rows, :] = q_rot
+        query = jnp.concatenate([q_rot, same.astype(BF16)], axis=0)
         for begin in range(0, length, QBLOCK):
             stop = begin + QBLOCK
-            q_block = q_rot[:, begin:stop]
-            starts = starts_ref[:, begin:stop]
-            parts = [(begin, stop, True)] + ([(0, begin, False)] if begin else [])
-            scores = []
-            top = None
-            for low, high, diagonal in parts:
-                s = dot(keys[low:high], q_block, 1, 0)
-                s = jnp.where(block_mask(low, high - low, begin, QBLOCK, starts, diagonal), s, -jnp.inf)
-                here = jnp.max(s, axis=0, keepdims=True)
-                top = here if top is None else jnp.maximum(top, here)
-                scores.append(s)
-            expos = [jnp.exp(s - top) for s in scores]
-            total = sum(jnp.sum(e, axis=0, keepdims=True) for e in expos)
-            inverse = 1.0 / total
             result = 0.0
-            for (low, high, _), e in zip(parts, expos):
-                result = result + dot(values[:, low:high], (e * inverse).astype(BF16), 1, 0)
+            for low, high, diagonal in key_parts(begin, window):
+                e = jnp.exp(dot(keys[low:high], query[:, begin:stop], 1, 0))
+                if diagonal:
+                    e = jnp.where(allowed, e, 0.0)
+                result = result + dot(values[:, low:high], e.astype(BF16), 1, 0)
+            total = result[size : size + 1]
+            result = result[:size] / total
+            exact_ref[rows, begin:stop] = result
             out_ref[rows, begin:stop] = result.astype(BF16)
-            log_ref[0, 0, h : h + 1, begin:stop] = top + jnp.log(total)
-
-
-def attention(qkv, starts, gain_q, gain_k, cosine, sine, size, group, pairs):
+            log_ref[0, 0, h : h + 1, begin:stop] = jnp.log(total)
+
+
+def attention(qkv, segment, gain_q, gain_k, cosine, sine, size, group, pairs, docs):
     rows, length = qkv.shape
     per = (group + 2) * size * pairs
     halves = rows // per
     unit = group * size
     q_rows, k_rows = per // unit, per // size
     full = lambda a: pl.BlockSpec(a.shape, lambda i, j: (0,) * a.ndim)
+    wide = pl.BlockSpec((unit, length), lambda i, j: (pairs * i + j, 0))
+    thin = pl.BlockSpec((size, length), lambda i, j: (pairs * i + j, 0))
     heads = halves * pairs * group
     return pl.pallas_call(
-        attention_kernel,
+        functools.partial(attention_kernel, docs=docs, window=length // 2),
         grid=(halves, pairs),
-        in_specs=[full(a) for a in (starts, gain_q, gain_k, cosine, sine)]
+        in_specs=[full(a) for a in (segment, gain_q, gain_k, cosine, sine)]
         + [
             pl.BlockSpec((unit, length), lambda i, j: (q_rows * i + j, 0)),
             pl.BlockSpec((size, length), lambda i, j: (k_rows * i + pairs * group + j, 0)),
             pl.BlockSpec((size, length), lambda i, j: (k_rows * i + pairs * (group + 1) + j, 0)),
         ],
         out_specs=[
-            pl.BlockSpec((unit, length), lambda i, j: (pairs * i + j, 0)),
-            pl.BlockSpec((1, 1, group, length), lambda i, j: (i, j, 0, 0)),
-            pl.BlockSpec((unit, length), lambda i, j: (pairs * i + j, 0)),
-            pl.BlockSpec((size, length), lambda i, j: (pairs * i + j, 0)),
-            pl.BlockSpec((size, length), lambda i, j: (pairs * i + j, 0)),
+            wide, wide, pl.BlockSpec((1, 1, group, length), lambda i, j: (i, j, 0, 0)), wide, thin, thin,
         ],
         out_shape=[
             jax.ShapeDtypeStruct((heads * size, length), BF16),
+            jax.ShapeDtypeStruct((heads * size, length), F32),
             jax.ShapeDtypeStruct((halves, pairs, group, length), F32),
             jax.ShapeDtypeStruct((heads * size, length), BF16),
             jax.ShapeDtypeStruct((halves * pairs * size, length), BF16),
             jax.ShapeDtypeStruct((halves * pairs * size, length), BF16),
         ],
+        cost_estimate=cost(40 * heads * size * length * length // 2, qkv, qkv),
         name="attention_forward",
-    )(starts, gain_q, gain_k, cosine, sine, qkv, qkv, qkv)
+    )(segment, gain_q, gain_k, cosine, sine, qkv, qkv, qkv)
 
 
 def attention_back_kernel(
-    starts_ref, gain_q_ref, gain_k_ref, cos_ref, sin_ref, q_ref, k_ref, qs_ref, ks_ref, vs_ref, log_ref, do_ref,
-    out_ref, gq_ref, gk_ref, dk_ref, dv_ref,
+    segment_ref, gain_q_ref, gain_k_ref, cos_ref, sin_ref, q_ref, k_ref, qs_ref, ks_ref, vs_ref, exact_ref, log_ref,
+    do_ref, out_ref, gq_ref, gk_ref, dk_ref, dv_ref, *, docs, window,
 ):
-    size = k_ref.shape[0]
-    length = k_ref.shape[1]
+    size, length = k_ref.shape
     group = q_ref.shape[0] // size
     pair, pairs = pl.program_id(1), pl.num_programs(1)
     cosine, sine = cos_ref[...], sin_ref[...]
@@ -398,42 +410,44 @@
         width = gq_ref.shape[1]
         return sum(terms[:, i : i + width] for i in range(0, length, width))
 
+    same = documents(segment_ref[...], docs, length)
+    threes = (lax.broadcasted_iota(jnp.int32, (8, length), 0) < 3).astype(F32)
     keys_t = ks_ref[...]
-    keys = keys_t.astype(F32).T.astype(BF16)
-    values = vs_ref[...].astype(F32).T.astype(BF16)
+    keys = jnp.concatenate([keys_t.astype(F32), (same - 1.0) * BLOCKED, threes], axis=0).T.astype(BF16)
+    values = jnp.concatenate([vs_ref[...].astype(F32), threes], axis=0).T.astype(BF16)
+    allowed = causal(QBLOCK)
     dk_ref[...] = jnp.zeros_like(dk_ref)
     dv_ref[...] = jnp.zeros_like(dv_ref)
     scale = size ** (-0.5)
     for h in range(group):
         rows = pl.ds(h * size, size)
         q_t, do_t = qs_ref[rows, :], do_ref[rows, :]
+        do_wide = do_t.astype(F32)
         q_nat = q_t.astype(F32).T.astype(BF16)
-        do_nat = do_t.astype(F32).T.astype(BF16)
+        do_nat = do_wide.T.astype(BF16)
+        delta = jnp.sum(do_wide * exact_ref[rows, :], axis=0, keepdims=True)
+        logs = [-v.astype(F32) for v in split_low(log_ref[0, 0, h : h + 1, :])]
+        deltas = [-v.astype(F32) for v in split_low(delta)]
+        zeros = jnp.zeros((5, length), F32)
+        query = jnp.concatenate(
+            [q_t, jnp.concatenate([same] + logs + [zeros], axis=0).astype(BF16)], axis=0
+        )
+        d_out = jnp.concatenate([do_wide] + deltas + [zeros], axis=0).astype(BF16)
         d_query = []
         for begin in range(0, length, QBLOCK):
             stop = begin + QBLOCK
-            starts = starts_ref[:, begin:stop]
-            logs = log_ref[0, 0, h : h + 1, begin:stop]
-            parts = [(begin, stop, True)] + ([(0, begin, False)] if begin else [])
-            probs, d_probs = [], []
-            delta = 0.0
-            for low, high, diagonal in parts:
-                s = dot(keys[low:high], q_t[:, begin:stop], 1, 0)
-                allowed = block_mask(low, high - low, begin, QBLOCK, starts, diagonal)
-                p = jnp.where(allowed, jnp.exp(s - logs), 0.0)
-                dp = dot(values[low:high], do_t[:, begin:stop], 1, 0)
-                delta = delta + jnp.sum(p * dp, axis=0, keepdims=True)
-                probs.append(p)
-                d_probs.append(dp)
             d_q = 0.0
-            for (low, high, _), p, dp in zip(parts, probs, d_probs):
-                ds = (p * (dp - delta)).astype(BF16)
+            for low, high, diagonal in key_parts(begin, window):
+                p = jnp.exp(dot(keys[low:high], query[:, begin:stop], 1, 0))
+                if diagonal:
+                    p = jnp.where(allowed, p, 0.0)
+                ds = (p * dot(values[low:high], d_out[:, begin:stop], 1, 0)).astype(BF16)
                 dv_ref[low:high, :] += dot(p.astype(BF16), do_nat[begin:stop], 1, 0)
                 dk_ref[low:high, :] += dot(ds, q_nat[begin:stop], 1, 0)
                 d_q = d_q + dot(keys_t[:, low:high], ds, 1, 0)
-            d_query.append((d_q * scale).astype(BF16))
+            d_query.append((d_q * scale).astype(BF16).astype(F32))
         d_q0, terms = rope_rows_back(
-            jnp.concatenate(d_query, axis=1).astype(F32), q_ref[rows, :], gain_q_ref[...], cosine, sine
+            jnp.concatenate(d_query, axis=1), q_ref[rows, :], gain_q_ref[...], cosine, sine
         )
         gq_ref[...] += fold(terms)
         out_ref[pl.ds((pair * group + h) * size, size), :] = d_q0.astype(BF16)
@@ -444,7 +458,7 @@
     out_ref[pl.ds((pairs * (group + 1) + pair) * size, size), :] = dv_ref[...].T.astype(BF16)
 
 
-def attention_back(qkv, qs, ks, vs, logs, d_out, starts, gain_q, gain_k, cosine, sine, size, group, pairs):
+def attention_back(qkv, qs, ks, vs, exact, logs, d_out, segment, gain_q, gain_k, cosine, sine, size, group, pairs, docs):
     rows, length = qkv.shape
     per = (group + 2) * size * pairs
     halves = rows // per
@@ -454,13 +468,13 @@
     wide = pl.BlockSpec((unit, length), lambda i, j: (pairs * i + j, 0))
     thin = pl.BlockSpec((size, length), lambda i, j: (pairs * i + j, 0))
     return pl.pallas_call(
-        attention_back_kernel,
+        functools.partial(attention_back_kernel, docs=docs, window=length // 2),
         grid=(halves, pairs),
-        in_specs=[full(a) for a in (starts, gain_q, gain_k, cosine, sine)]
+        in_specs=[full(a) for a in (segment, gain_q, gain_k, cosine, sine)]
         + [
             pl.BlockSpec((unit, length), lambda i, j: (q_rows * i + j, 0)),
             pl.BlockSpec((size, length), lambda i, j: (k_rows * i + pairs * group + j, 0)),
-            wide, thin, thin,
+            wide, thin, thin, wide,
             pl.BlockSpec((1, 1, group, length), lambda i, j: (i, j, 0, 0)),
             wide,
         ],
@@ -475,8 +489,9 @@
             jax.ShapeDtypeStruct((size, 128), F32),
         ],
         scratch_shapes=[pltpu.VMEM((length, size), F32), pltpu.VMEM((length, size), F32)],
+        cost_estimate=cost(80 * rows * length * length // 4, qkv, qkv),
         name="attention_backward",
-    )(starts, gain_q, gain_k, cosine, sine, qkv, qkv, qs, ks, vs, logs, d_out)
+    )(segment, gain_q, gain_k, cosine, sine, qkv, qkv, qs, ks, vs, exact, logs, d_out)
 
 
 LANES = 128
@@ -486,47 +501,101 @@
     return lax.div(i, blocks) * 2 * blocks + c * blocks + lax.rem(i, blocks)
 
 
-def ffn_kernel(
-    sel_ref, hn_ref, dm_ref, gate0_ref, gate1_ref, up0_ref, up1_ref, down0_ref, down1_ref,
-    act_ref, dg_ref, du_ref, hz0_ref, hz1_ref, hy0_ref, hy1_ref, dx0_ref, dx1_ref,
-):
+def front_kernel(sel_ref, own_ref, other_ref, gain_ref, query_ref, key_ref, value_ref, normed_ref, out_ref):
+    local = own_ref.shape[0]
+
     @pl.when(pl.program_id(0) == 0)
     def _():
-        x, y, zl = sel_ref[1], sel_ref[2], sel_ref[3]
-        width = hn_ref.shape[1] // 8
-        half = dm_ref.shape[1] // 2
+        for i, ref in enumerate((own_ref, other_ref)):
+            place = pl.multiple_of((sel_ref[0] if i == 0 else 1 - sel_ref[0]) * local, local)
+            v = ref[...].astype(F32)
+            v = v * lax.rsqrt(jnp.mean(v * v, axis=-1, keepdims=True) + EPSILON) * gain_ref[...]
+            normed_ref[pl.ds(place, local), :] = v.astype(BF16)
+
+    at = 0
+    for ref in (query_ref, key_ref, value_ref):
+        out_ref[at : at + ref.shape[1], :] = dot(ref[...], normed_ref[...], 0, 1)
+        at += ref.shape[1]
+
+
+def front(sel, own, other, gain, w_query, w_key, w_value):
+    local, d = own.shape
+    widths = [w.shape[1] // 4 for w in (w_query, w_key, w_value)]
+    part = pl.BlockSpec((local, d), lambda j, sel: (0, 0))
+    return pl.pallas_call(
+        front_kernel,
+        grid_spec=pltpu.PrefetchScalarGridSpec(
+            num_scalar_prefetch=1,
+            grid=(2,),
+            in_specs=[part, part, pl.BlockSpec((1, d), lambda j, sel: (0, 0))]
+            + [pl.BlockSpec((d, w), lambda j, sel: (0, 2 * j + sel[0])) for w in widths],
+            out_specs=[
+                pl.BlockSpec((2 * local, d), lambda j, sel: (0, 0)),
+                pl.BlockSpec((sum(widths), 2 * local), lambda j, sel: (j, 0)),
+            ],
+        ),
+        out_shape=[
+            jax.ShapeDtypeStruct((2 * local, d), BF16),
+            jax.ShapeDtypeStruct((2 * sum(widths), 2 * local), F32),
+        ],
+        cost_estimate=cost(4 * local * d * 2 * sum(widths), own, own, w_query, w_query, w_query),
+        name="norm_and_projections",
+    )(sel, own, other, gain, w_query, w_key, w_value)
+
+
+def ffn_kernel(
+    sel_ref, hn_ref, own_ref, other_ref, gate0_ref, gate1_ref, up0_ref, up1_ref, down0_ref, down1_ref,
+    act_ref, dg_ref, du_ref, gate_leave_ref, up_leave_ref, down_leave_ref, hy1_ref, hz1_ref, dx1_ref,
+    turned_ref, hz0_ref, hy0_ref, dm_ref, dx0_ref,
+):
+    tokens, d = hn_ref.shape
+
+    @pl.when(pl.program_id(0) == 0)
+    def _():
+        c, x, y, zl = [sel_ref[i] for i in range(4)]
+        local, half, rows = tokens // 2, d // 2, d // 8
+        for i, ref in enumerate((own_ref, other_ref)):
+            place = pl.multiple_of((c if i == 0 else 1 - c) * local, local)
+            dm_ref[pl.ds(place, local), :] = ref[...]
+        turned_ref[...] = hn_ref[...].T
         for order in range(2):
             for i in range(4):
                 high, low = divmod(i, 2)
-                to = slice(i * width, (i + 1) * width)
-                bit = zl if order else 1 - zl
-                block = 4 * high + 2 * bit + low
-                (hz0_ref, hz1_ref)[order][:, to] = hn_ref[:, pl.ds(pl.multiple_of(block * width, width), width)]
-                bit = y if order else 1 - y
-                block = 4 * high + 2 * low + bit
-                (hy0_ref, hy1_ref)[order][:, to] = hn_ref[:, pl.ds(pl.multiple_of(block * width, width), width)]
-            bit = x if order else 1 - x
-            (dx0_ref, dx1_ref)[order][...] = dm_ref[:, pl.ds(pl.multiple_of(bit * half, half), half)]
+                to = slice(i * rows, (i + 1) * rows)
+                block = 4 * high + 2 * (zl if order else 1 - zl) + low
+                (hz0_ref, hz1_ref)[order][to, :] = turned_ref[pl.ds(pl.multiple_of(block * rows, rows), rows), :]
+                block = 4 * high + 2 * low + (y if order else 1 - y)
+                (hy0_ref, hy1_ref)[order][to, :] = turned_ref[pl.ds(pl.multiple_of(block * rows, rows), rows), :]
+            place = pl.multiple_of((x if order else 1 - x) * half, half)
+            (dx0_ref, dx1_ref)[order][...] = dm_ref[:, pl.ds(place, half)]
 
     gate_w = jnp.concatenate([gate0_ref[...], gate1_ref[...]], axis=1)
     up_w = jnp.concatenate([up0_ref[...], up1_ref[...]], axis=1)
     down_w = jnp.concatenate([down0_ref[...], down1_ref[...]], axis=0)
-    gate = dot(hn_ref[...], gate_w, 1, 0)
-    up = dot(hn_ref[...], up_w, 1, 0)
-    d_act = dot(dm_ref[...], down_w, 1, 1)
-    sigmoid = 1.0 / (1.0 + jnp.exp(-gate))
-    silu = gate * sigmoid
-    act_ref[...] = (silu * up).astype(BF16)
-    du_ref[...] = (d_act * silu).astype(BF16)
-    dg_ref[...] = (d_act * up * (sigmoid + silu * (1.0 - sigmoid))).astype(BF16)
-
-
-def feed_forward(sel, hnormed, d_mlp, w_gate, w_up, w_down):
+    step = min(256, tokens)
+    for begin in range(0, tokens, step):
+        at = slice(begin, begin + step)
+        gate = dot(hn_ref[at, :], gate_w, 1, 0)
+        up = dot(hn_ref[at, :], up_w, 1, 0)
+        d_act = dot(dm_ref[at, :], down_w, 1, 1)
+        sigmoid = 1.0 / (1.0 + jnp.exp(-gate))
+        silu = gate * sigmoid
+        act_ref[at, :] = (silu * up).astype(BF16)
+        du_ref[at, :] = (d_act * silu).astype(BF16)
+        dg_ref[at, :] = (d_act * up * (sigmoid + silu * (1.0 - sigmoid))).astype(BF16)
+    act_turned = act_ref[...].T
+    up_leave_ref[...] = dot(hz0_ref[...], du_ref[...], 1, 0).astype(BF16)
+    gate_leave_ref[...] = dot(hy0_ref[...], dg_ref[...], 1, 0).astype(BF16)
+    down_leave_ref[...] = dot(act_turned, dx0_ref[...], 1, 0).astype(BF16)
+
+
+def feed_forward(sel, hnormed, d_own, d_other, w_gate, w_up, w_down):
     tokens, d = hnormed.shape
     units = w_gate.shape[1] // 2
     blocks = units // 2 // LANES
+    block = 2 * LANES
     whole = pl.BlockSpec((tokens, d), lambda j, sel: (0, 0))
-    half = pl.BlockSpec((tokens, d // 2), lambda j, sel: (0, 0))
+    part = pl.BlockSpec((tokens // 2, d), lambda j, sel: (0, 0))
     columns = [
         pl.BlockSpec((d, LANES), lambda j, sel, i=i: (0, local_block(2 * j + i, sel[0], blocks))) for i in range(2)
     ]
@@ -535,13 +604,25 @@
         ffn_kernel,
         grid_spec=pltpu.PrefetchScalarGridSpec(
             num_scalar_prefetch=1,
-            grid=(blocks,),
-            in_specs=[whole, whole] + columns + columns + rows,
-            out_specs=[pl.BlockSpec((tokens, 2 * LANES), lambda j, sel: (0, j))] * 3 + [half] * 6,
+            grid=(units // block,),
+            in_specs=[whole, part, part] + columns + columns + rows,
+            out_specs=[pl.BlockSpec((tokens, block), lambda j, sel: (0, j))] * 3
+            + [pl.BlockSpec((d // 2, block), lambda j, sel: (0, j))] * 2
+            + [pl.BlockSpec((block, d // 2), lambda j, sel: (j, 0))]
+            + [pl.BlockSpec((d // 2, tokens), lambda j, sel: (0, 0))] * 2
+            + [pl.BlockSpec((tokens, d // 2), lambda j, sel: (0, 0))],
+            scratch_shapes=[pltpu.VMEM((d, tokens), BF16)]
+            + [pltpu.VMEM((d // 2, tokens), BF16)] * 2
+            + [pltpu.VMEM((tokens, d), BF16), pltpu.VMEM((tokens, d // 2), BF16)],
         ),
-        out_shape=[jax.ShapeDtypeStruct((tokens, units), BF16)] * 3 + [jax.ShapeDtypeStruct((tokens, d // 2), BF16)] * 6,
+        out_shape=[jax.ShapeDtypeStruct((tokens, units), BF16)] * 3
+        + [jax.ShapeDtypeStruct((d // 2, units), BF16)] * 2
+        + [jax.ShapeDtypeStruct((units, d // 2), BF16)]
+        + [jax.ShapeDtypeStruct((d // 2, tokens), BF16)] * 2
+        + [jax.ShapeDtypeStruct((tokens, d // 2), BF16)],
+        cost_estimate=cost(12 * tokens * d * units, w_gate, w_gate, w_gate, w_gate),
         name="feed_forward",
-    )(sel, hnormed, d_mlp, w_gate, w_gate, w_up, w_up, w_down, w_down)
+    )(sel, hnormed, d_own, d_other, w_gate, w_gate, w_up, w_up, w_down, w_down)
 
 
 def ffn_back_kernel(sel_ref, dg_ref, du_ref, gate0_ref, gate1_ref, up0_ref, up1_ref, out_ref, low_ref):
@@ -567,12 +648,17 @@
             out_specs=[pl.BlockSpec((tokens, block), lambda j, sel: (0, j))] * 2,
         ),
         out_shape=[jax.ShapeDtypeStruct((tokens, d), t) for t in (F32, BF16)],
+        cost_estimate=cost(4 * tokens * d * units, d_gate, d_up, w_gate),
         name="feed_forward_back",
     )(sel, d_gate, d_up, w_gate, w_gate, w_up, w_up)
 
 
-def ffn_out_kernel(sel_ref, act_ref, down0_ref, down1_ref, out_ref):
-    out_ref[...] = dot(act_ref[...], jnp.concatenate([down0_ref[...], down1_ref[...]], axis=0), 1, 0)
+def ffn_out_kernel(sel_ref, act_ref, down0_ref, down1_ref, own_ref, low_ref):
+    local = own_ref.shape[0]
+    down_w = jnp.concatenate([down0_ref[...], down1_ref[...]], axis=0)
+    own_ref[...] = dot(act_ref[pl.ds(pl.multiple_of(sel_ref[0] * local, local), local), :], down_w, 1, 0)
+    other = act_ref[pl.ds(pl.multiple_of((1 - sel_ref[0]) * local, local), local), :]
+    low_ref[...] = dot(other, down_w, 1, 0).astype(BF16)
 
 
 def ffn_out(sel, act, w_down):
@@ -586,15 +672,20 @@
             num_scalar_prefetch=1,
             grid=(d // block,),
             in_specs=[pl.BlockSpec((tokens, units), lambda j, sel: (0, 0))] + weights,
-            out_specs=pl.BlockSpec((tokens, block), lambda j, sel: (0, j)),
+            out_specs=[pl.BlockSpec((tokens // 2, block), lambda j, sel: (0, j))] * 2,
         ),
-        out_shape=jax.ShapeDtypeStruct((tokens, d), F32),
+        out_shape=[jax.ShapeDtypeStruct((tokens // 2, d), t) for t in (F32, BF16)],
+        cost_estimate=cost(2 * tokens * d * units, act),
         name="feed_forward_out",
     )(sel, act, w_down, w_down)
 
 
 def tie(values, *others):
     return lax.optimization_barrier((tuple(values), others))[0]
+
+
+def cost(flops, *arrays):
+    return pl.CostEstimate(flops=flops, transcendentals=0, bytes_accessed=sum(a.size * a.dtype.itemsize for a in arrays))
 
 
 def add_up(terms):
@@ -634,10 +725,6 @@
 
 def own_rows(v, c, local):
     return pick(c, v[:local], v[local:])
-
-
-def other_rows(v, c, local):
-    return pick(c, v[local:], v[:local])
 
 
 def pair_body(
@@ -657,73 +744,68 @@
     gain_k = key_gain.astype(F32)[:, None]
 
     own_tokens = transpose_pair(tokens[0])
-    other_tokens = swap(own_tokens, "c")
-    (cot_low,) = tie([cotangent[0]], own_tokens)
-    own_cot = transpose_pair(cot_low)
-    d_mlp = in_order(c, own_cot, swap(own_cot, "c"), 0)
     lengths = jnp.where(c == x, doc_lengths[0], swap(doc_lengths[0], "c"))
     ends = jnp.cumsum(lengths)
     positions = jnp.arange(length, dtype=jnp.int32)
-    starts = jnp.max(jnp.where(ends[:, None] <= positions[None, :], ends[:, None], 0), axis=0, keepdims=True)
+    segment = jnp.sum((ends[:, None] <= positions[None, :]).astype(jnp.int32), axis=0, keepdims=True)
     half = size // 2
     spread = jnp.exp(jnp.arange(half, dtype=F32) * (-2.0 * math.log(1000000.0) / size))
     angles = spread[:, None] * positions.astype(F32)[None, :]
     cosine, sine = jnp.cos(angles), jnp.sin(angles)
-
     parts = [part_columns(w, c) for w in (w_query, w_key, w_value)]
     w_qkv = jnp.concatenate([p[i] for i in range(2) for p in parts], axis=1)
     out_w = part_rows(w_out, c)
     sel = jnp.stack([c, x, y, zl]).astype(jnp.int32)
-    w_qkv, out_w, cosine, sine, starts, sel, other_tokens = tie(
-        (w_qkv, out_w, cosine, sine, starts, sel, other_tokens)
-    )
-
-    inputs = in_order(c, own_tokens, other_tokens, 0).astype(F32)
-    normed = rms_scale(inputs, gain_attn).astype(BF16)
-    qkv = dot(w_qkv, normed, 0, 1)
-    attended_own, logs, qs, ks, vs = attention(qkv, starts, gain_q, gain_k, cosine, sine, size, group, pairs)
+    w_qkv, out_w, cosine, sine, sel, own_tokens = tie((w_qkv, out_w, cosine, sine, sel, own_tokens))
+    other_tokens = swap(own_tokens, "c")
+    cot_low, other_tokens = tie((cotangent[0], other_tokens))
+    own_cot = transpose_pair(cot_low)
+    normed, qkv = front(sel, own_tokens, other_tokens, gain_attn[None], w_query, w_key, w_value)
+    docs = doc_lengths.shape[1]
+    attended_own, exact, logs, qs, ks, vs = attention(
+        qkv, segment, gain_q, gain_k, cosine, sine, size, group, pairs, docs
+    )
+    attended_own, own_cot = tie((attended_own, own_cot))
     attended_other = swap(attended_own, "c")
+    other_cot = swap(own_cot, "c")
     width = attended_own.shape[0] // 2
     attended = jnp.concatenate(
         [in_order(c, attended_own[i : i + width], attended_other[i : i + width], 0) for i in (0, width)], axis=0
     )
+    inputs = in_order(c, own_tokens, other_tokens, 0).astype(F32)
     hidden = inputs + dot(attended, w_out, 0, 0)
     hnormed = rms_scale(hidden, gain_ffn).astype(BF16)
 
-    act, d_gate, d_up, hn_z0, hn_z1, hn_y0, hn_y1, dm_x0, dm_x1 = feed_forward(
-        sel, hnormed, d_mlp, w_gate, w_up, w_down
-    )
-    send_up = dot(hn_z0, d_up, 0, 0).astype(BF16)
-    send_down = dot(act, dm_x0, 0, 0).astype(BF16)
-    send_gate = dot(hn_y0, d_gate, 0, 0).astype(BF16)
+    act, d_gate, d_up, send_gate, send_up, send_down, hn_y, hn_z, dm_x = feed_forward(
+        sel, hnormed, own_cot, other_cot, w_gate, w_up, w_down
+    )
     come_up, come_down, come_gate = swap(send_up, "zl"), swap(send_down, "x"), swap(send_gate, "y")
-    d_gate, d_up, act = tie((d_gate, d_up, act), send_up, send_down, send_gate)
     d_hn, d_hn_low = ffn_back(sel, d_gate, d_up, w_gate, w_up)
     d_hn_other = swap(d_hn_low, "c")
-    hn_z1, hn_y1, dm_x1 = tie((hn_z1, hn_y1, dm_x1), d_hn)
-    keep_up = dot(hn_z1, d_up, 0, 0).astype(BF16)
-    keep_down = dot(act, dm_x1, 0, 0).astype(BF16)
-    keep_gate = dot(hn_y1, d_gate, 0, 0).astype(BF16)
-    (d_hn_other,) = tie((d_hn_other,), keep_up)
+    hn_y, hn_z, dm_x = tie((hn_y, hn_z, dm_x), d_hn)
+    keep_up = dot(hn_z, d_up, 1, 0).astype(BF16)
+    keep_gate = dot(hn_y, d_gate, 1, 0).astype(BF16)
+    keep_down = dot(act, dm_x, 0, 0).astype(BF16)
+    (d_hn_other,) = tie((d_hn_other,), keep_up, keep_gate, keep_down)
     d_hn = d_hn + d_hn_other.astype(F32)
     d_hidden_norm, ffn_gain_terms = norm_back(d_hn, hidden, gain_ffn)
-    d_hidden = d_mlp.astype(F32) + d_hidden_norm
+    d_hidden = in_order(c, own_cot, other_cot, 0).astype(F32) + d_hidden_norm
     d_attn = d_hidden.astype(BF16)
     d_attended = dot(out_w, d_attn, 1, 1).astype(BF16)
     units = d_gate.shape[1]
     rows = d // 8
-    d_attn_part = jnp.concatenate(part_columns(d_attn, c), axis=1)
-    attended_y = attended.reshape(4, 2, rows, length)
-    send_out = dot(lax.dynamic_index_in_dim(attended_y, 1 - y, 1, False).reshape(d // 2, length), d_attn_part, 1, 0)
-    keep_out = dot(lax.dynamic_index_in_dim(attended_y, y, 1, False).reshape(d // 2, length), d_attn_part, 1, 0)
-    send_out, keep_out = send_out.astype(BF16), keep_out.astype(BF16)
-    come_out = swap(send_out, "y")
-    (d_attended,) = tie((d_attended,), keep_up, keep_down, keep_gate, send_out, keep_out)
+    quarter = d // 4
+    send_out, keep_out = [
+        dot(attended, lax.dynamic_slice_in_dim(d_attn, (2 * i + c) * quarter, quarter, 1), 1, 0).astype(BF16)
+        for i in (1 - x, x)
+    ]
+    come_out = swap(send_out, "x")
+    (d_attended,) = tie((d_attended,), send_out, keep_out)
     d_qkv, gain_q_terms, gain_k_terms = attention_back(
-        qkv, qs, ks, vs, logs, d_attended, starts, gain_q, gain_k, cosine, sine, size, group, pairs
-    )
-
-    come_up, come_down, come_gate, d_qkv = tie((come_up, come_down, come_gate, d_qkv))
+        qkv, qs, ks, vs, exact, logs, d_attended, segment, gain_q, gain_k, cosine, sine, size, group, pairs, docs
+    )
+
+    come_up, come_down, come_gate, come_out, d_qkv = tie((come_up, come_down, come_gate, come_out, d_qkv))
     up = [v.reshape(2, 2, rows, units) for v in (keep_up, come_up)]
     down = [v.reshape(2, 2, units // 4, d // 2) for v in (keep_down, come_down)]
     gate = [v.reshape(2, 2, rows, units) for v in (keep_gate, come_gate)]
@@ -737,20 +819,15 @@
     send_qkv = dot(normed, lax.dynamic_slice_in_dim(d_qkv, (1 - x) * width, width, 0), 0, 1).astype(BF16)
     come_qkv = swap(send_qkv, "x")
     (d_qkv,) = tie((d_qkv,), send_qkv)
-    part = dot(d_qkv, w_qkv, 0, 1)
-    part_low = other_rows(part, c, local).astype(BF16)
+    part_low = dot(pick(c, d_qkv[:, local:], d_qkv[:, :local]), w_qkv, 0, 1).astype(BF16)
     part_other = swap(part_low, "c")
-    d_qkv, act = tie((d_qkv, act), part_low)
+    (d_qkv,) = tie((d_qkv,), part_low)
+    part = dot(pick(c, d_qkv[:, :local], d_qkv[:, local:]), w_qkv, 0, 1)
     keep_qkv = dot(normed, lax.dynamic_slice_in_dim(d_qkv, x * width, width, 0), 0, 1).astype(BF16)
-    part_out = ffn_out(sel, act, w_down)
-    out_low = other_rows(part_out, c, local).astype(BF16)
-    out_other = swap(out_low, "c")
-    d_normed = own_rows(part, c, local) + part_other.astype(F32)
-    d_input_norm, attn_gain_terms = norm_back(d_normed, own_rows(inputs, c, local), gain_attn)
+    (part_other,) = tie((part_other,), keep_qkv, part)
+    d_normed = part + part_other.astype(F32)
+    d_input_norm, attn_gain_terms = norm_back(d_normed, own_tokens.astype(F32), gain_attn)
     d_inputs = own_rows(d_hidden, c, local) + d_input_norm
-    output = own_rows(hidden, c, local) + own_rows(part_out, c, local) + out_other.astype(F32)
-    output_low, d_inputs_low = output.astype(BF16), d_inputs.astype(BF16)
-    output_other, d_inputs_other = transpose_pair(output_low), transpose_pair(d_inputs_low)
     gains = jnp.concatenate(
         [
             jnp.sum(attn_gain_terms, axis=0),
@@ -760,43 +837,52 @@
         ]
     ).reshape(-1, 128)
 
-    tied = gate[-1], down[-1], up[-1]
-    gate[-1], down[-1], up[-1] = tie(tied, output_low, d_inputs_low, gains, keep_qkv)
-    send_gate, send_down, send_up = leave(gate, 3, x), add_up(down).astype(BF16), leave(up, 1, y)
+    gate[-1], down[-1] = tie((gate[-1], down[-1]), d_inputs, gains)
+    send_gate, send_down = leave(gate, 3, x), add_up(down).astype(BF16)
     gate = stay(gate, 3, x) + [swap(send_gate, "x")]
     down = down + [lax.ppermute(send_down, ("zl", "c"), [(2, 0), (1, 3)])]
+    (act,) = tie((act,), send_gate, send_down)
+    reached = swap(gains, AXES[0])
+    part_out, out_low = ffn_out(sel, act, w_down)
+    out_other = swap(out_low, "c")
+    come_out, up[-1], come_qkv, reached = tie((come_out, up[-1], come_qkv, reached), part_out)
+    gains = gains + reached
+    reached = swap(gains, AXES[1])
+    send_up = leave(up, 1, y)
     up = stay(up, 1, y) + [swap(send_up, "y")]
-
-    come_out, come_qkv = tie((come_out, come_qkv), send_gate, send_down, send_up)
-    out = [v.reshape(2, 2, 1, rows, d // 2) for v in (keep_out, come_out)]
+    out = [v.reshape(2, 2, 2, rows, quarter) for v in (keep_out, come_out)]
     qkv_grad = [v.reshape(2, 2, 2, rows, width) for v in (keep_qkv, come_qkv)]
-    send_out, send_qkv = leave(out, 4, x), leave(qkv_grad, 2, y)
-    out = stay(out, 4, x) + [swap(send_out, "x")]
-    qkv_grad = stay(qkv_grad, 2, y) + [swap(send_qkv, "y")]
-
-    tied = gate[-1], down[-1], up[-1]
-    gate[-1], down[-1], up[-1] = tie(tied, send_out, send_qkv)
-    send_gate, send_down, send_up = leave(gate, 0, zh), leave(down, 0, zh), leave(up, 0, zh)
+    both = [out, qkv_grad]
+
+    def next_stage(both, axis, dim):
+        bit = lax.axis_index(axis)
+        send = jnp.concatenate([leave(t, dim, bit) for t in both], axis=-1)
+        come = swap(send, axis)
+        return [stay(t, dim, bit) + [v] for t, v in zip(both, (come[..., :quarter], come[..., quarter:]))]
+
+    both = next_stage(both, "y", 2)
+    out_other, reached = tie((out_other, reached), send_up)
+    gains = gains + reached
+    output = own_rows(hidden, c, local) + part_out + out_other.astype(F32)
+    results = jnp.concatenate([output.astype(BF16), d_inputs.astype(BF16)], axis=0)
+
+    gate[-1], down[-1], results, gains = tie((gate[-1], down[-1], results, gains))
+    reached = swap(gains, AXES[2])
+    send_gate, send_down = leave(gate, 0, zh), leave(down, 0, zh)
     gate = stay(gate, 0, zh) + [swap(send_gate, "zh")]
     down = stay(down, 0, zh) + [swap(send_down, "zh")]
+    up[-1], both[0][-1], both[1][-1], reached = tie((up[-1], both[0][-1], both[1][-1], reached), send_gate, send_down)
+    gains = gains + reached
+    reached = swap(gains, AXES[3])
+    send_up = leave(up, 0, zh)
     up = stay(up, 0, zh) + [swap(send_up, "zh")]
-
-    out[-1], qkv_grad[-1] = tie((out[-1], qkv_grad[-1]), send_gate, send_down, send_up)
-    send_out, send_qkv = leave(out, 1, zl), leave(qkv_grad, 1, zl)
-    out = stay(out, 1, zl) + [swap(send_out, "zl")]
-    qkv_grad = stay(qkv_grad, 1, zl) + [swap(send_qkv, "zl")]
-    for axis in AXES[:2]:
-        gains = gains + swap(gains, axis)
-    out[-1], qkv_grad[-1] = tie((out[-1], qkv_grad[-1]), gains)
-    send_out, send_qkv = leave(out, 0, zh), leave(qkv_grad, 0, zh)
-    out = stay(out, 0, zh) + [swap(send_out, "zh")]
-    qkv_grad = stay(qkv_grad, 0, zh) + [swap(send_qkv, "zh")]
-    for axis in AXES[2:]:
-        gains = gains + swap(gains, axis)
-    gains = gains.reshape(-1)
-
-    tied = gate[-1], down[-1], up[-1]
-    gate[-1], down[-1], up[-1] = tie(tied, send_out, send_qkv)
+    both = next_stage(both, "zl", 1)
+    results, reached = tie((results, reached), send_up)
+    results_other = transpose_pair(results)
+    gains = gains + reached
+    reached = swap(gains, AXES[4])
+    out, qkv_grad = next_stage(both, "zh", 0)
+
     total = add_up(down).reshape(-1, d // 2)
     n = total.shape[0] // 2
     own = pick(c, total[:n], total[n:])
@@ -804,21 +890,22 @@
     other = lax.ppermute(other, ("zl", "c"), [(0, 1), (3, 2)]).astype(F32)
     sum_down = jnp.where(zl == c, own, other)
     sum_gate, sum_up = [share_rows(add_up(t).reshape(rows, units // 2), c) for t in (gate, up)]
-    out[-1], qkv_grad[-1] = tie((out[-1], qkv_grad[-1]), sum_gate, sum_up, sum_down)
+    out[-1], qkv_grad[-1], reached = tie((out[-1], qkv_grad[-1], reached), sum_gate, sum_up, sum_down)
+    gains = (gains + reached).reshape(-1)
     both = jnp.concatenate([add_up(t).reshape(rows, -1) for t in (out, qkv_grad)], axis=1)
     n = rows // 2
     own = pick(c, both[:n], both[n:])
     other = swap(pick(c, both[n:], both[:n]).astype(BF16), "c").astype(F32)
     first, second = pick(c, own, other), pick(c, other, own)
-    out_width, q_width, kv_width = d // 4, pairs * group * size, pairs * size
-    ends_of = [0, out_width, out_width + q_width, out_width + q_width + kv_width, out_width + q_width + 2 * kv_width]
+    q_width, kv_width = pairs * group * size, pairs * size
+    ends_of = [0, quarter, quarter + q_width, quarter + q_width + kv_width, quarter + q_width + 2 * kv_width]
     sum_out, sum_query, sum_key, sum_value = [
         jnp.concatenate([first[:, low:high], second[:, low:high]], axis=1)
         for low, high in zip(ends_of[:-1], ends_of[1:])
     ]
     stays = c == x
-    output = jnp.where(stays, output, output_other.astype(F32))
-    d_inputs = jnp.where(stays, d_inputs, d_inputs_other.astype(F32))
+    output = jnp.where(stays, output, results_other[:local].astype(F32))
+    d_inputs = jnp.where(stays, d_inputs, results_other[local:].astype(F32))
     return (
         output[None],
         d_inputs[None],

time: 395 us -> 356 us (0.901)
  matrix products: 53.1 us -> 26.4 us
  starting transfers between devices: 61.5 us -> 45.8 us
  Pallas kernels: 95.6 us -> 111 us
  waiting for transfers between devices: 82.2 us -> 73.9 us
  local copies, waits for them, and re-layouts: 22.1 us -> 17.5 us
    dot_general x14 -> x11, matrix products: 53.1 us -> 26.4 us  [dot(): lax.dot_general(left, right, (((left_dim,), (right_dim,)), ((), ())), pre...]
    ppermute x34 -> x31, starting transfers between devices: 45.2 us -> 30.2 us  [swap(): return lax.ppermute(v, axis, [(0, 1), (1, 0)])]
    pallas_call x2 -> x3, Pallas kernels: 42.6 us -> 51 us  [the longest x1 30.6 us: attention_back(): pl.pallas_call(functools.partial(attention_back_kernel, docs=docs, window...]
    ppermute x34 -> x31, waiting for transfers between devices: 82.2 us -> 73.9 us  [swap(): return lax.ppermute(v, axis, [(0, 1), (1, 0)])]
    pallas_call x1, Pallas kernels: 25.3 us -> 32.4 us  [feed_forward(): pl.pallas_call(ffn_kernel, grid_spec=pltpu.PrefetchScalarGridSpec(num_sca...]
    convert_element_type x11 -> x12, other arithmetic: 10.4 us -> 15.7 us  [leave(): add_up([lax.dynamic_slice_in_dim(t, (1 - bit) * size, size, dim) for t in...]
    unnamed x115 -> x107, local copies, waits for them, and re-layouts: 16.3 us -> 11.9 us
    select_n x12 -> x11, other arithmetic: 12.8 us -> 14.2 us  [pick(): return jnp.where(bit == 0, low, high)]
  transfers between devices with their start and end apart: 40 -> 36, of which waited for: 9 -> 10; matrix products, arithmetic and copies ran while one was open for 25% -> 28% of each run, Pallas kernels for 13% -> 23%
where the time goes in v3:
time: 356 us; the launch traced here: 350 us
  Pallas kernels  111 us (31%)
  waiting for transfers between devices  73.9 us (21%)
  other arithmetic  73.3 us (21%)
  starting transfers between devices  45.8 us (13%)
  matrix products  26.4 us (7%)
  local copies, waits for them, and re-layouts  17.5 us (5%)
    ppermute x31, waiting for transfers between devices, swap(): return lax.ppermute(v, axis, [(0, 1), (1, 0)])  73.9 us
    pallas_call x1, Pallas kernels, feed_forward(): pl.pallas_call(ffn_kernel, grid_spec=pltpu.PrefetchScalarGridSpec(num_sca...  32.4 us
    pallas_call x1, Pallas kernels, attention_back(): pl.pallas_call(functools.partial(attention_back_kernel, docs=docs, window...  30.6 us
    ppermute x31, starting transfers between devices, swap(): return lax.ppermute(v, axis, [(0, 1), (1, 0)])  30.2 us
    dot_general x11, matrix products, dot(): lax.dot_general(left, right, (((left_dim,), (right_dim,)), ((), ())), pre...  26.4 us
    pallas_call x1, Pallas kernels, ffn_back(): pl.pallas_call(ffn_back_kernel, grid_spec=pltpu.PrefetchScalarGridSpec(nu...  17.4 us
    convert_element_type x12, other arithmetic, leave(): add_up([lax.dynamic_slice_in_dim(t, (1 - bit) * size, size, dim) for t in...  15.7 us
    select_n x11, other arithmetic, pick(): return jnp.where(bit == 0, low, high)  14.2 us
  transfers between devices with their start and end apart: 36, of which 10 were waited for; matrix products, arithmetic and copies ran while one was open for 28% of the time, Pallas kernels for 23%

profile of v3, /device:TPU:0, one launch (start us, length us, event | category | flops | bytes accessed | tf_op | source)
XLA Modules:
  0.0 349.8 jit_solution(7632138447190522631)
XLA Ops:
  0.7 2.0 collective-permute-start
  2.7 1.9 dynamic-slice_dynamic-update-slice_fusion.1
  5.2 1.7 dynamic-slice_dynamic-update-slice_fusion.5
  6.9 1.7 dynamic-slice_dynamic-update-slice_fusion.4
  8.6 1.9 dynamic-slice_dynamic-update-slice_fusion
  10.5 1.7 dynamic-slice_dynamic-update-slice_fusion.3
  12.2 1.7 dynamic-slice_dynamic-update-slice_fusion.2
  16.1 3.1 collective-permute-start.1
  22.2 9.4 %collective-permute-start.3 = (bf16[512,1024]{1,0:T(8,128)(2,1)}, bf16[512,1024]{1,0:T(8,128)(2,1)}, u32[]{:S(2)}, u32[]{:S(2)}) collective-permute-start(bf16[512,1024]{1,0:T(8,128)(2,1)} %bitcast.108), channel_id=1, source_target_pairs={{0,0},{1,2},{2,1},{3,3},{4,4},{5,6},{6,5},{7,7},{8,8},{9,10},{10,9... | collective-permute-start | bytes 3145736 | tf_op jit(solution)/shard_map/ppermute | solution.py:254
  31.7 9.1 %norm_and_projections.1 = (bf16[1024,1024]{1,0:T(8,128)(2,1)}, f32[1024,1024]{1,0:T(8,128)}) custom-call(s32[4]{0:T(128)} %pad_add_fusion.sel_ref, bf16[512,1024]{1,0:T(8,128)(2,1)} %copy-done.6, bf16[512,1024]{1,0:T(8,128)(2,1)} %collective-permute-done.1.other_ref, f32[1,1024]{1,0:T(1,128)} %bitcast.102, bf16[1024,1024]{1,0:T(8,128)(2,1)} %query_ref.1, ...), custom_call_target="tpu_custom_call" | custom-call | flops 2147483648 | bytes 8388608 | tf_op jit(solution)/shard_map/norm_and_projections/pallas_call | solution.py:525
  40.8 11.3 %attention_forward.1 = (bf16[512,1024]{1,0:T(8,128)(2,1)}, f32[512,1024]{1,0:T(8,128)}, f32[2,2,2,1024]{3,2,1,0:T(2,128)}, bf16[512,1024]{1,0:T(8,128)(2,1)}, bf...) custom-call(s32[1,1024]{1,0:T(1,128)} %bitcast.103, f32[64,1]{1,0:T(8,128)} %copy.31.gain_q_ref, ...), custom_call_target="tpu_custom_call" | custom-call | flops 10737418240 | bytes 8388608 | tf_op jit(solution)/shard_map/attention_forward/pallas_call | solution.py:370
  56.6 2.7 multiply_reduce_fusion.2
  59.3 2.1 multiply_convert_fusion.hn_ref
  62.0 32.4 %feed_forward.1 = (bf16[1024,2304]{1,0:T(8,128)(2,1)}, bf16[1024,2304]{1,0:T(8,128)(2,1)}, bf16[1024,2304]{1,0:T(8,128)(2,1)}, bf16[512,2304]{1,0:T(8,128)(2,1)}...) custom-call(s32[4]{0:T(128)} %pad_add_fusion.sel_ref, ...), custom_call_target="tpu_custom_call" | custom-call | flops 28991029248 | bytes 37748736 | tf_op jit(solution)/shard_map/feed_forward/pallas_call | solution.py:603
  94.4 1.6 collective-permute-start.6
  98.6 17.4 %feed_forward_back.1 = (f32[1024,1024]{1,0:T(8,128)}, bf16[1024,1024]{1,0:T(8,128)(2,1)}) custom-call(s32[4]{0:T(128)} %pad_add_fusion.sel_ref, bf16[1024,2304]{1,0:T(8,128)(2,1)} %get-tuple-element.97.dg_ref, bf16[1024,2304]{1,0:T(8,128)(2,1)} %get-tuple-element.98.du_ref, bf16[1024,4608]{1,0:T(8,128)(2,1)} %gate1_ref.3, bf16[1024,4608]{1,0:T(8,128)(2,1)} %gate1_ref.3, ...), custom_call_target="tpu_custom_call" | custom-call | flops 9663676416 | bytes 18874368 | tf_op jit(solution)/shard_map/feed_forward_back/pallas_call | solution.py:642
  116.0 5.3 %convolution_convert_fusion.2 = bf16[512,2304]{1,0:T(8,128)(2,1)S(1)} fusion(bf16[512,1024]{1,0:T(8,128)(2,1)} %get-tuple-element.100, bf16[1024,2304]{1,0:T(8,128)(2,1)} %get-tuple-element.97.dg_ref), kind=kOutput, calls=%fused_computation.2 | convolution fusion | flops 2417098752 | bytes 8126464 | tf_op jit(solution)/shard_map/dot_general | solution.py:266
  121.3 2.6 broadcast_select_fusion.3
  125.6 2.8 convolution_convert_fusion.1
  130.5 3.9 %convolution_convert_fusion = bf16[2304,512]{1,0:T(8,128)(2,1)} fusion(bf16[1024,2304]{1,0:T(8,128)(2,1)S(1)} %bitcast.86, bf16[1024,512]{1,0:T(8,128)(2,1)S(1)} %copy-done.47), kind=kOutput, calls=%fused_computation | convolution fusion | flops 2417098752 | bytes 8126464 | tf_op jit(solution)/shard_map/dot_general | solution.py:266
  135.9 3.7 %fusion.37 = (bf16[1024,1024]{1,0:T(8,128)(2,1)S(1)}, f32[1024,1024]{1,0:T(8,128)}) fusion(f32[1024]{0:T(1024)S(1)} %broadcast_multiply_fusion.1, f32[1024,1024]{1,0:T(8,128)S(1)} %copy-done.3, f32[1024]{0:T(1024)S(1)} %convert_element_type.390, f32[1024,1024]{1,0:T(8,128)S(1)} %copy-done.5, bf16[1024,1024]{1,0:T(8,128)(2,1)S(1)} %collective-permute-done.9, ...), kind=kLoop, calls=%fused_computation.144 | loop fusion | flops 13631488 | bytes 18886656 | tf_op jit(solution)/shard_map/convert_element_type | solution.py:793
  141.5 2.3 convolution_convert_fusion.6.do_ref
  145.3 30.6 %attention_backward.1 = (bf16[1024,1024]{1,0:T(8,128)(2,1)}, f32[64,128]{1,0:T(8,128)}, f32[64,128]{1,0:T(8,128)}) custom-call(s32[1,1024]{1,0:T(1,128)} %bitcast.104, f32[64,1]{1,0:T(8,128)} %copy.31.gain_q_ref, f32[64,1]{1,0:T(8,128)} %copy.32.gain_k_ref, f32[32,1024]{1,0:T(8,128)} %get-tuple-element.85.cos_ref, f32[32,1024]{1,0:T(8,128)} %get-tuple-element.86.sin_ref, ...), custom_call_target="tpu_custom_call" | custom-call | flops 21474836480 | bytes 8388608 | tf_op jit(solution)/shard_map/attention_backward/pallas_call | solution.py:470
  177.6 3.1 add_convert_fusion.2
  180.7 4.1 %select_convert_fusion = bf16[2,2,128,1152]{3,2,1,0:T(8,128)(2,1)} fusion(pred[]{:T(512)S(6)} %eq.10, bf16[2,2,128,2304]{3,2,1,0:T(8,128)(2,1)} %bitcast.22, bf16[2,2,128,2304]{3,2,1,0:T(8,128)(2,1)} %bitcast.77), kind=kLoop, calls=%fused_computation.16 | loop fusion | flops 4718592 | bytes 5898241 | tf_op jit(solution)/shard_map/convert_element_type | solution.py:701
  184.9 2.8 add_convert_fusion.1
  187.6 2.3 convolution_convert_fusion.5
  195.8 2.3 convolution_convert_fusion.3
  198.1 2.9 broadcast_select_fusion
  201.0 2.2 broadcast_select_fusion.7
  204.3 2.6 collective-permute-start.17
  206.9 5.1 %fusion.35 = (bf16[512,1024]{1,0:T(8,128)(2,1)}, f32[512,1024]{1,0:T(8,128)}) fusion(f32[512]{0:T(512)S(1)} %broadcast_multiply_fusion.2, bf16[512,1024]{1,0:T(8,128)(2,1)S(1)} %copy-done.7, f32[1024]{0:T(1024)S(1)} %copy-done.39, f32[512,1024]{1,0:T(8,128)S(1)} %fusion.12, bf16[512,1024]{1,0:T(8,128)(2,1)} %copy-done.18, f32[512]{0:T(512)S(1)} %add_rsqrt_fusion.1, ...), kind=kLoop, calls=%fused_computation.143 | loop fusion | flops 5767168 | bytes 11542529 | tf_op jit(solution)/shard_map/convert_element_type | solution.py:867
  212.0 8.3 %collective-permute-done.11 = bf16[2,1,128,2304]{3,2,1,0:T(8,128)(2,1)} collective-permute-done((bf16[2,1,128,2304]{3,2,1,0:T(8,128)(2,1)}, bf16[2,1,128,2304]{3,2,1,0:T(8,128)(2,1)}, u32[]{:S(2)}, u32[]{:S(2)}) %collective-permute-start.11) | collective-permute-done | bytes 1179680 | tf_op jit(solution)/shard_map/ppermute | solution.py:250
  220.3 2.9 select_convert_fusion.1
  224.2 3.2 add_convert_fusion
  228.8 10.3 %feed_forward_out.1 = (f32[512,1024]{1,0:T(8,128)}, bf16[512,1024]{1,0:T(8,128)(2,1)}) custom-call(s32[4]{0:T(128)} %pad_add_fusion.sel_ref, bf16[1024,2304]{1,0:T(8,128)(2,1)} %get-tuple-element.130.act_ref, bf16[4608,1024]{1,0:T(8,128)(2,1)} %down1_ref.3, bf16[4608,1024]{1,0:T(8,128)(2,1)} %down1_ref.3), custom_call_target="tpu_custom_call" | custom-call | flops 4831838208 | bytes 4718592 | tf_op jit(solution)/shard_map/feed_forward_out/pallas_call | solution.py:669
  239.1 5.0 %collective-permute-done.16 = bf16[1024,512]{1,0:T(8,128)(2,1)} collective-permute-done((bf16[1024,512]{1,0:T(8,128)(2,1)}, bf16[1024,512]{1,0:T(8,128)(2,1)}, u32[]{:S(2)}, u32[]{:S(2)}) %collective-permute-start.16) | collective-permute-done | bytes 1048608 | tf_op jit(solution)/shard_map/ppermute | solution.py:250
  249.9 1.6 collective-permute-start.18
  252.8 14.0 %collective-permute-done.22 = bf16[2,2,1,128,768]{4,3,2,1,0:T(8,128)(2,1)S(1)} collective-permute-done((bf16[2,2,1,128,768]{4,3,2,1,0:T(8,128)(2,1)S(1)}, bf16[2,2,1,128,768]{4,3,2,1,0:T(8,128)(2,1)S(1)}, u32[]{:S(2)}, u32[]{:S(2)}) %collective-permute-start.22) | collective-permute-done | bytes 786464 | tf_op jit(solution)/shard_map/ppermute | solution.py:250
  272.1 2.6 collective-permute-start.29
  276.9 5.1 %collective-permute-done.21 = bf16[2,1,128,1152]{3,2,1,0:T(8,128)(2,1)S(1)} collective-permute-done((bf16[2,1,128,1152]{3,2,1,0:T(8,128)(2,1)S(1)}, bf16[2,1,128,1152]{3,2,1,0:T(8,128)(2,1)S(1)}, u32[]{:S(2)}, u32[]{:S(2)}) %collective-permute-start.21) | collective-permute-done | bytes 589856 | tf_op jit(solution)/shard_map/ppermute | solution.py:250
  284.4 1.6 collective-permute-start.26
  286.0 2.6 collective-permute-start.31
  289.4 12.2 %collective-permute-done.29 = bf16[1,1,128,1152]{3,2,1,0:T(8,128)(2,1)S(1)} collective-permute-done((bf16[1,1,128,1152]{3,2,1,0:T(8,128)(2,1)S(1)}, bf16[1,1,128,1152]{3,2,1,0:T(8,128)(2,1)S(1)}, u32[]{:S(2)}, u32[]{:S(2)}) %collective-permute-start.29) | collective-permute-done | bytes 294944 | tf_op jit(solution)/shard_map/ppermute | solution.py:250
  303.8 21.9 %collective-permute-done.31 = bf16[1,1,128,1152]{3,2,1,0:T(8,128)(2,1)S(1)} collective-permute-done((bf16[1,1,128,1152]{3,2,1,0:T(8,128)(2,1)S(1)}, bf16[1,1,128,1152]{3,2,1,0:T(8,128)(2,1)S(1)}, u32[]{:S(2)}, u32[]{:S(2)}) %collective-permute-start.31) | collective-permute-done | bytes 294944 | tf_op jit(solution)/shard_map/ppermute | solution.py:250
  331.3 1.9 collective-permute-start.34
  334.1 6.4 %collective-permute-done.27 = bf16[1,1,1,128,768]{4,3,2,1,0:T(8,128)(2,1)S(1)} collective-permute-done((bf16[1,1,1,128,768]{4,3,2,1,0:T(8,128)(2,1)S(1)}, bf16[1,1,1,128,768]{4,3,2,1,0:T(8,128)(2,1)S(1)}, u32[]{:S(2)}, u32[]{:S(2)}) %collective-permute-start.27) | collective-permute-done | bytes 196640 | tf_op jit(solution)/shard_map/ppermute | solution.py:250
  346.9 2.7 select_bitcast_fusion
  (241 shorter events, 65.4 us)
Async XLA Ops:
  0.6 13.2 %copy-start = (bf16[1024,1024]{1,0:T(8,128)(2,1)S(1)}, bf16[1024,1024]{1,0:T(8,128)(2,1)}, u32[]{:S(2)}) copy-start(bf16[1024,1024]{1,0:T(8,128)(2,1)} %param.23) | copy-start | bytes 6291460
  0.7 15.5 %collective-permute-start = (bf16[512,1024]{1,0:T(8,128)(2,1)}, bf16[512,1024]{1,0:T(8,128)(2,1)S(1)}, u32[]{:S(2)}, u32[]{:S(2)}) collective-permute-start(bf16[512,1024]{1,0:T(8,128)(2,1)} %bitcast.107), channel_id=1, source_target_pairs={{0,0},{1,2},{2,1},{3,3},{4,4},{5,6},{6,5},{7,7},{8,8},{9,10},{10,9... | collective-permute-start | bytes 3145736 | tf_op jit(solution)/shard_map/ppermute | solution.py:254
  8.6 11.5 %copy-start.44 = (bf16[64]{0:T(256)(128)(2,1)S(1)}, bf16[64]{0:T(256)(128)(2,1)}, u32[]{:S(2)}) copy-start(bf16[64]{0:T(256)(128)(2,1)} %param.22) | copy-start | bytes 388
  8.6 12.2 %copy-start.40 = (bf16[1024]{0:T(1024)(128)(2,1)S(1)}, bf16[1024]{0:T(1024)(128)(2,1)}, u32[]{:S(2)}) copy-start(bf16[1024]{0:T(1024)(128)(2,1)} %param.17) | copy-start | bytes 6148
  16.1 15.5 %copy-start.6 = (bf16[512,1024]{1,0:T(8,128)(2,1)}, bf16[512,1024]{1,0:T(8,128)(2,1)S(1)}, u32[]{:S(2)}) copy-start(bf16[512,1024]{1,0:T(8,128)(2,1)S(1)} %collective-permute-done.own_ref) | copy-start | bytes 3145732
  16.1 6.1 %collective-permute-start.1 = (bf16[512,1024]{1,0:T(8,128)(2,1)S(1)}, bf16[512,1024]{1,0:T(8,128)(2,1)}, u32[]{:S(2)}, u32[]{:S(2)}) collective-permute-start(bf16[512,1024]{1,0:T(8,128)(2,1)S(1)} %collective-permute-done.own_ref), channel_id=1, source_target_pairs={{0,2},{2,0},{1,3},{3,1},{4,6},{6,4},{5,7},{7,5},{8,10},{10,8},{9,1... | collective-permute-start | bytes 3145736 | tf_op jit(solution)/shard_map/ppermute | solution.py:250
  19.2 2.1 collective-permute-start.2
  22.2 29.9 %collective-permute-start.3 = (bf16[512,1024]{1,0:T(8,128)(2,1)}, bf16[512,1024]{1,0:T(8,128)(2,1)}, u32[]{:S(2)}, u32[]{:S(2)}) collective-permute-start(bf16[512,1024]{1,0:T(8,128)(2,1)} %bitcast.108), channel_id=1, source_target_pairs={{0,0},{1,2},{2,1},{3,3},{4,4},{5,6},{6,5},{7,7},{8,8},{9,10},{10,9... | collective-permute-start | bytes 3145736 | tf_op jit(solution)/shard_map/ppermute | solution.py:254
  40.8 11.5 %copy-start.41 = (bf16[1024]{0:T(1024)(128)(2,1)S(1)}, bf16[1024]{0:T(1024)(128)(2,1)}, u32[]{:S(2)}) copy-start(bf16[1024]{0:T(1024)(128)(2,1)} %param.24) | copy-start | bytes 6148
  40.8 11.5 %copy-start.7 = (bf16[512,1024]{1,0:T(8,128)(2,1)S(1)}, bf16[512,1024]{1,0:T(8,128)(2,1)}, u32[]{:S(2)}) copy-start(bf16[512,1024]{1,0:T(8,128)(2,1)} %copy-done.6) | copy-start | bytes 3145732
  52.1 3.1 collective-permute-start.4
  54.1 8.0 %collective-permute-start.5 = (bf16[512,1024]{1,0:T(8,128)(2,1)}, bf16[512,1024]{1,0:T(8,128)(2,1)}, u32[]{:S(2)}, u32[]{:S(2)}) collective-permute-start(bf16[512,1024]{1,0:T(8,128)(2,1)} %collective-permute-done.3.own_ref), channel_id=1, source_target_pairs={{0,2},{2,0},{1,3},{3,1},{4,6},{6,4},{5,7},{7,5},{8,10},{10,8},{9,1... | collective-permute-start | bytes 3145736 | tf_op jit(solution)/shard_map/ppermute | solution.py:250
  94.4 83.1 %collective-permute-start.6 = (bf16[512,2304]{1,0:T(8,128)(2,1)}, bf16[512,2304]{1,0:T(8,128)(2,1)}, u32[]{:S(2)}, u32[]{:S(2)}) collective-permute-start(bf16[512,2304]{1,0:T(8,128)(2,1)} %get-tuple-element.101), channel_id=1, source_target_pairs={{0,8},{8,0},{1,9},{9,1},{2,10},{10,2},{3,11},{11,3},{4,12},{12,4},... | collective-permute-start | bytes 7077896 | tf_op jit(solution)/shard_map/ppermute | solution.py:250
  96.1 81.5 %collective-permute-start.7 = (bf16[2304,512]{1,0:T(8,128)(2,1)}, bf16[2304,512]{1,0:T(8,128)(2,1)}, u32[]{:S(2)}, u32[]{:S(2)}) collective-permute-start(bf16[2304,512]{1,0:T(8,128)(2,1)} %get-tuple-element.102), channel_id=1, source_target_pairs={{0,1},{1,0},{2,3},{3,2},{4,5},{5,4},{6,7},{7,6},{8,9},{9,8},{10,11... | collective-permute-start | bytes 7077896 | tf_op jit(solution)/shard_map/ppermute | solution.py:250
  97.0 80.6 %collective-permute-start.8 = (bf16[512,2304]{1,0:T(8,128)(2,1)}, bf16[512,2304]{1,0:T(8,128)(2,1)}, u32[]{:S(2)}, u32[]{:S(2)}) collective-permute-start(bf16[512,2304]{1,0:T(8,128)(2,1)} %get-tuple-element.103), channel_id=1, source_target_pairs={{0,4},{4,0},{1,5},{5,1},{2,6},{6,2},{3,7},{7,3},{8,12},{12,8},{9,1... | collective-permute-start | bytes 7077896 | tf_op jit(solution)/shard_map/ppermute | solution.py:250
  116.0 18.4 %collective-permute-start.9 = (bf16[1024,1024]{1,0:T(8,128)(2,1)}, bf16[1024,1024]{1,0:T(8,128)(2,1)S(1)}, u32[]{:S(2)}, u32[]{:S(2)}) collective-permute-start(bf16[1024,1024]{1,0:T(8,128)(2,1)} %get-tuple-element.104), channel_id=1, source_target_pairs={{0,2},{2,0},{1,3},{3,1},{4,6},{6,4},{5,7},{7,5},{8,10},{10,8},{9,1... | collective-permute-start | bytes 6291464 | tf_op jit(solution)/shard_map/ppermute | solution.py:250
  140.4 37.3 %collective-permute-start.10 = (bf16[1024,256]{1,0:T(8,128)(2,1)S(1)}, bf16[1024,256]{1,0:T(8,128)(2,1)S(1)}, u32[]{:S(2)}, u32[]{:S(2)}) collective-permute-start(bf16[1024,256]{1,0:T(8,128)(2,1)S(1)} %convolution_convert_fusion.8), channel_id=1, source_target_pairs={{0,1},{1,0},{2,3},{3,2},{4,5},{5,4},{6,7},{7,6},{8,9},{9,8},{10,11... | collective-permute-start | bytes 1572872 | tf_op jit(solution)/shard_map/ppermute | solution.py:250
  191.2 12.0 %collective-permute-start.13 = (bf16[512,1024]{1,0:T(8,128)(2,1)S(1)}, bf16[512,1024]{1,0:T(8,128)(2,1)S(1)}, u32[]{:S(2)}, u32[]{:S(2)}) collective-permute-start(bf16[512,1024]{1,0:T(8,128)(2,1)S(1)} %convolution_convert_fusion.4), channel_id=1, source_target_pairs={{0,2},{2,0},{1,3},{3,1},{4,6},{6,4},{5,7},{7,5},{8,10},{10,8},{9,1... | collective-permute-start | bytes 3145736 | tf_op jit(solution)/shard_map/ppermute | solution.py:250
  191.5 28.8 %collective-permute-start.11 = (bf16[2,1,128,2304]{3,2,1,0:T(8,128)(2,1)}, bf16[2,1,128,2304]{3,2,1,0:T(8,128)(2,1)}, u32[]{:S(2)}, u32[]{:S(2)}) collective-permute-start(bf16[2,1,128,2304]{3,2,1,0:T(8,128)(2,1)} %add_convert_fusion.2), channel_id=1, source_target_pairs={{0,8},{8,0},{1,9},{9,1},{2,10},{10,2},{3,11},{11,3},{4,12},{12,4},... | collective-permute-start | bytes 3538952 | tf_op jit(solution)/shard_map/ppermute | solution.py:250
  192.0 28.3 %collective-permute-start.12 = (bf16[2,1,576,512]{3,2,1,0:T(8,128)(2,1)}, bf16[2,1,576,512]{3,2,1,0:T(8,128)(2,1)}, u32[]{:S(2)}, u32[]{:S(2)}) collective-permute-start(bf16[2,1,576,512]{3,2,1,0:T(8,128)(2,1)} %add_convert_fusion.1), channel_id=1, source_target_pairs={{0,4},{4,0},{1,5},{5,1},{2,6},{6,2},{3,7},{7,3},{8,12},{12,8},{9,1... | collective-permute-start | bytes 3538952 | tf_op jit(solution)/shard_map/ppermute | solution.py:250
  192.5 51.7 %collective-permute-start.15 = (bf16[2,2,128,1152]{3,2,1,0:T(8,128)(2,1)}, bf16[2,2,128,1152]{3,2,1,0:T(8,128)(2,1)}, u32[]{:S(2)}, u32[]{:S(2)}) collective-permute-start(bf16[2,2,128,1152]{3,2,1,0:T(8,128)(2,1)} %select_convert_fusion), channel_id=1, source_target_pairs={{0,1},{1,0},{2,3},{3,2},{4,5},{5,4},{6,7},{7,6},{8,9},{9,8},{10,11... | collective-permute-start | bytes 3538952 | tf_op jit(solution)/shard_map/ppermute | solution.py:250
  193.4 50.7 %collective-permute-start.16 = (bf16[1024,512]{1,0:T(8,128)(2,1)}, bf16[1024,512]{1,0:T(8,128)(2,1)}, u32[]{:S(2)}, u32[]{:S(2)}) collective-permute-start(bf16[1024,512]{1,0:T(8,128)(2,1)} %convolution_convert_fusion.5), channel_id=1, source_target_pairs={{0,1},{1,0},{2,3},{3,2},{4,5},{5,4},{6,7},{7,6},{8,9},{9,8},{10,11... | collective-permute-start | bytes 3145736 | tf_op jit(solution)/shard_map/ppermute | solution.py:250
  204.3 39.9 %collective-permute-start.17 = (f32[17,128]{1,0:T(8,128)S(1)}, f32[17,128]{1,0:T(8,128)S(1)}, u32[]{:S(2)}, u32[]{:S(2)}) collective-permute-start(f32[17,128]{1,0:T(8,128)S(1)} %bitcast.100), channel_id=1, source_target_pairs={{0,16},{16,0},{1,17},{17,1},{2,18},{18,2},{3,19},{19,3},{4,20},{20... | collective-permute-start | bytes 26120 | tf_op jit(solution)/shard_map/ppermute | solution.py:250
  206.9 13.4 %copy-start.14 = (bf16[512,2304]{1,0:T(8,128)(2,1)S(1)}, bf16[512,2304]{1,0:T(8,128)(2,1)}, u32[]{:S(2)}) copy-start(bf16[512,2304]{1,0:T(8,128)(2,1)} %copy-done.13) | copy-start | bytes 7077892
  212.0 12.2 %copy-start.11 = (bf16[2304,512]{1,0:T(8,128)(2,1)S(1)}, bf16[2304,512]{1,0:T(8,128)(2,1)}, u32[]{:S(2)}) copy-start(bf16[2304,512]{1,0:T(8,128)(2,1)} %convolution_convert_fusion) | copy-start | bytes 7077892
  223.2 46.6 %collective-permute-start.19 = (bf16[2,1,128,1152]{3,2,1,0:T(8,128)(2,1)}, bf16[2,1,128,1152]{3,2,1,0:T(8,128)(2,1)}, u32[]{:S(2)}, u32[]{:S(2)}) collective-permute-start(bf16[2,1,128,1152]{3,2,1,0:T(8,128)(2,1)} %select_convert_fusion.1), channel_id=1, source_target_pairs={{0,1},{1,0},{2,3},{3,2},{4,5},{5,4},{6,7},{7,6},{8,9},{9,8},{10,11... | collective-permute-start | bytes 1769480 | tf_op jit(solution)/shard_map/ppermute | solution.py:250
  227.4 16.7 %copy-start.24 = (bf16[1024,512]{1,0:T(8,128)(2,1)S(1)}, bf16[1024,512]{1,0:T(8,128)(2,1)}, u32[]{:S(2)}) copy-start(bf16[1024,512]{1,0:T(8,128)(2,1)} %convolution_convert_fusion.3) | copy-start | bytes 3145732
  227.4 42.5 %collective-permute-start.20 = (bf16[2,1,576,512]{3,2,1,0:T(8,128)(2,1)}, bf16[2,1,576,512]{3,2,1,0:T(8,128)(2,1)S(1)}, u32[]{:S(2)}, u32[]{:S(2)}) collective-permute-start(bf16[2,1,576,512]{3,2,1,0:T(8,128)(2,1)} %add_convert_fusion), channel_id=1, source_target_pairs={{8,0},{2,10},{9,1},{3,11},{12,4},{6,14},{13,5},{7,15},{24,16},{18,... | collective-permute-start | bytes 3538952 | tf_op jit(solution)/shard_map/ppermute | solution.py:843
  244.1 24.3 %collective-permute-start.14 = (bf16[512,1024]{1,0:T(8,128)(2,1)}, bf16[512,1024]{1,0:T(8,128)(2,1)S(1)}, u32[]{:S(2)}, u32[]{:S(2)}) collective-permute-start(bf16[512,1024]{1,0:T(8,128)(2,1)} %get-tuple-element.132), channel_id=1, source_target_pairs={{0,2},{2,0},{1,3},{3,1},{4,6},{6,4},{5,7},{7,5},{8,10},{10,8},{9,1... | collective-permute-start | bytes 3145736 | tf_op jit(solution)/shard_map/ppermute | solution.py:250
  244.2 24.3 %copy-start.22 = (f32[512,1024]{1,0:T(8,128)S(1)}, f32[512,1024]{1,0:T(8,128)}, u32[]{:S(2)}) copy-start(f32[512,1024]{1,0:T(8,128)} %get-tuple-element.131) | copy-start | bytes 6291460
  246.8 20.0 %collective-permute-start.22 = (bf16[2,2,1,128,768]{4,3,2,1,0:T(8,128)(2,1)S(1)}, bf16[2,2,1,128,768]{4,3,2,1,0:T(8,128)(2,1)S(1)}, u32[]{:S(2)}, u32[]{:S(2)}) collective-permute-start(bf16[2,2,1,128,768]{4,3,2,1,0:T(8,128)(2,1)S(1)} %pad_maximum_fusion.2), channel_id=1, source_target_pairs={{0,4},{4,0},{1,5},{5,1},{2,6},{6,2},{3,7},{7,3},{8,12},{12,8},{9,1... | collective-permute-start | bytes 2359304 | tf_op jit(solution)/shard_map/ppermute | solution.py:250
  248.4 20.1 %copy-start.4 = (f32[1024,1024]{1,0:T(8,128)S(1)}, f32[1024,1024]{1,0:T(8,128)}, u32[]{:S(2)}) copy-start(f32[1024,1024]{1,0:T(8,128)} %copy-done.2) | copy-start | bytes 12582916
  249.9 18.5 %collective-permute-start.18 = (f32[17,128]{1,0:T(8,128)S(1)}, f32[17,128]{1,0:T(8,128)S(1)}, u32[]{:S(2)}, u32[]{:S(2)}) collective-permute-start(f32[17,128]{1,0:T(8,128)S(1)} %bitcast_add_fusion), channel_id=1, source_target_pairs={{0,8},{8,0},{1,9},{9,1},{2,10},{10,2},{3,11},{11,3},{4,12},{12,4},... | collective-permute-start | bytes 26120 | tf_op jit(solution)/shard_map/ppermute | solution.py:250
  266.8 15.1 %collective-permute-start.21 = (bf16[2,1,128,1152]{3,2,1,0:T(8,128)(2,1)S(1)}, bf16[2,1,128,1152]{3,2,1,0:T(8,128)(2,1)S(1)}, u32[]{:S(2)}, u32[]{:S(2)}) collective-permute-start(bf16[2,1,128,1152]{3,2,1,0:T(8,128)(2,1)S(1)} %add_convert_fusion.4), channel_id=1, source_target_pairs={{0,4},{4,0},{1,5},{5,1},{2,6},{6,2},{3,7},{7,3},{8,12},{12,8},{9,1... | collective-permute-start | bytes 1769480 | tf_op jit(solution)/shard_map/ppermute | solution.py:250
  269.9 12.2 %collective-permute-start.23 = (f32[17,128]{1,0:T(8,128)S(1)}, f32[17,128]{1,0:T(8,128)S(1)}, u32[]{:S(2)}, u32[]{:S(2)}) collective-permute-start(f32[17,128]{1,0:T(8,128)S(1)} %fusion.56), channel_id=1, source_target_pairs={{0,4},{4,0},{1,5},{5,1},{2,6},{6,2},{3,7},{7,3},{8,12},{12,8},{9,1... | collective-permute-start | bytes 26120 | tf_op jit(solution)/shard_map/ppermute | solution.py:250
  272.0 11.2 %copy-start.25 = (bf16[1024,512]{1,0:T(8,128)(2,1)S(1)}, bf16[1024,512]{1,0:T(8,128)(2,1)}, u32[]{:S(2)}) copy-start(bf16[1024,512]{1,0:T(8,128)(2,1)} %convolution_convert_fusion.3) | copy-start | bytes 3145732
  272.1 29.6 %collective-permute-start.29 = (bf16[1,1,128,1152]{3,2,1,0:T(8,128)(2,1)S(1)}, bf16[1,1,128,1152]{3,2,1,0:T(8,128)(2,1)S(1)}, u32[]{:S(2)}, u32[]{:S(2)}) collective-permute-start(bf16[1,1,128,1152]{3,2,1,0:T(8,128)(2,1)S(1)} %add_convert_fusion.7), channel_id=1, source_target_pairs={{0,16},{16,0},{1,17},{17,1},{2,18},{18,2},{3,19},{19,3},{4,20},{20... | collective-permute-start | bytes 884744 | tf_op jit(solution)/shard_map/ppermute | solution.py:250
  276.3 53.4 %collective-permute-start.33 = (bf16[1,1,576,512]{3,2,1,0:T(8,128)(2,1)S(1)}, bf16[1,1,576,512]{3,2,1,0:T(8,128)(2,1)S(1)}, u32[]{:S(2)}, u32[]{:S(2)}) collective-permute-start(bf16[1,1,576,512]{3,2,1,0:T(8,128)(2,1)S(1)} %add_convert_fusion.3), channel_id=1, source_target_pairs={{0,16},{16,0},{1,17},{17,1},{2,18},{18,2},{3,19},{19,3},{4,20},{20... | collective-permute-start | bytes 1769480 | tf_op jit(solution)/shard_map/ppermute | solution.py:250
  282.1 6.6 %collective-permute-start.24 = (f32[17,128]{1,0:T(8,128)S(1)}, f32[17,128]{1,0:T(8,128)S(1)}, u32[]{:S(2)}, u32[]{:S(2)}) collective-permute-start(f32[17,128]{1,0:T(8,128)S(1)} %add.531), channel_id=1, source_target_pairs={{0,2},{2,0},{1,3},{3,1},{4,6},{6,4},{5,7},{7,5},{8,10},{10,8},{9,1... | collective-permute-start | bytes 26120 | tf_op jit(solution)/shard_map/ppermute | solution.py:250
  284.4 42.5 %collective-permute-start.26 = (bf16[2,1,1,128,768]{4,3,2,1,0:T(8,128)(2,1)S(1)}, bf16[2,1,1,128,768]{4,3,2,1,0:T(8,128)(2,1)S(1)}, u32[]{:S(2)}, u32[]{:S(2)}) collective-permute-start(bf16[2,1,1,128,768]{4,3,2,1,0:T(8,128)(2,1)S(1)} %pad_maximum_fusion.5), channel_id=1, source_target_pairs={{0,8},{8,0},{1,9},{9,1},{2,10},{10,2},{3,11},{11,3},{4,12},{12,4},... | collective-permute-start | bytes 1179656 | tf_op jit(solution)/shard_map/ppermute | solution.py:250
  286.0 39.6 %collective-permute-start.31 = (bf16[1,1,128,1152]{3,2,1,0:T(8,128)(2,1)S(1)}, bf16[1,1,128,1152]{3,2,1,0:T(8,128)(2,1)S(1)}, u32[]{:S(2)}, u32[]{:S(2)}) collective-permute-start(bf16[1,1,128,1152]{3,2,1,0:T(8,128)(2,1)S(1)} %add_convert_fusion.6), channel_id=1, source_target_pairs={{0,16},{16,0},{1,17},{17,1},{2,18},{18,2},{3,19},{19,3},{4,20},{20... | collective-permute-start | bytes 884744 | tf_op jit(solution)/shard_map/ppermute | solution.py:250
  288.6 58.2 %collective-permute-start.25 = (bf16[1024,1024]{1,0:T(8,128)(2,1)S(1)}, bf16[1024,1024]{1,0:T(8,128)(2,1)S(1)}, u32[]{:S(2)}, u32[]{:S(2)}) collective-permute-start(bf16[1024,1024]{1,0:T(8,128)(2,1)S(1)} %pad_maximum_fusion.1), channel_id=1, source_target_pairs={{0,0},{1,2},{2,1},{3,3},{4,4},{5,6},{6,5},{7,7},{8,8},{9,10},{10,9... | collective-permute-start | bytes 6291464 | tf_op jit(solution)/shard_map/ppermute | solution.py:254
  301.6 40.0 %collective-permute-start.28 = (f32[17,128]{1,0:T(8,128)S(1)}, f32[17,128]{1,0:T(8,128)S(1)}, u32[]{:S(2)}, u32[]{:S(2)}) collective-permute-start(f32[17,128]{1,0:T(8,128)S(1)} %add.535), channel_id=1, source_target_pairs={{0,1},{1,0},{2,3},{3,2},{4,5},{5,4},{6,7},{7,6},{8,9},{9,8},{10,11... | collective-permute-start | bytes 26120 | tf_op jit(solution)/shard_map/ppermute | solution.py:250
  325.7 2.9 collective-permute-start.30
  326.9 2.7 collective-permute-start.32
  328.6 12.0 %collective-permute-start.27 = (bf16[1,1,1,128,768]{4,3,2,1,0:T(8,128)(2,1)S(1)}, bf16[1,1,1,128,768]{4,3,2,1,0:T(8,128)(2,1)S(1)}, u32[]{:S(2)}, u32[]{:S(2)}) collective-permute-start(bf16[1,1,1,128,768]{4,3,2,1,0:T(8,128)(2,1)S(1)} %pad_maximum_fusion.7), channel_id=1, source_target_pairs={{0,16},{16,0},{1,17},{17,1},{2,18},{18,2},{3,19},{19,3},{4,20},{20... | collective-permute-start | bytes 589832 | tf_op jit(solution)/shard_map/ppermute | solution.py:250
  331.3 9.3 %collective-permute-start.34 = (bf16[288,512]{1,0:T(8,128)(2,1)S(1)}, bf16[288,512]{1,0:T(8,128)(2,1)S(1)}, u32[]{:S(2)}, u32[]{:S(2)}) collective-permute-start(bf16[288,512]{1,0:T(8,128)(2,1)S(1)} %fusion.24), channel_id=1, source_target_pairs={{0,2},{10,8},{1,3},{11,9},{4,6},{14,12},{5,7},{15,13},{16,18},{26,... | collective-permute-start | bytes 884744 | tf_op jit(solution)/shard_map/ppermute | solution.py:890
  342.8 1.4 collective-permute-start.35
  (39 other events, 171.3 us)
